TPU v7x, 256 devices: a whole 4x4x8 slice. The times are simulated.
256 devices in a mesh: ty: 16 (over y, x_hi, core), tx: 16 (over z, x_lo).
Axes of the slice: x: 4 (x_hi: 2, x_lo: 2; x = x_hi * 2 + x_lo), y: 4, z: 8, core: 2. Of those that a mesh axis runs over, the one named last changes fastest.
Arguments:
- block_input: bfloat16 [1024, 768, 256], P('ty', 'tx'), may hold values from -6 to 6
- cotangent: bfloat16 [1024, 768, 256], P('ty', 'tx'), may hold values from -6 to 6
- tissue: int32 [64, 48], P('ty', 'tx'), may hold values 0 or 1
- dw_weight: float32 [49, 256], replicated, may hold values from -0.875 to 0.875
- dw_bias: float32 [256], replicated, may hold values from -3 to 3
- ln_gain: float32 [256], replicated, may hold values from 0.5 to 1.5
- ln_bias: float32 [256], replicated, may hold values from -3 to 3
- w_expand: bfloat16 [256, 1024], replicated, may hold values from -0.375 to 0.375
- b_expand: float32 [1024], replicated, may hold values from -3 to 3
- w_reduce: bfloat16 [1024, 256], replicated, may hold values from -0.1875 to 0.1875
- layer_scale: float32 [256], replicated, may hold values from 0.5 to 2
Outputs:
- grad_input: bfloat16 [1024, 768, 256], P('ty', 'tx')
- grad_dw: float32 [49, 256], replicated
- grad_expand: float32 [256, 1024], replicated
- grad_reduce: float32 [1024, 256], replicated
Inputs may be any that keep to these rules, and one draw needn't show every extreme that they name: 1 marks a tile with tissue.
All inputs are finite; a program needn't handle non-finite values. No bound on the sum of `tissue` on one device may be relied on, other than what follows from the above.
Results may differ from a plain program's by a relative error of at most 0.007.
Values may be sent and summed in bfloat16 or wider, within the bound.
No kernel may reach another device: no remote copies, remote signals or barrier semaphores. Data moves between devices by JAX's collectives and lax.ppermute only.
A program may use at most 256 MiB of HBM per device.

v0:
```python
import math

import jax
import jax.numpy as jnp
from jax import lax
from jax.sharding import PartitionSpec as P

TILE = 16


def with_halo(block, sides, width):
    for axis, dim in sides:
        count = lax.axis_size(axis)
        forward = [(i, i + 1) for i in range(count - 1)]
        backward = [(target, source) for source, target in forward]
        low = lax.ppermute(
            lax.slice_in_dim(block, block.shape[dim] - width, None, axis=dim), axis, forward
        )
        high = lax.ppermute(lax.slice_in_dim(block, 0, width, axis=dim), axis, backward)
        block = jnp.concatenate([low, block, high], axis=dim)
    return block


def depthwise(padded, kernel, rows, cols):
    total = jnp.zeros((rows, cols, padded.shape[2]), jnp.float32)
    for row_off in range(7):
        for col_off in range(7):
            window = padded[row_off : row_off + rows, col_off : col_off + cols].astype(jnp.float32)
            total = total + window * kernel[row_off * 7 + col_off]
    return total


def filter_grad(padded, grad, rows, cols):
    gradf = grad.astype(jnp.float32)
    taps = []
    for row_off in range(7):
        for col_off in range(7):
            window = padded[row_off : row_off + rows, col_off : col_off + cols].astype(jnp.float32)
            taps.append(jnp.sum(window * gradf, axis=(0, 1)))
    return jnp.stack(taps)


def branch_back(pre, masked, ln_gain, ln_bias, w_expand, b_expand, w_reduce, layer_scale):
    center = pre - jnp.mean(pre, axis=-1, keepdims=True)
    rstd = lax.rsqrt(jnp.mean(center * center, axis=-1, keepdims=True) + 1e-06)
    nhat = center * rstd
    normed = (nhat * ln_gain + ln_bias).astype(jnp.bfloat16)
    zvals = jnp.dot(normed, w_expand, preferred_element_type=jnp.float32) + b_expand
    cdf = 0.5 * (1.0 + jax.scipy.special.erf(zvals * 0.7071067811865476))
    hidden = (zvals * cdf).astype(jnp.bfloat16)
    go_vals = (layer_scale * masked.astype(jnp.float32)).astype(jnp.bfloat16)
    dhid = jnp.dot(go_vals, w_reduce.T, preferred_element_type=jnp.float32)
    slope = cdf + zvals * jnp.exp(-0.5 * zvals * zvals) * 0.3989422804014327
    dzvals = (dhid * slope).astype(jnp.bfloat16)
    dnorm = jnp.dot(dzvals, w_expand.T, preferred_element_type=jnp.float32) * ln_gain
    grad = rstd * (
        dnorm
        - jnp.mean(dnorm, axis=-1, keepdims=True)
        - nhat * jnp.mean(dnorm * nhat, axis=-1, keepdims=True)
    )
    return (grad.astype(jnp.bfloat16), hidden, normed, go_vals, dzvals)


def body(
    block_input,
    cotangent,
    tissue,
    dw_weight,
    dw_bias,
    ln_gain,
    ln_bias,
    w_expand,
    b_expand,
    w_reduce,
    layer_scale,
):
    rows, cols, chans = block_input.shape
    mask = jnp.repeat(jnp.repeat(tissue, TILE, axis=0), TILE, axis=1)
    masked = (cotangent.astype(jnp.float32) * mask[:, :, None].astype(jnp.float32)).astype(
        jnp.bfloat16
    )
    params = (ln_gain, ln_bias, w_expand, b_expand, w_reduce, layer_scale)
    input_pad = with_halo(block_input, (("ty", 0), ("tx", 1)), 3)
    pre = depthwise(input_pad, dw_weight, rows, cols) + dw_bias
    grad, hidden, normed, go_vals, dzvals = branch_back(
        pre.reshape(-1, chans), masked.reshape(-1, chans), *params
    )
    grad_core = grad.reshape(rows, cols, chans)
    grad_pad = with_halo(grad_core, (("ty", 0), ("tx", 1)), 3)
    factor = 1.0 / math.sqrt(rows * lax.axis_size("ty") * cols * lax.axis_size("tx"))
    local_reduce = jnp.dot(hidden.T, go_vals, preferred_element_type=jnp.float32)
    local_expand = jnp.dot(normed.T, dzvals, preferred_element_type=jnp.float32)
    local_dw = filter_grad(input_pad, grad_core, rows, cols)
    total_expand, total_reduce, total_dw = lax.psum(
        (local_expand, local_reduce, local_dw), ("ty", "tx")
    )
    result = cotangent.astype(jnp.float32) + depthwise(grad_pad, dw_weight[::-1], rows, cols)
    return (
        result.astype(jnp.bfloat16),
        total_dw * factor,
        total_expand * factor,
        total_reduce * factor,
    )


def solution(mesh):
    placed = (
        P("ty", "tx", None),
        P("ty", "tx", None),
        P("ty", "tx"),
        P(),
        P(),
        P(),
        P(),
        P(),
        P(),
        P(),
        P(),
    )
    return jax.shard_map(
        body,
        mesh=mesh,
        in_specs=placed,
        out_specs=(P("ty", "tx", None), P(), P(), P()),
        check_vma=False,
    )
```

profile of v0, /device:TPU:2, one launch (start us, length us, event | category | flops | bytes accessed | tf_op | source)
XLA Modules:
  0.0 527.7 jit_solution(16179048149840862890)
XLA Ops:
  8.2 1.3 collective-permute-start.1
  9.5 3.0 collective-permute-start
  14.7 2.0 fusion.8
  16.7 1.6 fusion.132
  20.4 3.8 collective-permute-start.2
  24.2 2.0 collective-permute-start.3
  27.4 4.8 collective-permute-done.3
  32.2 61.1 %fusion.180 = (f32[64,48]{1,0:T(8,128)S(1)}, f32[64,48,256]{2,1,0:T(8,128)}) fusion(f32[256]{0:T(256)S(1)} %copy-done.23, f32[256]{0:T(256)S(1)} %bitcast.232, bf16[70,3,256]{2,1,0:T(4,128)(2,1)S(1)} %collective-permute-done.3, bf16[70,48,256]{2,1,0:T(8,128)(2,1)} %copy-done.4, f32[256]{0:T(256)S(1)} %bitcast.234, f32[256]{0:T(256)S(1)} %bitcast.140, ...), kind=kLoop, calls=%fused_computation.358 | loop fusion | flops 215479296 | bytes 16154624 | tf_op jit(solution)/shard_map/reduce_sum | solution.py:44
  93.5 2.8 multiply_reduce_fusion.1
  96.4 3.1 add_convert_fusion
  99.6 1.8 fusion.188
  101.4 5.5 %fusion.6 = f32[1024,256]{1,0:T(8,128)} fusion(bf16[3072,256]{1,0:T(8,128)(2,1)S(1)} %copy-done.12, f32[3072,1024]{1,0:T(8,128)S(1)} %fusion.188, f32[1024]{0:T(1024)S(1)} %copy-done.27), kind=kOutput, calls=%fused_computation.99 | convolution fusion | flops 1629487104 | bytes 15208448 | tf_op jit(solution)/shard_map/dot_general | solution.py:91
  106.9 7.0 %fusion.5 = bf16[3072,1024]{1,0:T(8,128)(2,1)S(1)} fusion(f32[3072,1024]{1,0:T(8,128)S(1)} %fusion.188, bf16[3072,256]{1,0:T(8,128)(2,1)S(1)} %copy-done.12, bf16[1024,256]{1,0:T(8,128)(2,1)S(1)} %copy-done.26, f32[1024]{0:T(1024)S(1)} %copy-done.27), kind=kOutput, calls=%fused_computation.96 | convolution fusion | flops 1645215744 | bytes 20975616 | tf_op jit(solution)/shard_map/dot_general | solution.py:52
  113.9 2.7 copy-done.9
  116.5 2.8 fusion.189
  119.3 6.2 %fusion.179 = (f32[3072]{0:T(1024)S(1)}, f32[3072]{0:T(1024)S(1)}, f32[3072,256]{1,0:T(8,128)S(1)}) fusion(f32[3072]{0:T(1024)S(1)} %rsqrt.12, f32[3072]{0:T(1024)S(1)} %div.16, f32[64,48,256]{2,1,0:T(8,128)} %get-tuple-element.64, f32[256]{0:T(256)S(1)} %copy-done.25, bf16[3072,1024]{1,0:T(8,128)(2,1)} %copy-done.9, bf16[256,1024]{1,0:T(8,128)(2,1)S(1)} %copy-done), kind=kOutput, calls=%fused_computation.357 | convolution fusion | flops 1615325184 | bytes 13157376 | tf_op jit(solution)/shard_map/dot_general | solution.py:55
  125.5 2.5 multiply_convert_fusion.2
  129.4 3.8 collective-permute-start.4
  133.2 5.1 fusion.129
  138.3 6.0 %fusion.131 = (f32[256]{0:T(256)S(1)}, f32[256]{0:T(256)S(1)}, f32[256]{0:T(256)S(1)}, f32[256]{0:T(256)S(1)}, f32[256]{0:T(256)S(1)}, /*index=5*/f32[256]{0:T(2...) fusion(bf16[64,48,256]{2,1,0:T(8,128)(2,1)S(1)} %bitcast.127, bf16[70,3,256]{2,1,0:T(4,128)(2,1)S(1)} %collective-permute-done.3, ...), kind=kLoop, calls=%fused_computation.276 | loop fusion | flops 43251456 | bytes 3409920 | tf_op jit(solution)/shard_map/reduce_sum | solution.py:39
  144.3 6.4 %fusion.130 = (f32[256]{0:T(256)S(1)}, f32[256]{0:T(256)S(1)}, f32[256]{0:T(256)S(1)}, f32[256]{0:T(256)S(1)}, f32[256]{0:T(256)S(1)}, /*index=5*/f32[256]{0:T(2...) fusion(bf16[64,48,256]{2,1,0:T(8,128)(2,1)S(1)} %bitcast.128, bf16[70,3,256]{2,1,0:T(4,128)(2,1)S(1)} %collective-permute-done.3, ...), kind=kLoop, calls=%fused_computation.275 | loop fusion | flops 43251456 | bytes 3409920 | tf_op jit(solution)/shard_map/reduce_sum | solution.py:39
  150.6 5.0 fusion.126
  155.7 5.1 fusion.127
  161.7 84.7 %psum.21 = f32[49,256]{1,0:T(8,128)S(1)} all-reduce(f32[49,256]{1,0:T(8,128)S(1)} %stack.199), channel_id=1, replica_groups=mesh['ty'=16,'tx'=16] {'ty','tx'}, use_global_device_ids=true, to_apply=%region_53.0 | all-reduce | flops 12544 | bytes 100352 | tf_op jit(solution)/shard_map/psum | solution.py:94
  246.5 2.0 collective-permute-start.6
  248.5 3.9 collective-permute-start.7
  253.1 3.9 collective-permute-done.6
  257.0 2.6 maximum_maximum_fusion
  259.6 33.2 %fusion.9 = bf16[64,48,256]{2,1,0:T(8,128)(2,1)} fusion(bf16[64,48,256]{2,1,0:T(8,128)(2,1)} %param.12, bf16[64,48,256]{2,1,0:T(8,128)(2,1)} %bitcast.134, bf16[3,48,256]{2,1,0:T(8,128)(2,1)S(1)} %collective-permute-done.5, bf16[3,48,256]{2,1,0:T(8,128)(2,1)S(1)} %collective-permute-done.4, bf16[70,51,256]{2,1,0:T(8,128)(2,1)S(1)} %get-tuple-element.66, ...), kind=kLoop, calls=%fused_computation.154 | loop fusion | flops 121896960 | bytes 70976512 | tf_op jit(solution)/shard_map/convert_element_type | solution.py:99
  292.9 223.4 %all-reduce.3.cloned.1.call-done = (f32[256,1024]{1,0:T(8,128)}, f32[1024,256]{1,0:T(8,128)}) async-done(((f32[256,1024]{1,0:T(8,128)}, f32[1024,256]{1,0:T(8,128)}), (f32[256,1024]{1,0:T(8,128)}, f32[1024,256]{1,0:T(8,128)})) %all-reduce.3.cloned.1.call-update) | async-done | bytes 2097168 | tf_op jit(solution)/shard_map/psum | solution.py:94
  516.2 2.3 broadcast_multiply_fusion.1
  518.6 2.3 broadcast_multiply_fusion
  (88 shorter events, 9.5 us)
Async XLA Ops:
  7.2 92.4 %copy-start = (bf16[256,1024]{1,0:T(8,128)(2,1)S(1)}, bf16[256,1024]{1,0:T(8,128)(2,1)}, u32[]{:S(2)}) copy-start(bf16[256,1024]{1,0:T(8,128)(2,1)} %param.18) | copy-start | bytes 1572868
  7.2 9.5 %copy-start.22 = (f32[256]{0:T(256)S(1)}, f32[256]{0:T(256)}, u32[]{:S(2)}) copy-start(f32[256]{0:T(256)} %param.21) | copy-start | bytes 3076
  7.2 509.0 %all-reduce.3.cloned.1.call-start = ((), (), s32[]{:S(2)}) async-start(), calls=%async_computation | async-start | bytes 4194304 | tf_op jit(solution)/shard_map/psum | solution.py:94
  8.2 10.4 %collective-permute-start.1 = (bf16[3,48,256]{2,1,0:T(8,128)(2,1)S(1)}, bf16[3,48,256]{2,1,0:T(8,128)(2,1)S(1)}, u32[]{:S(2)}, u32[]{:S(2)}) collective-permute-start(bf16[3,48,256]{2,1,0:T(8,128)(2,1)S(1)} %get-tuple-element.76), channel_id=1, source_target_pairs={{16,0},{32,16},{48,32},{64,48},{80,64},{96,80},{112,96},{128,112},... | collective-permute-start | bytes 221192 | tf_op jit(solution)/shard_map/ppermute | solution.py:19
  9.5 8.8 %collective-permute-start = (bf16[3,48,256]{2,1,0:T(8,128)(2,1)S(1)}, bf16[3,48,256]{2,1,0:T(8,128)(2,1)S(1)}, u32[]{:S(2)}, u32[]{:S(2)}) collective-permute-start(bf16[3,48,256]{2,1,0:T(8,128)(2,1)S(1)} %get-tuple-element.77), channel_id=1, source_target_pairs={{0,16},{16,32},{32,48},{48,64},{64,80},{80,96},{96,112},{112,128},... | collective-permute-start | bytes 221192 | tf_op jit(solution)/shard_map/ppermute | solution.py:16
  14.6 3.6 copy-start.13
  14.6 3.7 copy-start.10
  18.3 13.9 %copy-start.23 = (f32[256]{0:T(256)S(1)}, f32[256]{0:T(256)}, u32[]{:S(2)}) copy-start(f32[256]{0:T(256)} %param.15) | copy-start | bytes 3076
  18.7 74.6 %copy-start.2 = (bf16[67,48,256]{2,1,0:T(8,128)(2,1)}, bf16[67,48,256]{2,1,0:T(8,128)(2,1)S(1)}, u32[]{:S(2)}) copy-start(bf16[67,48,256]{2,1,0:T(8,128)(2,1)S(1)} %get-tuple-element.80) | copy-start | bytes 4939780
  20.4 7.0 %collective-permute-start.2 = (bf16[70,3,256]{2,1,0:T(4,128)(2,1)S(1)}, bf16[70,3,256]{2,1,0:T(4,128)(2,1)S(1)}, u32[]{:S(2)}, u32[]{:S(2)}) collective-permute-start(bf16[70,3,256]{2,1,0:T(4,128)(2,1)S(1)} %get-tuple-element.69), channel_id=1, source_target_pairs={{0,1},{1,2},{2,3},{3,4},{4,5},{5,6},{6,7},{7,8},{8,9},{9,10},{10,1... | collective-permute-start | bytes 322568 | tf_op jit(solution)/shard_map/ppermute | solution.py:16
  24.2 8.0 %collective-permute-start.3 = (bf16[70,3,256]{2,1,0:T(4,128)(2,1)S(1)}, bf16[70,3,256]{2,1,0:T(4,128)(2,1)S(1)}, u32[]{:S(2)}, u32[]{:S(2)}) collective-permute-start(bf16[70,3,256]{2,1,0:T(4,128)(2,1)S(1)} %get-tuple-element.70), channel_id=1, source_target_pairs={{1,0},{2,1},{3,2},{4,3},{5,4},{6,5},{7,6},{8,7},{9,8},{10,9},{11,1... | collective-permute-start | bytes 322568 | tf_op jit(solution)/shard_map/ppermute | solution.py:19
  26.2 67.1 %copy-start.14 = (f32[1,256]{1,0:T(1,128)}, f32[1,256]{1,0:T(1,128)S(1)}, u32[]{:S(2)}) copy-start(f32[1,256]{1,0:T(1,128)S(1)} %get-tuple-element.123) | copy-start | bytes 3076
  26.3 67.1 %copy-start.15 = (f32[1,256]{1,0:T(1,128)}, f32[1,256]{1,0:T(1,128)S(1)}, u32[]{:S(2)}) copy-start(f32[1,256]{1,0:T(1,128)S(1)} %get-tuple-element.124) | copy-start | bytes 3076
  26.3 67.1 %copy-start.16 = (f32[1,256]{1,0:T(1,128)}, f32[1,256]{1,0:T(1,128)S(1)}, u32[]{:S(2)}) copy-start(f32[1,256]{1,0:T(1,128)S(1)} %get-tuple-element.125) | copy-start | bytes 3076
  26.3 67.1 %copy-start.17 = (f32[1,256]{1,0:T(1,128)}, f32[1,256]{1,0:T(1,128)S(1)}, u32[]{:S(2)}) copy-start(f32[1,256]{1,0:T(1,128)S(1)} %get-tuple-element.126) | copy-start | bytes 3076
  26.3 67.1 %copy-start.18 = (f32[1,256]{1,0:T(1,128)}, f32[1,256]{1,0:T(1,128)S(1)}, u32[]{:S(2)}) copy-start(f32[1,256]{1,0:T(1,128)S(1)} %get-tuple-element.127) | copy-start | bytes 3076
  26.3 67.1 %copy-start.19 = (f32[1,256]{1,0:T(1,128)}, f32[1,256]{1,0:T(1,128)S(1)}, u32[]{:S(2)}) copy-start(f32[1,256]{1,0:T(1,128)S(1)} %get-tuple-element.128) | copy-start | bytes 3076
  26.3 67.1 %copy-start.20 = (f32[1,256]{1,0:T(1,128)}, f32[1,256]{1,0:T(1,128)S(1)}, u32[]{:S(2)}) copy-start(f32[1,256]{1,0:T(1,128)S(1)} %get-tuple-element.129) | copy-start | bytes 3076
  26.3 67.1 %copy-start.21 = (f32[1,256]{1,0:T(1,128)}, f32[1,256]{1,0:T(1,128)S(1)}, u32[]{:S(2)}) copy-start(f32[1,256]{1,0:T(1,128)S(1)} %get-tuple-element.130) | copy-start | bytes 3076
  93.4 3.0 copy-start.24
  93.4 3.0 copy-start.25
  101.4 5.5 %copy-start.26 = (bf16[1024,256]{1,0:T(8,128)(2,1)S(1)}, bf16[1024,256]{1,0:T(8,128)(2,1)}, u32[]{:S(2)}) copy-start(bf16[1024,256]{1,0:T(8,128)(2,1)} %param.20) | copy-start | bytes 1572868
  119.3 6.2 %copy-start.8 = (f32[64,48,256]{2,1,0:T(8,128)S(1)}, f32[64,48,256]{2,1,0:T(8,128)}, u32[]{:S(2)}) copy-start(f32[64,48,256]{2,1,0:T(8,128)} %get-tuple-element.64) | copy-start | bytes 9437188
  125.5 7.6 %copy-start.5 = (bf16[70,48,256]{2,1,0:T(8,128)(2,1)S(1)}, bf16[70,48,256]{2,1,0:T(8,128)(2,1)}, u32[]{:S(2)}) copy-start(bf16[70,48,256]{2,1,0:T(8,128)(2,1)} %copy-done.4) | copy-start | bytes 5160964
  125.5 7.6 %copy-start.7 = (bf16[67,48,256]{2,1,0:T(8,128)(2,1)S(1)}, bf16[67,48,256]{2,1,0:T(8,128)(2,1)}, u32[]{:S(2)}) copy-start(bf16[67,48,256]{2,1,0:T(8,128)(2,1)} %copy-done.6) | copy-start | bytes 4939780
  125.5 7.6 %copy-start.11 = (bf16[64,48,256]{2,1,0:T(8,128)(2,1)S(1)}, bf16[64,48,256]{2,1,0:T(8,128)(2,1)}, u32[]{:S(2)}) copy-start(bf16[64,48,256]{2,1,0:T(8,128)(2,1)} %param.11) | copy-start | bytes 4718596
  128.1 118.4 %copy-start.1 = (bf16[3072,256]{1,0:T(8,128)(2,1)}, bf16[3072,256]{1,0:T(8,128)(2,1)S(1)}, u32[]{:S(2)}) copy-start(bf16[3072,256]{1,0:T(8,128)(2,1)S(1)} %multiply_convert_fusion.2) | copy-start | bytes 4718596
  128.1 118.3 %collective-permute-start.5 = (bf16[3,48,256]{2,1,0:T(8,128)(2,1)S(1)}, bf16[3,48,256]{2,1,0:T(8,128)(2,1)S(1)}, u32[]{:S(2)}, u32[]{:S(2)}) collective-permute-start(bf16[3,48,256]{2,1,0:T(8,128)(2,1)S(1)} %bitcast.137), channel_id=1, source_target_pairs={{16,0},{32,16},{48,32},{64,48},{80,64},{96,80},{112,96},{128,112},... | collective-permute-start | bytes 221192 | tf_op jit(solution)/shard_map/ppermute | solution.py:19
  129.4 117.0 %collective-permute-start.4 = (bf16[3,48,256]{2,1,0:T(8,128)(2,1)S(1)}, bf16[3,48,256]{2,1,0:T(8,128)(2,1)S(1)}, u32[]{:S(2)}, u32[]{:S(2)}) collective-permute-start(bf16[3,48,256]{2,1,0:T(8,128)(2,1)S(1)} %bitcast.136), channel_id=1, source_target_pairs={{0,16},{16,32},{32,48},{48,64},{64,80},{80,96},{96,112},{112,128},... | collective-permute-start | bytes 221192 | tf_op jit(solution)/shard_map/ppermute | solution.py:16
  150.6 10.1 %copy-start.3 = (bf16[67,48,256]{2,1,0:T(8,128)(2,1)S(1)}, bf16[67,48,256]{2,1,0:T(8,128)(2,1)}, u32[]{:S(2)}) copy-start(bf16[67,48,256]{2,1,0:T(8,128)(2,1)} %copy-done.2) | copy-start | bytes 4939780
  246.5 10.5 %collective-permute-start.6 = (bf16[70,3,256]{2,1,0:T(4,128)(2,1)S(1)}, bf16[70,3,256]{2,1,0:T(4,128)(2,1)S(1)}, u32[]{:S(2)}, u32[]{:S(2)}) collective-permute-start(bf16[70,3,256]{2,1,0:T(4,128)(2,1)S(1)} %get-tuple-element.67), channel_id=1, source_target_pairs={{0,1},{1,2},{2,3},{3,4},{4,5},{5,6},{6,7},{7,8},{8,9},{9,10},{10,1... | collective-permute-start | bytes 322568 | tf_op jit(solution)/shard_map/ppermute | solution.py:16
  248.5 8.5 %collective-permute-start.7 = (bf16[70,3,256]{2,1,0:T(4,128)(2,1)S(1)}, bf16[70,3,256]{2,1,0:T(4,128)(2,1)S(1)}, u32[]{:S(2)}, u32[]{:S(2)}) collective-permute-start(bf16[70,3,256]{2,1,0:T(4,128)(2,1)S(1)} %get-tuple-element.68), channel_id=1, source_target_pairs={{1,0},{2,1},{3,2},{4,3},{5,4},{6,5},{7,6},{8,7},{9,8},{10,9},{11,1... | collective-permute-start | bytes 322568 | tf_op jit(solution)/shard_map/ppermute | solution.py:19
  (5 other events, 9.3 us)
Sparse Core Ops, SparseCore 0:
  253.2 262.9 all-reduce.2
where the time goes:
time: 528 us
  waiting for transfers between devices  233 us (44%)
  other arithmetic  143 us (27%)
  blocking collectives  84.7 us (16%)
  matrix products  23.2 us (4%)
  starting transfers between devices  21.1 us (4%)
  between operations  14.7 us (3%)
  local copies, waits for them, and re-layouts  7.49 us (1%)
    psum x1, waiting for transfers between devices, body(): lax.psum((local_expand, local_reduce, local_dw), ('ty', 'tx'))  223 us
    psum x1, blocking collectives, body(): lax.psum((local_expand, local_reduce, local_dw), ('ty', 'tx'))  84.7 us
    reduce_sum x1, other arithmetic, branch_back(): center = pre - jnp.mean(pre, axis=-1, keepdims=True)  61.1 us
    convert_element_type x1, other arithmetic, body(): result.astype(jnp.bfloat16)  33.2 us
    reduce_sum x6, other arithmetic, filter_grad(): taps.append(jnp.sum(window * gradf, axis=(0, 1)))  28.4 us
    ppermute x4, starting transfers between devices, with_halo(): lax.ppermute(lax.slice_in_dim(block, block.shape[dim] - width, None, axis...  12.6 us
  transfers between devices with their start and end apart: 9, of which 4 were waited for; matrix products, arithmetic and copies ran while one was open for 13% of the time, Pallas kernels for 0%

commit v1 on v0

v1 whole, which is shorter than its diff:
```python
import functools
import math

import jax
import jax.numpy as jnp
import numpy as np
from jax import lax
from jax.experimental import pallas as pl
from jax.experimental.pallas import tpu as pltpu
from jax.sharding import Mesh, PartitionSpec as P

F32, BF16 = jnp.float32, jnp.bfloat16
TILE = 16
LANES = 128
RG = 8
CB = 3
DW_ROWS = 32
VMEM = pl.BlockSpec(memory_space=pltpu.VMEM)
PARAMS = dict(vmem_limit_bytes=56 << 20)


def nn(a, b):
    return lax.dot_general(a, b, (((1,), (0,)), ((), ())), preferred_element_type=F32)


def nt(a, b):
    return lax.dot_general(a, b, (((1,), (1,)), ((), ())), preferred_element_type=F32)


def half(h):
    return slice(h * LANES, (h + 1) * LANES)


def spread_weights(w_ref, wide, flip):
    for h in range(2):
        for t in range(49):
            s = 48 - t if flip else t
            wide[h, t] = jnp.broadcast_to(w_ref[s : s + 1, half(h)], (8, LANES))


def fill(pad, core, top, bottom, left, right):
    rows, cols = core.shape[0], core.shape[1]
    for h in range(2):

        def put(i, _):
            pad[h, 3 + i, 8 : 8 + cols, :] = core[i, :, half(h)].astype(F32)
            return 0

        lax.fori_loop(0, rows, put, 0, unroll=4)
        for i in range(3):
            pad[h, i, 8 : 8 + cols, :] = top[i, :, half(h)].astype(F32)
            pad[h, 3 + rows + i, 8 : 8 + cols, :] = bottom[i, :, half(h)].astype(F32)
            for r in range(rows + 6):
                pad[h, r, 5 + i : 6 + i, :] = left[i, r : r + 1, half(h)].astype(F32)
                pad[h, r, 8 + cols + i : 9 + cols + i, :] = right[i, r : r + 1, half(h)].astype(F32)


def stencil(pad, wide, h, row, col):
    acc = [[None] * CB for _ in range(RG)]
    for b in range(7):
        w = [wide[h, a * 7 + b] for a in range(7)]
        for r in range(RG + 6):
            for c in range(CB):
                v = pad[h, row + r, pl.ds(col + c * 8 + 5 + b, 8), :]
                for a in range(7):
                    i = r - a
                    if 0 <= i < RG:
                        p = v * w[a]
                        acc[i][c] = p if acc[i][c] is None else acc[i][c] + p
    return acc


def branch_kernel(
    tissue, x_ref, top, bottom, left, right, cot, w_ref, bias, gain, shift, we, be, wr, scale,
    g_ref, acc_ref,
    pad, wide, u_ref, rstd_ref, normed, normed_t, go, go_t, hid, dz, dn,
):
    step = pl.program_id(0)
    rows, cols, chans = cot.shape
    pix = rows * cols
    hidden = we.shape[1]
    chunk = 256

    @pl.when(step == 0)
    def _():
        spread_weights(w_ref, wide, False)
        fill(pad, x_ref, top, bottom, left, right)
        acc_ref[...] = jnp.zeros_like(acc_ref)

    ng = cols // (8 * CB)
    for h in range(2):

        def conv(n, _):
            row, col = (n // ng) * RG, (n % ng) * (8 * CB)
            acc = stencil(pad, wide, h, step * rows + row, col)
            for i in range(RG):
                for c in range(CB):
                    at = pl.multiple_of((row + i) * cols + col + c * 8, 8)
                    u_ref[pl.ds(at, 8), half(h)] = acc[i][c] + bias[0:1, half(h)]
            return 0

        lax.fori_loop(0, (rows // RG) * ng, conv, 0)

    tiles = cols // TILE
    for c in range(tiles):
        keep = tissue[step, c].astype(F32)
        part = cot[:, c * TILE : (c + 1) * TILE, :].astype(F32) * (scale[0:1, :] * keep)
        for i in range(rows):
            go[i * cols + c * TILE : i * cols + (c + 1) * TILE, :] = part[i].astype(BF16)

    def norm(i, _):
        at = pl.ds(pl.multiple_of(i * cols, cols), cols)
        u = u_ref[at, :]
        center = u - jnp.sum(u, axis=-1, keepdims=True) * (1.0 / chans)
        var = jnp.sum(center * center, axis=-1, keepdims=True) * (1.0 / chans)
        rstd = lax.rsqrt(var + 1e-06)
        nhat = center * rstd
        u_ref[at, :] = nhat
        rstd_ref[at, :] = jnp.broadcast_to(rstd, (cols, LANES))
        normed[at, :] = (nhat * gain[0:1, :] + shift[0:1, :]).astype(BF16)
        return 0

    lax.fori_loop(0, rows, norm, 0, unroll=4)
    normed_t[...] = normed[...].T
    go_t[...] = go[...].T

    def mlp(k, _):
        at = pl.ds(pl.multiple_of(k * chunk, chunk), chunk)
        z = nn(normed[...], we[:, at]) + be[0:1, at]
        cdf = 0.5 * (1.0 + lax.erf(z * 0.7071067811865476))
        hid[...] = (z * cdf).astype(BF16)
        slope = cdf + z * jnp.exp(-0.5 * z * z) * 0.3989422804014327
        dz[...] = (nt(go[...], wr[at, :]) * slope).astype(BF16)
        part = nt(dz[...], we[:, at])
        @pl.when(k == 0)
        def _():
            dn[...] = part
        @pl.when(k > 0)
        def _():
            dn[...] += part
        acc_ref[0:chans, at] += nn(normed_t[...], dz[...])
        acc_ref[chans : 2 * chans, at] += nn(go_t[...], hid[...])
        return 0

    lax.fori_loop(0, hidden // chunk, mlp, 0)

    def back(i, _):
        at = pl.ds(pl.multiple_of(i * cols, cols), cols)
        nhat = u_ref[at, :]
        d = dn[at, :] * gain[0:1, :]
        first = jnp.sum(d, axis=-1, keepdims=True) * (1.0 / chans)
        second = jnp.sum(d * nhat, axis=-1, keepdims=True) * (1.0 / chans)
        rstd = rstd_ref[at, :]
        g = jnp.concatenate([rstd, rstd], axis=1) * (d - first - nhat * second)
        g_ref[i] = g.astype(BF16)
        return 0

    lax.fori_loop(0, rows, back, 0, unroll=4)


def branch(x, halo, cot, tissue, w, bias, gain, shift, we, be, wr, scale):
    rows, cols, chans = x.shape
    hidden = we.shape[1]
    pix = TILE * cols
    block = pl.BlockSpec((TILE, cols, chans), lambda s, t: (s, 0, 0))
    grid = pltpu.PrefetchScalarGridSpec(
        num_scalar_prefetch=1,
        grid=(rows // TILE,),
        in_specs=[VMEM] * 5 + [block] + [VMEM] * 8,
        out_specs=[block, pl.BlockSpec((2 * chans, hidden), lambda s, t: (0, 0))],
        scratch_shapes=[
            pltpu.VMEM((2, rows + 6, cols + 16, LANES), F32),
            pltpu.VMEM((2, 49, 8, LANES), F32),
            pltpu.VMEM((pix, chans), F32),
            pltpu.VMEM((pix, LANES), F32),
            pltpu.VMEM((pix, chans), BF16),
            pltpu.VMEM((chans, pix), BF16),
            pltpu.VMEM((pix, chans), BF16),
            pltpu.VMEM((chans, pix), BF16),
            pltpu.VMEM((pix, 256), BF16),
            pltpu.VMEM((pix, 256), BF16),
            pltpu.VMEM((pix, chans), F32),
        ],
    )
    return pl.pallas_call(
        branch_kernel,
        grid_spec=grid,
        out_shape=(
            jax.ShapeDtypeStruct(x.shape, BF16),
            jax.ShapeDtypeStruct((2 * chans, hidden), F32),
        ),
        compiler_params=pltpu.CompilerParams(**PARAMS),
        name="branch",
    )(tissue, x, *halo, cot, w, bias, gain, shift, we, be, wr, scale)


def filter_kernel(x_ref, top, bottom, left, right, g_ref, o_ref, pad, gpad):
    rows, cols, _ = g_ref.shape
    fill(pad, x_ref, top, bottom, left, right)
    o_ref[...] = jnp.zeros_like(o_ref)
    for h in range(2):
        for i in range(3):
            gpad[i] = jnp.zeros((cols, LANES), F32)
            gpad[rows + 3 + i] = jnp.zeros((cols, LANES), F32)

        def put(i, _):
            gpad[3 + i] = g_ref[i, :, half(h)].astype(F32)
            return 0

        lax.fori_loop(0, rows, put, 0, unroll=4)
        for first, count in ((0, 4), (4, 3)):

            def step(n, accs):
                r, col = first + n // (cols // 8), (n % (cols // 8)) * 8
                xs = [pad[h, r, pl.ds(col + 5 + b, 8), :] for b in range(7)]
                out = []
                for k in range(count):
                    g = gpad[r - (first + k) + 3, pl.ds(pl.multiple_of(col, 8), 8), :]
                    out += [accs[k * 7 + b] + xs[b] * g for b in range(7)]
                return tuple(out)

            zero = jnp.zeros((8, LANES), F32)
            accs = lax.fori_loop(
                0, (rows + count - 1) * (cols // 8), step, (zero,) * (7 * count), unroll=6
            )
            for k in range(count):
                for b in range(7):
                    t = (first + k) * 7 + b
                    at = (t % 4) * 256 + h * LANES
                    o_ref[t // 4 : t // 4 + 1, at : at + LANES] = jnp.sum(
                        accs[k * 7 + b], axis=0, keepdims=True
                    )


def filter_grad(x, halo, g):
    rows, cols, _ = x.shape
    return pl.pallas_call(
        filter_kernel,
        out_shape=jax.ShapeDtypeStruct((DW_ROWS, 1024), F32),
        in_specs=[VMEM] * 6,
        out_specs=VMEM,
        scratch_shapes=[
            pltpu.VMEM((2, rows + 6, cols + 16, LANES), F32),
            pltpu.VMEM((rows + 6, cols, LANES), F32),
        ],
        compiler_params=pltpu.CompilerParams(**PARAMS),
        name="filter_grad",
    )(x, *halo, g)


def input_kernel(g_ref, top, bottom, left, right, cot, w_ref, o_ref, pad, wide):
    rows, cols, _ = g_ref.shape
    spread_weights(w_ref, wide, True)
    fill(pad, g_ref, top, bottom, left, right)
    ng = cols // (8 * CB)
    for h in range(2):

        def step(n, _):
            row, col = (n // ng) * RG, (n % ng) * (8 * CB)
            acc = stencil(pad, wide, h, row, col)
            for i in range(RG):
                at = pl.ds(pl.multiple_of(col, 8), 8 * CB)
                value = jnp.concatenate(acc[i], axis=0)
                o_ref[row + i, at, half(h)] = (
                    cot[row + i, at, half(h)].astype(F32) + value
                ).astype(BF16)
            return 0

        lax.fori_loop(0, (rows // RG) * ng, step, 0)


def input_grad(g, halo, cot, w):
    rows, cols, _ = g.shape
    return pl.pallas_call(
        input_kernel,
        out_shape=jax.ShapeDtypeStruct(g.shape, BF16),
        in_specs=[VMEM] * 7,
        out_specs=VMEM,
        scratch_shapes=[
            pltpu.VMEM((2, rows + 6, cols + 16, LANES), F32),
            pltpu.VMEM((2, 49, 8, LANES), F32),
        ],
        compiler_params=pltpu.CompilerParams(**PARAMS),
        name="input_grad",
    )(g, *halo, cot, w)


def shifts(count):
    forward = [(i, i + 1) for i in range(count - 1)]
    return forward, [(b, a) for a, b in forward]


def halo_of(block, ty, tx, sizes):
    rows, cols = block.shape[:2]
    forward, backward = shifts(sizes[0])
    top = lax.ppermute(block[rows - 3 :], ty, forward)
    bottom = lax.ppermute(block[:3], ty, backward)

    def edge(at):
        parts = [p[:, at : at + 3].transpose(1, 0, 2) for p in (top, block, bottom)]
        return jnp.concatenate(parts, axis=1)

    forward, backward = shifts(sizes[1])
    left = lax.ppermute(edge(cols - 3), tx, forward)
    right = lax.ppermute(edge(0), tx, backward)
    return top, bottom, left, right


AXES = ("y", "x_hi", "core", "z", "x_lo")
SIZES = (4, 2, 2, 8, 2)
TY, TX = AXES[:3], AXES[3:]
PAIRS = ("core", "x_lo", "x_hi")
REST = ("y", "z")


def swap(value, axis):
    at = AXES.index(axis)
    index = np.arange(math.prod(SIZES)).reshape(SIZES)
    other = np.flip(index, axis=at)
    pairs = [(int(a), int(b)) for a, b in zip(index.ravel(), other.ravel())]
    return lax.ppermute(value, AXES, pairs)


def total(parts):
    parts = list(parts)
    rows = sum(p.shape[0] for p in parts)
    for axis in PAIRS:
        upper = lax.axis_index(axis) == 1
        width = parts[0].shape[1] // 2
        send = [jnp.where(upper, p[:, :width], p[:, width:]) for p in parts]
        got = swap(jnp.concatenate([s.astype(BF16) for s in send]), axis).astype(F32)
        kept, first = [], 0
        for p in parts:
            mine = jnp.where(upper, p[:, width:], p[:, :width])
            kept.append(mine + got[first : first + p.shape[0]])
            first += p.shape[0]
        parts = kept
    count = math.prod(SIZES[AXES.index(a)] for a in REST)
    whole = jnp.concatenate([p.astype(BF16) for p in parts])
    width = whole.shape[1]
    split = whole.reshape(count, rows // count, width)
    split = lax.all_to_all(split, REST, 0, 0, tiled=True)
    mine = jnp.sum(split.astype(F32), axis=0).astype(BF16)
    out = lax.all_to_all(jnp.broadcast_to(mine, split.shape), REST, 0, 0, tiled=True)
    out = out.reshape(rows, width)
    for axis in reversed(PAIRS):
        upper = lax.axis_index(axis) == 1
        got = swap(out, axis)
        low, high = jnp.where(upper, got, out), jnp.where(upper, out, got)
        out = jnp.concatenate([low, high], axis=1)
    return out


def body(x, cot, tissue, w, bias, gain, shift, we, be, wr, scale):
    rows, cols, chans = x.shape
    line = lambda v: v.reshape(1, -1)
    sizes = (math.prod(SIZES[:3]), math.prod(SIZES[3:]))
    factor = 1.0 / math.sqrt(rows * sizes[0] * cols * sizes[1])
    halo = halo_of(x, TY, TX, sizes)
    g, sums = branch(
        x, halo, cot, tissue, w, line(bias), line(gain), line(shift), we, line(be), wr, line(scale)
    )
    dw = filter_grad(x, halo, g)
    result = input_grad(g, halo_of(g, TY, TX, sizes), cot, w)
    out = total((sums, dw)).astype(F32) * factor
    taps = out[2 * chans :].reshape(-1, chans)[: w.shape[0]]
    return result, taps, out[:chans], out[chans : 2 * chans].T


def solution(mesh):
    fine = Mesh(mesh.devices.reshape(SIZES), AXES)
    pixels = P(TY, TX, None)
    return jax.shard_map(
        body,
        mesh=fine,
        in_specs=(pixels, pixels, P(TY, TX)) + (P(),) * 8,
        out_specs=(pixels, P(), P(), P()),
        check_vma=False,
    )
```

time: 528 us -> 205 us (0.39)
  waiting for transfers between devices: 233 us -> 45.5 us
  other arithmetic: 143 us -> 3.85 us
  Pallas kernels: 0 us -> 89.3 us
  blocking collectives: 84.7 us -> 22.2 us
  matrix products: 23.2 us -> 0 us
  between operations: 14.7 us -> 1.08 us
  starting transfers between devices: 21.1 us -> 29.8 us
    psum x1 -> x0, waiting for transfers between devices: 223 us -> none  [body(): lax.psum((local_expand, local_reduce, local_dw), ('ty', 'tx'))]
    reduce_sum x8 -> x1, other arithmetic: 92.3 us -> 0.05 us  [total(): mine = jnp.sum(split.astype(F32), axis=0).astype(BF16)]
    pallas_call x0 -> x3, Pallas kernels: none -> 89.3 us  [the longest x1 48.8 us: branch(): pl.pallas_call(branch_kernel, grid_spec=grid, out_shape=(jax.ShapeDtypeSt...]
    psum x1 -> x0, blocking collectives: 84.7 us -> none  [body(): lax.psum((local_expand, local_reduce, local_dw), ('ty', 'tx'))]
    convert_element_type x6 -> x11, other arithmetic: 43.1 us -> 2.36 us  [the longest x3 1.23 us: total(): swap(jnp.concatenate([s.astype(BF16) for s in send]), axis).astype(F32)]
    ppermute x8 -> x14, waiting for transfers between devices: 9.83 us -> 35.3 us  [the longest x6 23.7 us: swap(): return lax.ppermute(value, AXES, pairs)]
    dot_general x5 -> x0, matrix products: 23.2 us -> none  [the longest x1 6.95 us: branch_back(): dhid = jnp.dot(go_vals, w_reduce.T, preferred_element_type=jnp.float32)]
    all_to_all x0 -> x1, blocking collectives: none -> 22.2 us  [total(): split = lax.all_to_all(split, REST, 0, 0, tiled=True)]
  transfers between devices with their start and end apart: 9 -> 15, of which waited for: 4 -> 10; matrix products, arithmetic and copies ran while one was open for 13% -> 2% of each run, Pallas kernels for 0% -> 10%
where the time goes in v1:
time: 205 us; the launch traced here: 203 us
  Pallas kernels  89.3 us (44%)
  waiting for transfers between devices  45.5 us (22%)
  starting transfers between devices  29.8 us (15%)
  blocking collectives  22.2 us (11%)
  local copies, waits for them, and re-layouts  11.7 us (6%)
  other arithmetic  3.85 us (2%)
    pallas_call x1, Pallas kernels, branch(): pl.pallas_call(branch_kernel, grid_spec=grid, out_shape=(jax.ShapeDtypeSt...  48.8 us
    ppermute x6, waiting for transfers between devices, swap(): return lax.ppermute(value, AXES, pairs)  23.7 us
    all_to_all x1, blocking collectives, total(): split = lax.all_to_all(split, REST, 0, 0, tiled=True)  22.2 us
    pallas_call x1, Pallas kernels, filter_grad(): pl.pallas_call(filter_kernel, out_shape=jax.ShapeDtypeStruct((DW_ROWS, 10...  20.7 us
    pallas_call x1, Pallas kernels, input_grad(): pl.pallas_call(input_kernel, out_shape=jax.ShapeDtypeStruct(g.shape, BF16...  19.7 us
    all_to_all x1, waiting for transfers between devices, total(): lax.all_to_all(jnp.broadcast_to(mine, split.shape), REST, 0, 0, tiled=True)  10.1 us
    ppermute x2, waiting for transfers between devices, halo_of(): right = lax.ppermute(edge(0), tx, backward)  8.94 us
    ppermute x2, starting transfers between devices, halo_of(): left = lax.ppermute(edge(cols - 3), tx, forward)  8.63 us
  transfers between devices with their start and end apart: 15, of which 10 were waited for; matrix products, arithmetic and copies ran while one was open for 2% of the time, Pallas kernels for 10%

profile of v1, /device:TPU:2, one launch (start us, length us, event | category | flops | bytes accessed | tf_op | source)
XLA Modules:
  0.0 203.4 jit_solution(16457777617224844663)
XLA Ops:
  0.6 0.9 fusion.4
  1.6 1.7 collective-permute-start
  3.4 1.3 collective-permute-start.1
  4.7 1.1 fusion.3
  6.0 2.6 %collective-permute-done.1 = bf16[3,48,256]{2,0,1:T(4,128)(2,1)S(1)} collective-permute-done((bf16[3,48,256]{2,0,1:T(4,128)(2,1)S(1)}, bf16[3,48,256]{2,0,1:T(4,128)(2,1)S(1)}, u32[]{:S(2)}, u32[]{:S(2)}) %collective-permute-start.1) | collective-permute-done | bytes 73760 | tf_op jit(solution)/shard_map/ppermute | solution.py:297
  8.6 4.7 %collective-permute-start.2 = (bf16[3,70,256]{2,1,0:T(8,128)(2,1)S(1)}, bf16[3,70,256]{2,1,0:T(8,128)(2,1)S(1)}, u32[]{:S(2)}, u32[]{:S(2)}) collective-permute-start(bf16[3,70,256]{2,1,0:T(8,128)(2,1)S(1)} %pad_maximum_fusion.6), channel_id=1, source_target_pairs={{0,1},{1,2},{2,3},{3,4},{4,5},{5,6},{6,7},{7,8},{8,9},{9,10},{10,1... | collective-permute-start | bytes 322568 | tf_op jit(solution)/shard_map/ppermute | solution.py:304
  13.3 1.9 collective-permute-start.3
  16.5 4.3 %collective-permute-done.3.right = bf16[3,70,256]{2,1,0:T(8,128)(2,1)S(1)} collective-permute-done((bf16[3,70,256]{2,1,0:T(8,128)(2,1)S(1)}, bf16[3,70,256]{2,1,0:T(8,128)(2,1)S(1)}, u32[]{:S(2)}, u32[]{:S(2)}) %collective-permute-start.3) | collective-permute-done | bytes 107552 | tf_op jit(solution)/shard_map/ppermute | solution.py:305
  21.5 48.8 %branch.1 = (bf16[64,48,256]{2,1,0:T(8,128)(2,1)}, f32[512,1024]{1,0:T(8,128)}) custom-call(s32[4,3]{1,0:T(4,128)} %tissue.1, bf16[64,48,256]{2,1,0:T(8,128)(2,1)} %x_ref.3, bf16[3,48,256]{2,1,0:T(8,128)(2,1)} %copy.34.top, bf16[3,48,256]{2,1,0:T(8,128)(2,1)} %copy.35.bottom, bf16[3,70,256]{2,1,0:T(8,128)(2,1)} %copy-done.4, bf16[3,70,256]{2,1,0:T(8,128)(2,1)} %copy-done.5, ...), custom_call_target="tpu_custom_call" | custom-call | tf_op jit(solution)/shard_map/branch/pallas_call | solution.py:185
  70.4 20.7 %filter_grad.1 = f32[32,1024]{1,0:T(8,128)} custom-call(bf16[64,48,256]{2,1,0:T(8,128)(2,1)} %x_ref.3, bf16[3,48,256]{2,1,0:T(8,128)(2,1)} %copy.34.top, bf16[3,48,256]{2,1,0:T(8,128)(2,1)} %copy.35.bottom, bf16[3,70,256]{2,1,0:T(8,128)(2,1)} %copy-done.4, bf16[3,70,256]{2,1,0:T(8,128)(2,1)} %copy-done.5, bf16[64,48,256]{2,1,0:T(8,128)(2,1)} %get-tuple-element.6.g_ref), custom_call_target="tpu_custom_call" | custom-call | tf_op jit(solution)/shard_map/filter_grad/pallas_call | solution.py:237
  91.1 0.9 select_convert_fusion.3
  92.1 3.4 %collective-permute-start.8 = (bf16[544,512]{1,0:T(8,128)(2,1)S(1)}, bf16[544,512]{1,0:T(8,128)(2,1)}, u32[]{:S(2)}, u32[]{:S(2)}) collective-permute-start(bf16[544,512]{1,0:T(8,128)(2,1)S(1)} %pad_maximum_fusion), channel_id=1, source_target_pairs={{0,16},{1,17},{2,18},{3,19},{4,20},{5,21},{6,22},{7,23},{8,24},{9,... | collective-permute-start | bytes 1671176 | tf_op jit(solution)/shard_map/ppermute | solution.py:321
  95.5 1.7 collective-permute-done.8
  97.2 1.2 convert_element_type.40
  99.6 8.9 %collective-permute-done.9 = bf16[544,256]{1,0:T(8,128)(2,1)S(1)} collective-permute-done((bf16[544,256]{1,0:T(8,128)(2,1)S(1)}, bf16[544,256]{1,0:T(8,128)(2,1)S(1)}, u32[]{:S(2)}, u32[]{:S(2)}) %collective-permute-start.9) | collective-permute-done | bytes 278560 | tf_op jit(solution)/shard_map/ppermute | solution.py:321
  108.7 1.9 collective-permute-start.10
  110.6 4.8 %collective-permute-done.10 = bf16[544,128]{1,0:T(8,128)(2,1)S(1)} collective-permute-done((bf16[544,128]{1,0:T(8,128)(2,1)S(1)}, bf16[544,128]{1,0:T(8,128)(2,1)S(1)}, u32[]{:S(2)}, u32[]{:S(2)}) %collective-permute-start.10) | collective-permute-done | bytes 139296 | tf_op jit(solution)/shard_map/ppermute | solution.py:321
  115.6 22.2 %all_to_all.10 = bf16[32,17,128]{2,1,0:T(8,128)(2,1)S(1)} all-to-all(bf16[32,17,128]{2,1,0:T(8,128)(2,1)S(1)} %reshape.37), channel_id=1, replica_groups=mesh['y'=4,'x_hi'=2,'core'=2,'z'=8,'x_lo'=2] {'y','z'}, dimensions={0} | all-to-all | bytes 278528 | tf_op jit(solution)/shard_map/all_to_all | solution.py:342
  138.5 3.9 %all-to-all-start.1 = ((bf16[32,17,128]{2,1,0:T(8,128)(2,1)}), bf16[32,17,128]{2,1,0:T(8,128)(2,1)S(1)}, u32[]{:S(2)}, u32[]{:S(2)}) async-start(bf16[32,17,128]{2,1,0:T(8,128)(2,1)} %broadcast_in_dim.3), calls=%async_computation.1 | async-start | bytes 393216 | tf_op jit(solution)/shard_map/all_to_all | solution.py:344
  143.0 10.1 %all-to-all-done.1 = bf16[32,17,128]{2,1,0:T(8,128)(2,1)S(1)} async-done(((bf16[32,17,128]{2,1,0:T(8,128)(2,1)}), bf16[32,17,128]{2,1,0:T(8,128)(2,1)S(1)}, u32[]{:S(2)}, u32[]{:S(2)}) %all-to-all-start.1) | async-done | bytes 139296 | tf_op jit(solution)/shard_map/all_to_all | solution.py:344
  153.1 1.6 collective-permute-start.11
  154.8 1.3 collective-permute-start.5
  156.1 3.7 %collective-permute-done.11 = bf16[544,128]{1,0:T(8,128)(2,1)S(1)} collective-permute-done((bf16[544,128]{1,0:T(8,128)(2,1)S(1)}, bf16[544,128]{1,0:T(8,128)(2,1)S(1)}, u32[]{:S(2)}, u32[]{:S(2)}) %collective-permute-start.11) | collective-permute-done | bytes 139296 | tf_op jit(solution)/shard_map/ppermute | solution.py:321
  159.9 0.8 collective-permute-start.12
  160.6 1.3 collective-permute-start.4
  162.0 4.5 %collective-permute-done.12 = bf16[544,256]{1,0:T(8,128)(2,1)S(1)} collective-permute-done((bf16[544,256]{1,0:T(8,128)(2,1)S(1)}, bf16[544,256]{1,0:T(8,128)(2,1)S(1)}, u32[]{:S(2)}, u32[]{:S(2)}) %collective-permute-start.12) | collective-permute-done | bytes 278560 | tf_op jit(solution)/shard_map/ppermute | solution.py:321
  166.8 3.9 %collective-permute-start.6 = (bf16[3,70,256]{2,1,0:T(8,128)(2,1)S(1)}, bf16[3,70,256]{2,1,0:T(8,128)(2,1)S(1)}, u32[]{:S(2)}, u32[]{:S(2)}) collective-permute-start(bf16[3,70,256]{2,1,0:T(8,128)(2,1)S(1)} %pad_maximum_fusion.8), channel_id=1, source_target_pairs={{0,1},{1,2},{2,3},{3,4},{4,5},{5,6},{6,7},{7,8},{8,9},{9,10},{10,1... | collective-permute-start | bytes 322568 | tf_op jit(solution)/shard_map/ppermute | solution.py:304
  170.8 1.9 collective-permute-start.7
  174.2 4.6 %collective-permute-done.7.right = bf16[3,70,256]{2,1,0:T(8,128)(2,1)S(1)} collective-permute-done((bf16[3,70,256]{2,1,0:T(8,128)(2,1)S(1)}, bf16[3,70,256]{2,1,0:T(8,128)(2,1)S(1)}, u32[]{:S(2)}, u32[]{:S(2)}) %collective-permute-start.7) | collective-permute-done | bytes 107552 | tf_op jit(solution)/shard_map/ppermute | solution.py:305
  179.4 19.7 %input_grad.1 = bf16[64,48,256]{2,1,0:T(8,128)(2,1)} custom-call(bf16[64,48,256]{2,1,0:T(8,128)(2,1)} %get-tuple-element.6.g_ref, bf16[3,48,256]{2,1,0:T(8,128)(2,1)} %copy.40.top, bf16[3,48,256]{2,1,0:T(8,128)(2,1)} %copy.41.bottom, bf16[3,70,256]{2,1,0:T(8,128)(2,1)} %copy-done.6, bf16[3,70,256]{2,1,0:T(8,128)(2,1)} %copy-done.7, ...), custom_call_target="tpu_custom_call" | custom-call | tf_op jit(solution)/shard_map/input_grad/pallas_call | solution.py:274
  199.7 1.3 slice_bitcast_fusion
  201.4 1.3 copy.44
  (74 shorter events, 9.2 us)
Async XLA Ops:
  1.6 4.3 %collective-permute-start = (bf16[3,48,256]{2,0,1:T(4,128)(2,1)S(1)}, bf16[3,48,256]{2,0,1:T(4,128)(2,1)S(1)}, u32[]{:S(2)}, u32[]{:S(2)}) collective-permute-start(bf16[3,48,256]{2,0,1:T(4,128)(2,1)S(1)} %copy.45), channel_id=1, source_target_pairs={{0,16},{16,32},{32,48},{48,64},{64,80},{80,96},{96,112},{112,128},... | collective-permute-start | bytes 221192 | tf_op jit(solution)/shard_map/ppermute | solution.py:296
  3.4 5.1 %collective-permute-start.1 = (bf16[3,48,256]{2,0,1:T(4,128)(2,1)S(1)}, bf16[3,48,256]{2,0,1:T(4,128)(2,1)S(1)}, u32[]{:S(2)}, u32[]{:S(2)}) collective-permute-start(bf16[3,48,256]{2,0,1:T(4,128)(2,1)S(1)} %copy.46), channel_id=1, source_target_pairs={{16,0},{32,16},{48,32},{64,48},{80,64},{96,80},{112,96},{128,112},... | collective-permute-start | bytes 221192 | tf_op jit(solution)/shard_map/ppermute | solution.py:297
  8.6 7.9 %collective-permute-start.2 = (bf16[3,70,256]{2,1,0:T(8,128)(2,1)S(1)}, bf16[3,70,256]{2,1,0:T(8,128)(2,1)S(1)}, u32[]{:S(2)}, u32[]{:S(2)}) collective-permute-start(bf16[3,70,256]{2,1,0:T(8,128)(2,1)S(1)} %pad_maximum_fusion.6), channel_id=1, source_target_pairs={{0,1},{1,2},{2,3},{3,4},{4,5},{5,6},{6,7},{7,8},{8,9},{9,10},{10,1... | collective-permute-start | bytes 322568 | tf_op jit(solution)/shard_map/ppermute | solution.py:304
  13.3 7.5 %collective-permute-start.3 = (bf16[3,70,256]{2,1,0:T(8,128)(2,1)S(1)}, bf16[3,70,256]{2,1,0:T(8,128)(2,1)S(1)}, u32[]{:S(2)}, u32[]{:S(2)}) collective-permute-start(bf16[3,70,256]{2,1,0:T(8,128)(2,1)S(1)} %pad_maximum_fusion.7), channel_id=1, source_target_pairs={{1,0},{2,1},{3,2},{4,3},{5,4},{6,5},{7,6},{8,7},{9,8},{10,9},{11,1... | collective-permute-start | bytes 322568 | tf_op jit(solution)/shard_map/ppermute | solution.py:305
  16.5 4.3 %copy-start.4 = (bf16[3,70,256]{2,1,0:T(8,128)(2,1)}, bf16[3,70,256]{2,1,0:T(8,128)(2,1)S(1)}, u32[]{:S(2)}) copy-start(bf16[3,70,256]{2,1,0:T(8,128)(2,1)S(1)} %collective-permute-done.2.left) | copy-start | bytes 322564
  20.9 0.6 copy-start.5
  70.3 21.6 %copy-start.2 = (f32[512,1024]{1,0:T(8,128)S(1)}, f32[512,1024]{1,0:T(8,128)}, u32[]{:S(2)}) copy-start(f32[512,1024]{1,0:T(8,128)} %get-tuple-element.7) | copy-start | bytes 6291460
  92.1 5.1 %collective-permute-start.8 = (bf16[544,512]{1,0:T(8,128)(2,1)S(1)}, bf16[544,512]{1,0:T(8,128)(2,1)}, u32[]{:S(2)}, u32[]{:S(2)}) collective-permute-start(bf16[544,512]{1,0:T(8,128)(2,1)S(1)} %pad_maximum_fusion), channel_id=1, source_target_pairs={{0,16},{1,17},{2,18},{3,19},{4,20},{5,21},{6,22},{7,23},{8,24},{9,... | collective-permute-start | bytes 1671176 | tf_op jit(solution)/shard_map/ppermute | solution.py:321
  98.4 0.9 copy-start.3
  99.5 9.0 %collective-permute-start.9 = (bf16[544,256]{1,0:T(8,128)(2,1)S(1)}, bf16[544,256]{1,0:T(8,128)(2,1)S(1)}, u32[]{:S(2)}, u32[]{:S(2)}) collective-permute-start(bf16[544,256]{1,0:T(8,128)(2,1)S(1)} %pad_maximum_fusion.2), channel_id=1, source_target_pairs={{0,1},{1,0},{2,3},{3,2},{4,5},{5,4},{6,7},{7,6},{8,9},{9,8},{10,11... | collective-permute-start | bytes 835592 | tf_op jit(solution)/shard_map/ppermute | solution.py:321
  108.7 33.7 %copy-start = (bf16[64,48,256]{2,1,0:T(8,128)(2,1)S(1)}, bf16[64,48,256]{2,1,0:T(8,128)(2,1)}, u32[]{:S(2)}) copy-start(bf16[64,48,256]{2,1,0:T(8,128)(2,1)} %get-tuple-element.6.g_ref) | copy-start | bytes 4718596
  108.7 6.7 %collective-permute-start.10 = (bf16[544,128]{1,0:T(8,128)(2,1)S(1)}, bf16[544,128]{1,0:T(8,128)(2,1)S(1)}, u32[]{:S(2)}, u32[]{:S(2)}) collective-permute-start(bf16[544,128]{1,0:T(8,128)(2,1)S(1)} %pad_maximum_fusion.4), channel_id=1, source_target_pairs={{0,32},{1,33},{2,34},{3,35},{4,36},{5,37},{6,38},{7,39},{8,40},{9,... | collective-permute-start | bytes 417800 | tf_op jit(solution)/shard_map/ppermute | solution.py:321
  138.5 14.6 %all-to-all-start.1 = ((bf16[32,17,128]{2,1,0:T(8,128)(2,1)}), bf16[32,17,128]{2,1,0:T(8,128)(2,1)S(1)}, u32[]{:S(2)}, u32[]{:S(2)}) async-start(bf16[32,17,128]{2,1,0:T(8,128)(2,1)} %broadcast_in_dim.3), calls=%async_computation.1 | async-start | bytes 393216 | tf_op jit(solution)/shard_map/all_to_all | solution.py:344
  153.1 6.6 %collective-permute-start.11 = (bf16[544,128]{1,0:T(8,128)(2,1)S(1)}, bf16[544,128]{1,0:T(8,128)(2,1)S(1)}, u32[]{:S(2)}, u32[]{:S(2)}) collective-permute-start(bf16[544,128]{1,0:T(8,128)(2,1)S(1)} %reshape.38), channel_id=1, source_target_pairs={{0,32},{1,33},{2,34},{3,35},{4,36},{5,37},{6,38},{7,39},{8,40},{9,... | collective-permute-start | bytes 417800 | tf_op jit(solution)/shard_map/ppermute | solution.py:321
  154.8 7.2 %collective-permute-start.5 = (bf16[3,48,256]{2,0,1:T(4,128)(2,1)S(1)}, bf16[3,48,256]{2,0,1:T(4,128)(2,1)S(1)}, u32[]{:S(2)}, u32[]{:S(2)}) collective-permute-start(bf16[3,48,256]{2,0,1:T(4,128)(2,1)S(1)} %get-tuple-element.20), channel_id=1, source_target_pairs={{16,0},{32,16},{48,32},{64,48},{80,64},{96,80},{112,96},{128,112},... | collective-permute-start | bytes 221192 | tf_op jit(solution)/shard_map/ppermute | solution.py:297
  159.9 6.6 %collective-permute-start.12 = (bf16[544,256]{1,0:T(8,128)(2,1)S(1)}, bf16[544,256]{1,0:T(8,128)(2,1)S(1)}, u32[]{:S(2)}, u32[]{:S(2)}) collective-permute-start(bf16[544,256]{1,0:T(8,128)(2,1)S(1)} %pad_maximum_fusion.3), channel_id=1, source_target_pairs={{0,1},{1,0},{2,3},{3,2},{4,5},{5,4},{6,7},{7,6},{8,9},{9,8},{10,11... | collective-permute-start | bytes 835592 | tf_op jit(solution)/shard_map/ppermute | solution.py:321
  160.6 6.1 %collective-permute-start.4 = (bf16[3,48,256]{2,0,1:T(4,128)(2,1)S(1)}, bf16[3,48,256]{2,0,1:T(4,128)(2,1)S(1)}, u32[]{:S(2)}, u32[]{:S(2)}) collective-permute-start(bf16[3,48,256]{2,0,1:T(4,128)(2,1)S(1)} %get-tuple-element.21), channel_id=1, source_target_pairs={{0,16},{16,32},{32,48},{48,64},{64,80},{80,96},{96,112},{112,128},... | collective-permute-start | bytes 221192 | tf_op jit(solution)/shard_map/ppermute | solution.py:296
  166.7 32.5 %collective-permute-start.13 = (bf16[544,512]{1,0:T(8,128)(2,1)S(1)}, bf16[544,512]{1,0:T(8,128)(2,1)S(1)}, u32[]{:S(2)}, u32[]{:S(2)}) collective-permute-start(bf16[544,512]{1,0:T(8,128)(2,1)S(1)} %pad_maximum_fusion.1), channel_id=1, source_target_pairs={{0,16},{1,17},{2,18},{3,19},{4,20},{5,21},{6,22},{7,23},{8,24},{9,... | collective-permute-start | bytes 1671176 | tf_op jit(solution)/shard_map/ppermute | solution.py:321
  166.8 7.3 %collective-permute-start.6 = (bf16[3,70,256]{2,1,0:T(8,128)(2,1)S(1)}, bf16[3,70,256]{2,1,0:T(8,128)(2,1)S(1)}, u32[]{:S(2)}, u32[]{:S(2)}) collective-permute-start(bf16[3,70,256]{2,1,0:T(8,128)(2,1)S(1)} %pad_maximum_fusion.8), channel_id=1, source_target_pairs={{0,1},{1,2},{2,3},{3,4},{4,5},{5,6},{6,7},{7,8},{8,9},{9,10},{10,1... | collective-permute-start | bytes 322568 | tf_op jit(solution)/shard_map/ppermute | solution.py:304
  170.8 8.0 %collective-permute-start.7 = (bf16[3,70,256]{2,1,0:T(8,128)(2,1)S(1)}, bf16[3,70,256]{2,1,0:T(8,128)(2,1)S(1)}, u32[]{:S(2)}, u32[]{:S(2)}) collective-permute-start(bf16[3,70,256]{2,1,0:T(8,128)(2,1)S(1)} %pad_maximum_fusion.9), channel_id=1, source_target_pairs={{1,0},{2,1},{3,2},{4,3},{5,4},{6,5},{7,6},{8,7},{9,8},{10,9},{11,1... | collective-permute-start | bytes 322568 | tf_op jit(solution)/shard_map/ppermute | solution.py:305
  174.2 4.6 %copy-start.6 = (bf16[3,70,256]{2,1,0:T(8,128)(2,1)}, bf16[3,70,256]{2,1,0:T(8,128)(2,1)S(1)}, u32[]{:S(2)}) copy-start(bf16[3,70,256]{2,1,0:T(8,128)(2,1)S(1)} %collective-permute-done.6.left) | copy-start | bytes 322564
  178.8 0.6 copy-start.7
  199.7 1.7 copy-start.1
  201.4 1.3 slice-start

commit v2 on v1

v2 whole, which is shorter than its diff:
```python
import math

import jax
import jax.numpy as jnp
import numpy as np
from jax import lax
from jax.experimental import pallas as pl
from jax.experimental.pallas import tpu as pltpu
from jax.sharding import Mesh, PartitionSpec as P


F32, BF16 = jnp.float32, jnp.bfloat16
TILE = 16
LANES = 128
RG = 8
CB = 3
TAPS = 64
VMEM = pl.BlockSpec(memory_space=pltpu.VMEM)
PARAMS = dict(vmem_limit_bytes=56 << 20)


def nn(a, b):
    return lax.dot_general(a, b, (((1,), (0,)), ((), ())), preferred_element_type=F32)


def nt(a, b):
    return lax.dot_general(a, b, (((1,), (1,)), ((), ())), preferred_element_type=F32)


def half(h):
    return slice(h * LANES, (h + 1) * LANES)


def spread_weights(w_ref, wide, flip, halves=(0, 1)):
    for k, h in enumerate(halves):
        for t in range(49):
            s = 48 - t if flip else t
            wide[k, t] = jnp.broadcast_to(w_ref[s : s + 1, half(h)], (8, LANES))


def fill(pad, core, top, bottom, left, right, halves=(0, 1)):
    rows, cols = core.shape[0], core.shape[1]
    for k, h in enumerate(halves):

        def put(i, _):
            pad[k, 3 + i, 8 : 8 + cols, :] = core[i, :, half(h)].astype(F32)
            return 0

        lax.fori_loop(0, rows, put, 0, unroll=4)
        for i in range(3):
            pad[k, i, 8 : 8 + cols, :] = top[i, :, half(h)].astype(F32)
            pad[k, 3 + rows + i, 8 : 8 + cols, :] = bottom[i, :, half(h)].astype(F32)

        def side(first, count):
            for j in range(3):
                lv = left[j, pl.ds(first, count), half(h)].astype(F32)
                rv = right[j, pl.ds(first, count), half(h)].astype(F32)
                for r in range(count):
                    pad[k, first + r, 5 + j : 6 + j, :] = lv[r : r + 1]
                    pad[k, first + r, 8 + cols + j : 9 + cols + j, :] = rv[r : r + 1]

        def eight(i, _):
            side(i * 8, 8)
            return 0

        lax.fori_loop(0, (rows + 6) // 8, eight, 0)
        side((rows + 6) // 8 * 8, (rows + 6) % 8)


def stencil(pad, wide, h, row, col):
    acc = [[None] * CB for _ in range(RG)]
    for b in range(7):
        w = [wide[h, a * 7 + b] for a in range(7)]
        for r in range(RG + 6):
            for c in range(CB):
                v = pad[h, row + r, pl.ds(col + c * 8 + 5 + b, 8), :]
                for a in range(7):
                    i = r - a
                    if 0 <= i < RG:
                        p = v * w[a]
                        acc[i][c] = p if acc[i][c] is None else acc[i][c] + p
    return acc


def branch_kernel(
    tissue, x_ref, top, bottom, left, right, cot, w_ref, bias, gain, shift, we, be, wr, scale,
    g_ref, acc_ref,
    pad, wide, u_ref, nhat_ref, rstd_ref, normed, normed_t, go, go_t, hid, dz, dn,
):
    step = pl.program_id(0)
    rows, cols, chans = cot.shape
    hidden = we.shape[1]
    chunk = 256

    @pl.when(step == 0)
    def _():
        spread_weights(w_ref, wide, False)
        fill(pad, x_ref, top, bottom, left, right)
        acc_ref[...] = jnp.zeros_like(acc_ref)

    ng = cols // (8 * CB)
    for h in range(2):

        def conv(n, _):
            row, col = (n // ng) * RG, (n % ng) * (8 * CB)
            acc = stencil(pad, wide, h, step * rows + row, col)
            for i in range(RG):
                for c in range(CB):
                    at = pl.multiple_of((row + i) * cols + col + c * 8, 8)
                    u_ref[pl.ds(at, 8), half(h)] = acc[i][c] + bias[0:1, half(h)]
            return 0

        lax.fori_loop(0, (rows // RG) * ng, conv, 0)

    tiles = cols // TILE
    for c in range(tiles):
        keep = tissue[step, c].astype(F32)
        part = cot[:, c * TILE : (c + 1) * TILE, :].astype(F32) * (scale[0:1, :] * keep)
        for i in range(rows):
            go[i * cols + c * TILE : i * cols + (c + 1) * TILE, :] = part[i].astype(BF16)

    def norm(i, _):
        at = pl.ds(pl.multiple_of(i * cols, cols), cols)
        u = u_ref[at, :]
        center = u - jnp.sum(u, axis=-1, keepdims=True) * (1.0 / chans)
        var = jnp.sum(center * center, axis=-1, keepdims=True) * (1.0 / chans)
        rstd = lax.rsqrt(var + 1e-06)
        nhat = center * rstd
        nhat_ref[at, :] = nhat
        rstd_ref[at, :] = jnp.broadcast_to(rstd, (cols, LANES))
        normed[at, :] = (nhat * gain[0:1, :] + shift[0:1, :]).astype(BF16)
        return 0

    lax.fori_loop(0, rows, norm, 0, unroll=4)
    normed_t[...] = normed[...].T
    go_t[...] = go[...].T

    for k in range(hidden // chunk):
        at = slice(k * chunk, (k + 1) * chunk)
        z = nn(normed[...], we[:, at]) + be[0:1, at]
        cdf = 0.5 * (1.0 + lax.erf(z * 0.7071067811865476))
        hid[:, at] = (z * cdf).astype(BF16)
        slope = cdf + z * jnp.exp(-0.5 * z * z) * 0.3989422804014327
        dz[:, at] = (nt(go[...], wr[at, :]) * slope).astype(BF16)
    dn[...] = nt(dz[...], we[...])
    acc_ref[0:chans, :] += nn(normed_t[...], dz[...])
    acc_ref[chans : 2 * chans, :] += nn(go_t[...], hid[...])

    def back(i, _):
        at = pl.ds(pl.multiple_of(i * cols, cols), cols)
        nhat = nhat_ref[at, :]
        d = dn[at, :] * gain[0:1, :]
        first = jnp.sum(d, axis=-1, keepdims=True) * (1.0 / chans)
        second = jnp.sum(d * nhat, axis=-1, keepdims=True) * (1.0 / chans)
        rstd = rstd_ref[at, :]
        g = jnp.concatenate([rstd, rstd], axis=1) * (d - first - nhat * second)
        g_ref[i] = g.astype(BF16)
        return 0

    lax.fori_loop(0, rows, back, 0, unroll=4)


def branch(x, halo, cot, tissue, w, bias, gain, shift, we, be, wr, scale):
    rows, cols, chans = x.shape
    hidden = we.shape[1]
    pix = TILE * cols
    block = pl.BlockSpec((TILE, cols, chans), lambda s, t: (s, 0, 0))
    grid = pltpu.PrefetchScalarGridSpec(
        num_scalar_prefetch=1,
        grid=(rows // TILE,),
        in_specs=[VMEM] * 5 + [block] + [VMEM] * 8,
        out_specs=[block, pl.BlockSpec((2 * chans, hidden), lambda s, t: (0, 0))],
        scratch_shapes=[
            pltpu.VMEM((2, rows + 6, cols + 16, LANES), F32),
            pltpu.VMEM((2, 49, 8, LANES), F32),
            pltpu.VMEM((pix, chans), F32),
            pltpu.VMEM((pix, chans), F32),
            pltpu.VMEM((pix, LANES), F32),
            pltpu.VMEM((pix, chans), BF16),
            pltpu.VMEM((chans, pix), BF16),
            pltpu.VMEM((pix, chans), BF16),
            pltpu.VMEM((chans, pix), BF16),
            pltpu.VMEM((pix, hidden), BF16),
            pltpu.VMEM((pix, hidden), BF16),
            pltpu.VMEM((pix, chans), F32),
        ],
    )
    return pl.pallas_call(
        branch_kernel,
        grid_spec=grid,
        out_shape=(
            jax.ShapeDtypeStruct(x.shape, BF16),
            jax.ShapeDtypeStruct((2 * chans, hidden), F32),
        ),
        compiler_params=pltpu.CompilerParams(**PARAMS),
        cost_estimate=cost(32),
        name="branch",
    )(tissue, x, *halo, cot, w, bias, gain, shift, we, be, wr, scale)


def lane_half(shape, h):
    return pl.BlockSpec(shape[:-1] + (LANES,), lambda i, h=h: (0,) * (len(shape) - 1) + (h,))


def cost(us):
    return pl.CostEstimate(flops=0, transcendentals=0, bytes_accessed=int(us * 3.69e6))


def filter_kernel(x_ref, top, bottom, left, right, g_ref, o_ref, pad, gpad):
    rows, cols, _ = g_ref.shape
    fill(pad, x_ref, top, bottom, left, right, (0,))
    o_ref[...] = jnp.zeros_like(o_ref)
    for i in range(3):
        gpad[i] = jnp.zeros((cols, LANES), F32)
        gpad[rows + 3 + i] = jnp.zeros((cols, LANES), F32)

    def put(i, _):
        gpad[3 + i] = g_ref[i].astype(F32)
        return 0

    lax.fori_loop(0, rows, put, 0, unroll=4)
    for first, count in ((0, 4), (4, 3)):

        def step(n, accs):
            r = first + n // 2
            base = (n % 2) * (cols // 2)
            for c in range(cols // 16):
                xs = [pad[0, r, pl.ds(base + c * 8 + 5 + b, 8), :] for b in range(7)]
                out = []
                for k in range(count):
                    at = pl.ds(pl.multiple_of(base + c * 8, 8), 8)
                    g = gpad[r - (first + k) + 3, at, :]
                    out += [accs[k * 7 + b] + xs[b] * g for b in range(7)]
                accs = tuple(out)
            return accs

        zero = jnp.zeros((8, LANES), F32)
        accs = lax.fori_loop(0, (rows + count - 1) * 2, step, (zero,) * (7 * count), unroll=8)
        for k in range(count):
            for b in range(7):
                t = (first + k) * 7 + b
                o_ref[t : t + 1, :] = jnp.sum(accs[k * 7 + b], axis=0, keepdims=True)


def filter_grad(x, halo, g, h):
    rows, cols, _ = x.shape
    arrays = (x, *halo, g)
    return pl.pallas_call(
        filter_kernel,
        grid=(1,),
        out_shape=jax.ShapeDtypeStruct((TAPS, LANES), F32),
        in_specs=[lane_half(a.shape, h) for a in arrays],
        out_specs=pl.BlockSpec((TAPS, LANES), lambda i: (0, 0)),
        scratch_shapes=[
            pltpu.VMEM((1, rows + 6, cols + 16, LANES), F32),
            pltpu.VMEM((rows + 6, cols, LANES), F32),
        ],
        compiler_params=pltpu.CompilerParams(**PARAMS),
        cost_estimate=cost(7),
        name="filter_grad",
    )(*arrays)


def input_kernel(g_ref, top, bottom, left, right, cot, w_ref, o_ref, pad, wide, out):
    rows, cols, _ = g_ref.shape
    spread_weights(w_ref, wide, True, (0,))
    fill(pad, g_ref, top, bottom, left, right, (0,))
    ng = cols // (8 * CB)

    def step(n, _):
        row, col = (n // ng) * RG, (n % ng) * (8 * CB)
        acc = stencil(pad, wide, 0, row, col)
        for i in range(RG):
            for c in range(CB):
                at = pl.ds(pl.multiple_of(col + c * 8, 8), 8)
                out[row + i, at, :] = acc[i][c]
        return 0

    lax.fori_loop(0, (rows // RG) * ng, step, 0)

    def last(i, _):
        o_ref[i] = (cot[i].astype(F32) + out[i]).astype(BF16)
        return 0

    lax.fori_loop(0, rows, last, 0, unroll=4)


def input_grad(g, halo, cot, w, h):
    rows, cols, _ = g.shape
    arrays = (g, *halo, cot, w)
    return pl.pallas_call(
        input_kernel,
        grid=(1,),
        out_shape=jax.ShapeDtypeStruct((rows, cols, LANES), BF16),
        in_specs=[lane_half(a.shape, h) for a in arrays],
        out_specs=pl.BlockSpec((rows, cols, LANES), lambda i: (0, 0, 0)),
        scratch_shapes=[
            pltpu.VMEM((1, rows + 6, cols + 16, LANES), F32),
            pltpu.VMEM((1, 49, 8, LANES), F32),
            pltpu.VMEM((rows, cols, LANES), F32),
        ],
        compiler_params=pltpu.CompilerParams(**PARAMS),
        cost_estimate=cost(7),
        name="input_grad",
    )(*arrays)


def shifts(count):
    forward = [(i, i + 1) for i in range(count - 1)]
    return forward, [(b, a) for a, b in forward]


def halo_of(block, sizes):
    rows, cols = block.shape[:2]
    forward, backward = shifts(sizes[0])
    top = lax.ppermute(block[rows - 3 :], TY, forward)
    bottom = lax.ppermute(block[:3], TY, backward)

    def edge(at):
        parts = [p[:, at : at + 3].transpose(1, 0, 2) for p in (top, block, bottom)]
        return jnp.concatenate(parts, axis=1)

    forward, backward = shifts(sizes[1])
    left = lax.ppermute(edge(cols - 3), TX, forward)
    right = lax.ppermute(edge(0), TX, backward)
    return top, bottom, left, right


AXES = ("y", "x_hi", "core", "z", "x_lo")
SIZES = (4, 2, 2, 8, 2)
TY, TX = AXES[:3], AXES[3:]
PAIRS = ("core", "x_lo", "x_hi")
REST = ("y", "z")


def swap(value, axis):
    at = AXES.index(axis)
    index = np.arange(math.prod(SIZES)).reshape(SIZES)
    other = np.flip(index, axis=at)
    pairs = [(int(a), int(b)) for a, b in zip(index.ravel(), other.ravel())]
    return lax.ppermute(value, AXES, pairs)


def scatter(value):
    for axis in PAIRS:
        upper = lax.axis_index(axis) == 1
        width = value.shape[1] // 2
        low, high = value[:, :width], value[:, width:]
        got = swap(jnp.where(upper, low, high).astype(BF16), axis)
        value = jnp.where(upper, high, low) + got.astype(F32)
    return value


def exchange(value, taps):
    count = math.prod(SIZES[AXES.index(a)] for a in REST)
    blocks = [value.reshape(count, -1, LANES), taps.reshape(count, -1, LANES)]
    rows = blocks[0].shape[1]
    split = jnp.concatenate([b.astype(BF16) for b in blocks], axis=1)
    split = lax.all_to_all(split, REST, 0, 0, tiled=True)
    mine = jnp.sum(split.astype(F32), axis=0).astype(BF16)
    out = lax.all_to_all(jnp.broadcast_to(mine, split.shape), REST, 0, 0, tiled=True)
    return out[:, :rows].reshape(value.shape), out[:, rows:].reshape(taps.shape).astype(F32)


def gather(out, taps):
    shape = taps.shape
    for axis in reversed(PAIRS):
        upper = lax.axis_index(axis) == 1
        rows, width = out.shape
        sent = jnp.concatenate([out, taps.astype(BF16).reshape(-1, width)])
        got = swap(sent, axis)
        other = got[:rows]
        taps = taps + got[rows:].astype(F32).reshape(shape)
        out = jnp.concatenate([jnp.where(upper, other, out), jnp.where(upper, out, other)], axis=1)
    return out, taps


def body(x, cot, tissue, w, bias, gain, shift, we, be, wr, scale):
    rows, cols, chans = x.shape
    line = lambda v: v.reshape(1, -1)
    sizes = (math.prod(SIZES[:3]), math.prod(SIZES[3:]))
    factor = 1.0 / math.sqrt(rows * sizes[0] * cols * sizes[1])
    halo = halo_of(x, sizes)
    g, sums = branch(
        x, halo, cot, tissue, w, line(bias), line(gain), line(shift), we, line(be), wr, line(scale)
    )
    part = scatter(sums)
    taps = []
    for h in range(2):
        taps.append(filter_grad(x, halo, g, h))
    ghalo = halo_of(g, sizes)
    out, taps = exchange(part, jnp.concatenate(taps))
    result = []
    for h in range(2):
        result.append(input_grad(g, ghalo, cot, w, h))
    out, taps = gather(out, taps)
    out = out.astype(F32) * factor
    taps = (jnp.concatenate([taps[:TAPS], taps[TAPS:]], axis=1) * factor)[: w.shape[0]]
    return jnp.concatenate(result, axis=2), taps, out[:chans], out[chans:].T


def solution(mesh):
    fine = Mesh(mesh.devices.reshape(SIZES), AXES)
    pixels = P(TY, TX, None)
    return jax.shard_map(
        body,
        mesh=fine,
        in_specs=(pixels, pixels, P(TY, TX)) + (P(),) * 8,
        out_specs=(pixels, P(), P(), P()),
        check_vma=False,
    )
```

time: 205 us -> 186 us (0.907)
  Pallas kernels: 89.3 us -> 70.3 us
  waiting for transfers between devices: 45.5 us -> 39.3 us
  other arithmetic: 3.85 us -> 9.33 us
    pallas_call x1, Pallas kernels: 48.8 us -> 31.7 us  [branch(): pl.pallas_call(branch_kernel, grid_spec=grid, out_shape=(jax.ShapeDtypeSt...]
    ppermute x6, waiting for transfers between devices: 23.7 us -> 17.4 us  [swap(): return lax.ppermute(value, AXES, pairs)]
    concatenate x6, other arithmetic: 0.15 us -> 2.56 us  [the longest x1 2.45 us: body(): return (jnp.concatenate(result, axis=2), taps, out[:chans], out[chans:].T)]
    pallas_call x2 -> x4, Pallas kernels: 40.5 us -> 38.6 us  [the longest x2 21.5 us: input_grad(): pl.pallas_call(input_kernel, grid=(1,), out_shape=jax.ShapeDtypeStruct((r...]
  transfers between devices with their start and end apart: 15 -> 15, of which waited for: 10 -> 8; matrix products, arithmetic and copies ran while one was open for 2% -> 5% of each run, Pallas kernels for 10% -> 21%
where the time goes in v2:
time: 186 us; the launch traced here: 184 us
  Pallas kernels  70.3 us (38%)
  waiting for transfers between devices  39.3 us (21%)
  starting transfers between devices  31.7 us (17%)
  blocking collectives  21.8 us (12%)
  local copies, waits for them, and re-layouts  10.6 us (6%)
  other arithmetic  9.33 us (5%)
    pallas_call x1, Pallas kernels, branch(): pl.pallas_call(branch_kernel, grid_spec=grid, out_shape=(jax.ShapeDtypeSt...  31.7 us
    all_to_all x1, blocking collectives, exchange(): split = lax.all_to_all(split, REST, 0, 0, tiled=True)  21.8 us
    pallas_call x2, Pallas kernels, input_grad(): pl.pallas_call(input_kernel, grid=(1,), out_shape=jax.ShapeDtypeStruct((r...  21.5 us
    ppermute x6, waiting for transfers between devices, swap(): return lax.ppermute(value, AXES, pairs)  17.4 us
    pallas_call x2, Pallas kernels, filter_grad(): pl.pallas_call(filter_kernel, grid=(1,), out_shape=jax.ShapeDtypeStruct((...  17.1 us
    all_to_all x1, waiting for transfers between devices, exchange(): lax.all_to_all(jnp.broadcast_to(mine, split.shape), REST, 0, 0, tiled=True)  10.2 us
    ppermute x6, starting transfers between devices, swap(): return lax.ppermute(value, AXES, pairs)  9.28 us
    ppermute x2, waiting for transfers between devices, halo_of(): right = lax.ppermute(edge(0), TX, backward)  9.08 us
  transfers between devices with their start and end apart: 15, of which 8 were waited for; matrix products, arithmetic and copies ran while one was open for 5% of the time, Pallas kernels for 21%

profile of v2, /device:TPU:2, one launch (start us, length us, event | category | flops | bytes accessed | tf_op | source)
XLA Modules:
  0.0 184.1 jit_solution(15646993818659082215)
XLA Ops:
  1.6 1.7 collective-permute-start
  3.4 1.3 collective-permute-start.1
  6.0 2.6 %collective-permute-done.1 = bf16[3,48,256]{2,0,1:T(4,128)(2,1)S(1)} collective-permute-done((bf16[3,48,256]{2,0,1:T(4,128)(2,1)S(1)}, bf16[3,48,256]{2,0,1:T(4,128)(2,1)S(1)}, u32[]{:S(2)}, u32[]{:S(2)}) %collective-permute-start.1) | collective-permute-done | bytes 73760 | tf_op jit(solution)/shard_map/ppermute | solution.py:317
  8.6 4.7 %collective-permute-start.2 = (bf16[3,70,256]{2,1,0:T(8,128)(2,1)S(1)}, bf16[3,70,256]{2,1,0:T(8,128)(2,1)S(1)}, u32[]{:S(2)}, u32[]{:S(2)}) collective-permute-start(bf16[3,70,256]{2,1,0:T(8,128)(2,1)S(1)} %pad_maximum_fusion.7), channel_id=1, source_target_pairs={{0,1},{1,2},{2,3},{3,4},{4,5},{5,6},{6,7},{7,8},{8,9},{9,10},{10,1... | collective-permute-start | bytes 322568 | tf_op jit(solution)/shard_map/ppermute | solution.py:324
  13.3 1.9 %collective-permute-start.3 = (bf16[3,70,256]{2,1,0:T(8,128)(2,1)S(1)}, bf16[3,70,256]{2,1,0:T(8,128)(2,1)S(1)}, u32[]{:S(2)}, u32[]{:S(2)}) collective-permute-start(bf16[3,70,256]{2,1,0:T(8,128)(2,1)S(1)} %pad_maximum_fusion.8), channel_id=1, source_target_pairs={{1,0},{2,1},{3,2},{4,3},{5,4},{6,5},{7,6},{8,7},{9,8},{10,9},{11,1... | collective-permute-start | bytes 322568 | tf_op jit(solution)/shard_map/ppermute | solution.py:325
  16.5 4.3 %collective-permute-done.3.right = bf16[3,70,256]{2,1,0:T(8,128)(2,1)S(1)} collective-permute-done((bf16[3,70,256]{2,1,0:T(8,128)(2,1)S(1)}, bf16[3,70,256]{2,1,0:T(8,128)(2,1)S(1)}, u32[]{:S(2)}, u32[]{:S(2)}) %collective-permute-start.3) | collective-permute-done | bytes 107552 | tf_op jit(solution)/shard_map/ppermute | solution.py:325
  21.5 31.7 %branch.1 = (bf16[64,48,256]{2,1,0:T(8,128)(2,1)}, f32[512,1024]{1,0:T(8,128)}) custom-call(s32[4,3]{1,0:T(4,128)} %tissue.1, bf16[64,48,256]{2,1,0:T(8,128)(2,1)} %x_ref.5, bf16[3,48,256]{2,1,0:T(8,128)(2,1)} %copy.19.top, bf16[3,48,256]{2,1,0:T(8,128)(2,1)} %copy.20.bottom, bf16[3,70,256]{2,1,0:T(8,128)(2,1)} %copy-done.2, bf16[3,70,256]{2,1,0:T(8,128)(2,1)} %copy-done.3, ...), custom_call_target="tpu_custom_call" | custom-call | bytes 118080000 | tf_op jit(solution)/shard_map/branch/pallas_call | solution.py:188
  53.2 1.6 select_convert_fusion
  54.9 3.4 %collective-permute-start.8 = (bf16[512,512]{1,0:T(8,128)(2,1)S(1)}, bf16[512,512]{1,0:T(8,128)(2,1)S(1)}, u32[]{:S(2)}, u32[]{:S(2)}) collective-permute-start(bf16[512,512]{1,0:T(8,128)(2,1)S(1)} %select_convert_fusion), channel_id=1, source_target_pairs={{0,16},{1,17},{2,18},{3,19},{4,20},{5,21},{6,22},{7,23},{8,24},{9,... | collective-permute-start | bytes 1572872 | tf_op jit(solution)/shard_map/ppermute | solution.py:341
  58.3 1.5 collective-permute-done.8
  59.8 1.8 convert_add_fusion
  61.8 8.6 %collective-permute-done.9 = bf16[512,256]{1,0:T(8,128)(2,1)S(1)} collective-permute-done((bf16[512,256]{1,0:T(8,128)(2,1)S(1)}, bf16[512,256]{1,0:T(8,128)(2,1)S(1)}, u32[]{:S(2)}, u32[]{:S(2)}) %collective-permute-start.9) | collective-permute-done | bytes 262176 | tf_op jit(solution)/shard_map/ppermute | solution.py:341
  70.5 1.9 %collective-permute-start.10 = (bf16[512,128]{1,0:T(8,128)(2,1)S(1)}, bf16[512,128]{1,0:T(8,128)(2,1)S(1)}, u32[]{:S(2)}, u32[]{:S(2)}) collective-permute-start(bf16[512,128]{1,0:T(8,128)(2,1)S(1)} %select_convert_fusion.2), channel_id=1, source_target_pairs={{0,32},{1,33},{2,34},{3,35},{4,36},{5,37},{6,38},{7,39},{8,40},{9,... | collective-permute-start | bytes 393224 | tf_op jit(solution)/shard_map/ppermute | solution.py:341
  72.4 8.5 %filter_grad.3 = f32[64,128]{1,0:T(8,128)} custom-call(bf16[64,48,256]{2,1,0:T(8,128)(2,1)} %x_ref.5, bf16[3,48,256]{2,1,0:T(8,128)(2,1)} %copy.19.top, bf16[3,48,256]{2,1,0:T(8,128)(2,1)} %copy.20.bottom, bf16[3,70,256]{2,1,0:T(8,128)(2,1)} %copy-done.2, bf16[3,70,256]{2,1,0:T(8,128)(2,1)} %copy-done.3, bf16[64,48,256]{2,1,0:T(8,128)(2,1)} %get-tuple-element.6.g_ref), custom_call_target="tpu_custom_call" | custom-call | bytes 25830000 | tf_op jit(solution)/shard_map/filter_grad/pallas_call | solution.py:248
  81.7 8.5 %filter_grad.2 = f32[64,128]{1,0:T(8,128)} custom-call(bf16[64,48,256]{2,1,0:T(8,128)(2,1)} %x_ref.5, bf16[3,48,256]{2,1,0:T(8,128)(2,1)} %copy.19.top, bf16[3,48,256]{2,1,0:T(8,128)(2,1)} %copy.20.bottom, bf16[3,70,256]{2,1,0:T(8,128)(2,1)} %copy-done.2, bf16[3,70,256]{2,1,0:T(8,128)(2,1)} %copy-done.3, bf16[64,48,256]{2,1,0:T(8,128)(2,1)} %get-tuple-element.6.g_ref), custom_call_target="tpu_custom_call" | custom-call | bytes 25830000 | tf_op jit(solution)/shard_map/filter_grad/pallas_call | solution.py:248
  91.2 21.8 %all_to_all.10 = bf16[32,20,128]{2,1,0:T(8,128)(2,1)S(1)} all-to-all(bf16[32,20,128]{2,1,0:T(8,128)(2,1)S(1)} %pad_maximum_fusion.5), channel_id=1, replica_groups=mesh['y'=4,'x_hi'=2,'core'=2,'z'=8,'x_lo'=2] {'y','z'}, dimensions={0} | all-to-all | bytes 327680 | tf_op jit(solution)/shard_map/all_to_all | solution.py:359
  113.7 4.0 %all-to-all-start.1 = ((bf16[32,20,128]{2,1,0:T(8,128)(2,1)}), bf16[32,20,128]{2,1,0:T(8,128)(2,1)S(1)}, u32[]{:S(2)}, u32[]{:S(2)}) async-start(bf16[32,20,128]{2,1,0:T(8,128)(2,1)} %broadcast_in_dim.3), calls=%async_computation.1 | async-start | bytes 393216 | tf_op jit(solution)/shard_map/all_to_all | solution.py:361
  118.3 10.2 %all-to-all-done.1 = bf16[32,20,128]{2,1,0:T(8,128)(2,1)S(1)} async-done(((bf16[32,20,128]{2,1,0:T(8,128)(2,1)}), bf16[32,20,128]{2,1,0:T(8,128)(2,1)S(1)}, u32[]{:S(2)}, u32[]{:S(2)}) %all-to-all-start.1) | async-done | bytes 163872 | tf_op jit(solution)/shard_map/all_to_all | solution.py:361
  128.6 2.2 %collective-permute-start.11 = (bf16[640,128]{1,0:T(8,128)(2,1)S(1)}, bf16[640,128]{1,0:T(8,128)(2,1)S(1)}, u32[]{:S(2)}, u32[]{:S(2)}) collective-permute-start(bf16[640,128]{1,0:T(8,128)(2,1)S(1)} %pad_maximum_fusion.6), channel_id=1, source_target_pairs={{0,32},{1,33},{2,34},{3,35},{4,36},{5,37},{6,38},{7,39},{8,40},{9,... | collective-permute-start | bytes 491528 | tf_op jit(solution)/shard_map/ppermute | solution.py:341
  131.4 1.3 collective-permute-start.5
  132.7 2.7 %collective-permute-done.11 = bf16[640,128]{1,0:T(8,128)(2,1)S(1)} collective-permute-done((bf16[640,128]{1,0:T(8,128)(2,1)S(1)}, bf16[640,128]{1,0:T(8,128)(2,1)S(1)}, u32[]{:S(2)}, u32[]{:S(2)}) %collective-permute-start.11) | collective-permute-done | bytes 163872 | tf_op jit(solution)/shard_map/ppermute | solution.py:341
  135.6 1.5 collective-permute-start.12
  137.1 1.3 collective-permute-start.4
  138.4 4.6 %collective-permute-done.12 = bf16[576,256]{1,0:T(8,128)(2,1)S(1)} collective-permute-done((bf16[576,256]{1,0:T(8,128)(2,1)S(1)}, bf16[576,256]{1,0:T(8,128)(2,1)S(1)}, u32[]{:S(2)}, u32[]{:S(2)}) %collective-permute-start.12) | collective-permute-done | bytes 294944 | tf_op jit(solution)/shard_map/ppermute | solution.py:341
  143.6 4.2 %collective-permute-start.6 = (bf16[3,70,256]{2,1,0:T(8,128)(2,1)S(1)}, bf16[3,70,256]{2,1,0:T(8,128)(2,1)S(1)}, u32[]{:S(2)}, u32[]{:S(2)}) collective-permute-start(bf16[3,70,256]{2,1,0:T(8,128)(2,1)S(1)} %pad_maximum_fusion.9), channel_id=1, source_target_pairs={{0,1},{1,2},{2,3},{3,4},{4,5},{5,6},{6,7},{7,8},{8,9},{9,10},{10,1... | collective-permute-start | bytes 322568 | tf_op jit(solution)/shard_map/ppermute | solution.py:324
  147.9 1.9 %collective-permute-start.7 = (bf16[3,70,256]{2,1,0:T(8,128)(2,1)S(1)}, bf16[3,70,256]{2,1,0:T(8,128)(2,1)S(1)}, u32[]{:S(2)}, u32[]{:S(2)}) collective-permute-start(bf16[3,70,256]{2,1,0:T(8,128)(2,1)S(1)} %pad_maximum_fusion.10), channel_id=1, source_target_pairs={{1,0},{2,1},{3,2},{4,3},{5,4},{6,5},{7,6},{8,7},{9,8},{10,9},{11,1... | collective-permute-start | bytes 322568 | tf_op jit(solution)/shard_map/ppermute | solution.py:325
  151.1 4.7 %collective-permute-done.7.right = bf16[3,70,256]{2,1,0:T(8,128)(2,1)S(1)} collective-permute-done((bf16[3,70,256]{2,1,0:T(8,128)(2,1)S(1)}, bf16[3,70,256]{2,1,0:T(8,128)(2,1)S(1)}, u32[]{:S(2)}, u32[]{:S(2)}) %collective-permute-start.7) | collective-permute-done | bytes 107552 | tf_op jit(solution)/shard_map/ppermute | solution.py:325
  156.5 10.7 %input_grad.3 = bf16[64,48,128]{2,1,0:T(8,128)(2,1)} custom-call(bf16[64,48,256]{2,1,0:T(8,128)(2,1)} %get-tuple-element.6.g_ref, bf16[3,48,256]{2,1,0:T(8,128)(2,1)} %copy.25.top, bf16[3,48,256]{2,1,0:T(8,128)(2,1)} %copy.26.bottom, bf16[3,70,256]{2,1,0:T(8,128)(2,1)} %copy-done.4, bf16[3,70,256]{2,1,0:T(8,128)(2,1)} %copy-done.5, ...), custom_call_target="tpu_custom_call" | custom-call | bytes 25830000 | tf_op jit(solution)/shard_map/input_grad/pallas_call | solution.py:291
  167.2 10.8 %input_grad.2 = bf16[64,48,128]{2,1,0:T(8,128)(2,1)} custom-call(bf16[64,48,256]{2,1,0:T(8,128)(2,1)} %get-tuple-element.6.g_ref, bf16[3,48,256]{2,1,0:T(8,128)(2,1)} %copy.25.top, bf16[3,48,256]{2,1,0:T(8,128)(2,1)} %copy.26.bottom, bf16[3,70,256]{2,1,0:T(8,128)(2,1)} %copy-done.4, bf16[3,70,256]{2,1,0:T(8,128)(2,1)} %copy-done.5, ...), custom_call_target="tpu_custom_call" | custom-call | bytes 25830000 | tf_op jit(solution)/shard_map/input_grad/pallas_call | solution.py:291
  178.0 2.4 %pad_maximum_fusion = bf16[64,48,256]{2,1,0:T(8,128)(2,1)} fusion(bf16[64,48,128]{2,1,0:T(8,128)(2,1)S(1)} %copy-done.1, bf16[64,48,128]{2,1,0:T(8,128)(2,1)} %input_grad.2), kind=kLoop, calls=%fused_computation.1 | loop fusion | flops 3145728 | bytes 3145728 | tf_op jit(solution)/shard_map/concatenate | solution.py:399
  181.0 1.2 slice_bitcast_fusion
  182.1 1.3 copy.33
  (72 shorter events, 12.0 us)
Async XLA Ops:
  1.6 4.3 %collective-permute-start = (bf16[3,48,256]{2,0,1:T(4,128)(2,1)S(1)}, bf16[3,48,256]{2,0,1:T(4,128)(2,1)S(1)}, u32[]{:S(2)}, u32[]{:S(2)}) collective-permute-start(bf16[3,48,256]{2,0,1:T(4,128)(2,1)S(1)} %copy.34), channel_id=1, source_target_pairs={{0,16},{16,32},{32,48},{48,64},{64,80},{80,96},{96,112},{112,128},... | collective-permute-start | bytes 221192 | tf_op jit(solution)/shard_map/ppermute | solution.py:316
  3.4 5.1 %collective-permute-start.1 = (bf16[3,48,256]{2,0,1:T(4,128)(2,1)S(1)}, bf16[3,48,256]{2,0,1:T(4,128)(2,1)S(1)}, u32[]{:S(2)}, u32[]{:S(2)}) collective-permute-start(bf16[3,48,256]{2,0,1:T(4,128)(2,1)S(1)} %copy.35), channel_id=1, source_target_pairs={{16,0},{32,16},{48,32},{64,48},{80,64},{96,80},{112,96},{128,112},... | collective-permute-start | bytes 221192 | tf_op jit(solution)/shard_map/ppermute | solution.py:317
  8.6 8.0 %collective-permute-start.2 = (bf16[3,70,256]{2,1,0:T(8,128)(2,1)S(1)}, bf16[3,70,256]{2,1,0:T(8,128)(2,1)S(1)}, u32[]{:S(2)}, u32[]{:S(2)}) collective-permute-start(bf16[3,70,256]{2,1,0:T(8,128)(2,1)S(1)} %pad_maximum_fusion.7), channel_id=1, source_target_pairs={{0,1},{1,2},{2,3},{3,4},{4,5},{5,6},{6,7},{7,8},{8,9},{9,10},{10,1... | collective-permute-start | bytes 322568 | tf_op jit(solution)/shard_map/ppermute | solution.py:324
  13.3 7.5 %collective-permute-start.3 = (bf16[3,70,256]{2,1,0:T(8,128)(2,1)S(1)}, bf16[3,70,256]{2,1,0:T(8,128)(2,1)S(1)}, u32[]{:S(2)}, u32[]{:S(2)}) collective-permute-start(bf16[3,70,256]{2,1,0:T(8,128)(2,1)S(1)} %pad_maximum_fusion.8), channel_id=1, source_target_pairs={{1,0},{2,1},{3,2},{4,3},{5,4},{6,5},{7,6},{8,7},{9,8},{10,9},{11,1... | collective-permute-start | bytes 322568 | tf_op jit(solution)/shard_map/ppermute | solution.py:325
  16.5 4.3 %copy-start.2 = (bf16[3,70,256]{2,1,0:T(8,128)(2,1)}, bf16[3,70,256]{2,1,0:T(8,128)(2,1)S(1)}, u32[]{:S(2)}) copy-start(bf16[3,70,256]{2,1,0:T(8,128)(2,1)S(1)} %collective-permute-done.2.left) | copy-start | bytes 322564
  20.9 0.6 copy-start.3
  54.9 4.9 %collective-permute-start.8 = (bf16[512,512]{1,0:T(8,128)(2,1)S(1)}, bf16[512,512]{1,0:T(8,128)(2,1)S(1)}, u32[]{:S(2)}, u32[]{:S(2)}) collective-permute-start(bf16[512,512]{1,0:T(8,128)(2,1)S(1)} %select_convert_fusion), channel_id=1, source_target_pairs={{0,16},{1,17},{2,18},{3,19},{4,20},{5,21},{6,22},{7,23},{8,24},{9,... | collective-permute-start | bytes 1572872 | tf_op jit(solution)/shard_map/ppermute | solution.py:341
  61.7 8.7 %collective-permute-start.9 = (bf16[512,256]{1,0:T(8,128)(2,1)S(1)}, bf16[512,256]{1,0:T(8,128)(2,1)S(1)}, u32[]{:S(2)}, u32[]{:S(2)}) collective-permute-start(bf16[512,256]{1,0:T(8,128)(2,1)S(1)} %select_convert_fusion.1), channel_id=1, source_target_pairs={{0,1},{1,0},{2,3},{3,2},{4,5},{5,4},{6,7},{7,6},{8,9},{9,8},{10,11... | collective-permute-start | bytes 786440 | tf_op jit(solution)/shard_map/ppermute | solution.py:341
  70.5 20.6 %collective-permute-start.10 = (bf16[512,128]{1,0:T(8,128)(2,1)S(1)}, bf16[512,128]{1,0:T(8,128)(2,1)S(1)}, u32[]{:S(2)}, u32[]{:S(2)}) collective-permute-start(bf16[512,128]{1,0:T(8,128)(2,1)S(1)} %select_convert_fusion.2), channel_id=1, source_target_pairs={{0,32},{1,33},{2,34},{3,35},{4,36},{5,37},{6,38},{7,39},{8,40},{9,... | collective-permute-start | bytes 393224 | tf_op jit(solution)/shard_map/ppermute | solution.py:341
  90.2 27.5 %copy-start = (bf16[64,48,256]{2,1,0:T(8,128)(2,1)S(1)}, bf16[64,48,256]{2,1,0:T(8,128)(2,1)}, u32[]{:S(2)}) copy-start(bf16[64,48,256]{2,1,0:T(8,128)(2,1)} %get-tuple-element.6.g_ref) | copy-start | bytes 4718596
  113.7 14.8 %all-to-all-start.1 = ((bf16[32,20,128]{2,1,0:T(8,128)(2,1)}), bf16[32,20,128]{2,1,0:T(8,128)(2,1)S(1)}, u32[]{:S(2)}, u32[]{:S(2)}) async-start(bf16[32,20,128]{2,1,0:T(8,128)(2,1)} %broadcast_in_dim.3), calls=%async_computation.1 | async-start | bytes 393216 | tf_op jit(solution)/shard_map/all_to_all | solution.py:361
  128.6 6.9 %collective-permute-start.11 = (bf16[640,128]{1,0:T(8,128)(2,1)S(1)}, bf16[640,128]{1,0:T(8,128)(2,1)S(1)}, u32[]{:S(2)}, u32[]{:S(2)}) collective-permute-start(bf16[640,128]{1,0:T(8,128)(2,1)S(1)} %pad_maximum_fusion.6), channel_id=1, source_target_pairs={{0,32},{1,33},{2,34},{3,35},{4,36},{5,37},{6,38},{7,39},{8,40},{9,... | collective-permute-start | bytes 491528 | tf_op jit(solution)/shard_map/ppermute | solution.py:341
  131.4 6.9 %collective-permute-start.5 = (bf16[3,48,256]{2,0,1:T(4,128)(2,1)S(1)}, bf16[3,48,256]{2,0,1:T(4,128)(2,1)S(1)}, u32[]{:S(2)}, u32[]{:S(2)}) collective-permute-start(bf16[3,48,256]{2,0,1:T(4,128)(2,1)S(1)} %get-tuple-element.16), channel_id=1, source_target_pairs={{16,0},{32,16},{48,32},{64,48},{80,64},{96,80},{112,96},{128,112},... | collective-permute-start | bytes 221192 | tf_op jit(solution)/shard_map/ppermute | solution.py:317
  135.6 7.4 %collective-permute-start.12 = (bf16[576,256]{1,0:T(8,128)(2,1)S(1)}, bf16[576,256]{1,0:T(8,128)(2,1)S(1)}, u32[]{:S(2)}, u32[]{:S(2)}) collective-permute-start(bf16[576,256]{1,0:T(8,128)(2,1)S(1)} %pad_maximum_fusion.3), channel_id=1, source_target_pairs={{0,1},{1,0},{2,3},{3,2},{4,5},{5,4},{6,7},{7,6},{8,9},{9,8},{10,11... | collective-permute-start | bytes 884744 | tf_op jit(solution)/shard_map/ppermute | solution.py:341
  137.1 6.5 %collective-permute-start.4 = (bf16[3,48,256]{2,0,1:T(4,128)(2,1)}, bf16[3,48,256]{2,0,1:T(4,128)(2,1)S(1)}, u32[]{:S(2)}, u32[]{:S(2)}) collective-permute-start(bf16[3,48,256]{2,0,1:T(4,128)(2,1)} %get-tuple-element.17), channel_id=1, source_target_pairs={{0,16},{16,32},{32,48},{48,64},{64,80},{80,96},{96,112},{112,128},... | collective-permute-start | bytes 221192 | tf_op jit(solution)/shard_map/ppermute | solution.py:316
  143.2 37.2 %collective-permute-start.13 = (bf16[544,512]{1,0:T(8,128)(2,1)S(1)}, bf16[544,512]{1,0:T(8,128)(2,1)S(1)}, u32[]{:S(2)}, u32[]{:S(2)}) collective-permute-start(bf16[544,512]{1,0:T(8,128)(2,1)S(1)} %pad_maximum_fusion.1), channel_id=1, source_target_pairs={{0,16},{1,17},{2,18},{3,19},{4,20},{5,21},{6,22},{7,23},{8,24},{9,... | collective-permute-start | bytes 1671176 | tf_op jit(solution)/shard_map/ppermute | solution.py:341
  143.6 7.5 %collective-permute-start.6 = (bf16[3,70,256]{2,1,0:T(8,128)(2,1)S(1)}, bf16[3,70,256]{2,1,0:T(8,128)(2,1)S(1)}, u32[]{:S(2)}, u32[]{:S(2)}) collective-permute-start(bf16[3,70,256]{2,1,0:T(8,128)(2,1)S(1)} %pad_maximum_fusion.9), channel_id=1, source_target_pairs={{0,1},{1,2},{2,3},{3,4},{4,5},{5,6},{6,7},{7,8},{8,9},{9,10},{10,1... | collective-permute-start | bytes 322568 | tf_op jit(solution)/shard_map/ppermute | solution.py:324
  147.9 8.0 %collective-permute-start.7 = (bf16[3,70,256]{2,1,0:T(8,128)(2,1)S(1)}, bf16[3,70,256]{2,1,0:T(8,128)(2,1)S(1)}, u32[]{:S(2)}, u32[]{:S(2)}) collective-permute-start(bf16[3,70,256]{2,1,0:T(8,128)(2,1)S(1)} %pad_maximum_fusion.10), channel_id=1, source_target_pairs={{1,0},{2,1},{3,2},{4,3},{5,4},{6,5},{7,6},{8,7},{9,8},{10,9},{11,1... | collective-permute-start | bytes 322568 | tf_op jit(solution)/shard_map/ppermute | solution.py:325
  151.1 4.8 %copy-start.4 = (bf16[3,70,256]{2,1,0:T(8,128)(2,1)}, bf16[3,70,256]{2,1,0:T(8,128)(2,1)S(1)}, u32[]{:S(2)}) copy-start(bf16[3,70,256]{2,1,0:T(8,128)(2,1)S(1)} %collective-permute-done.6.left) | copy-start | bytes 322564
  155.8 0.6 copy-start.5
  167.2 10.8 %copy-start.1 = (bf16[64,48,128]{2,1,0:T(8,128)(2,1)S(1)}, bf16[64,48,128]{2,1,0:T(8,128)(2,1)}, u32[]{:S(2)}) copy-start(bf16[64,48,128]{2,1,0:T(8,128)(2,1)} %input_grad.3) | copy-start | bytes 2359300

commit v3 on v2

v3 whole, which is shorter than its diff:
```python
import math

import jax
import jax.numpy as jnp
import numpy as np
from jax import lax
from jax.experimental import pallas as pl
from jax.experimental.pallas import tpu as pltpu
from jax.sharding import Mesh, PartitionSpec as P


F32, BF16 = jnp.float32, jnp.bfloat16
TILE = 16
LANES = 128
RG = 8
CB = 3
TAPS = 64
SPAN = 80
VMEM = pl.BlockSpec(memory_space=pltpu.VMEM)
PARAMS = dict(vmem_limit_bytes=56 << 20)


def nn(a, b):
    return lax.dot_general(a, b, (((1,), (0,)), ((), ())), preferred_element_type=F32)


def nt(a, b):
    return lax.dot_general(a, b, (((1,), (1,)), ((), ())), preferred_element_type=F32)


def half(h):
    return slice(h * LANES, (h + 1) * LANES)


def spread_weights(w_ref, wide, flip, halves=(0, 1)):
    for k, h in enumerate(halves):
        for t in range(49):
            s = 48 - t if flip else t
            wide[k, t] = jnp.broadcast_to(w_ref[s : s + 1, half(h)], (8, LANES))


def fill(pad, core, top, bottom, left, right, halves=(0, 1)):
    rows, cols = core.shape[0], core.shape[1]
    span = left.shape[0] // 3
    for k, h in enumerate(halves):

        def put(i, _):
            pad[k, 3 + i, 8 : 8 + cols, :] = core[i, :, half(h)].astype(F32)
            return 0

        lax.fori_loop(0, rows, put, 0, unroll=4)
        for i in range(3):
            pad[k, i, 8 : 8 + cols, :] = top[i * cols : (i + 1) * cols, half(h)].astype(F32)
            pad[k, 3 + rows + i, 8 : 8 + cols, :] = bottom[
                i * cols : (i + 1) * cols, half(h)
            ].astype(F32)

        def side(first, count):
            for j in range(3):
                at = pl.ds(pl.multiple_of(j * span + first, 8), 8)
                lv = left[at, half(h)].astype(F32)
                rv = right[at, half(h)].astype(F32)
                for r in range(count):
                    pad[k, first + r, 5 + j : 6 + j, :] = lv[r : r + 1]
                    pad[k, first + r, 8 + cols + j : 9 + cols + j, :] = rv[r : r + 1]

        def eight(i, _):
            side(i * 8, 8)
            return 0

        lax.fori_loop(0, (rows + 6) // 8, eight, 0)
        side((rows + 6) // 8 * 8, (rows + 6) % 8)


def stencil(pad, wide, h, row, col):
    acc = [[None] * CB for _ in range(RG)]
    for b in range(7):
        w = [wide[h, a * 7 + b] for a in range(7)]
        for r in range(RG + 6):
            for c in range(CB):
                v = pad[h, row + r, pl.ds(col + c * 8 + 5 + b, 8), :]
                for a in range(7):
                    i = r - a
                    if 0 <= i < RG:
                        p = v * w[a]
                        acc[i][c] = p if acc[i][c] is None else acc[i][c] + p
    return acc


def filter_sums(pad, gpad, taps):
    rows, cols = gpad.shape[1] - 6, gpad.shape[2]
    for h in range(2):
        for first, count in ((0, 4), (4, 3)):

            def step(n, accs):
                r = first + n // 2
                base = (n % 2) * (cols // 2)
                for c in range(cols // 16):
                    xs = [pad[h, r, pl.ds(base + c * 8 + 5 + b, 8), :] for b in range(7)]
                    out = []
                    for k in range(count):
                        at = pl.ds(pl.multiple_of(base + c * 8, 8), 8)
                        g = gpad[h, r - (first + k) + 3, at, :]
                        out += [accs[k * 7 + b] + xs[b] * g for b in range(7)]
                    accs = tuple(out)
                return accs

            zero = jnp.zeros((8, LANES), F32)
            accs = lax.fori_loop(0, (rows + count - 1) * 2, step, (zero,) * (7 * count), unroll=8)
            for k in range(count):
                for b in range(7):
                    t = h * TAPS + (first + k) * 7 + b
                    taps[t : t + 1, :] = jnp.sum(accs[k * 7 + b], axis=0, keepdims=True)
        taps[h * TAPS + 49 : (h + 1) * TAPS, :] = jnp.zeros((TAPS - 49, LANES), F32)


def branch_kernel(
    tissue, upper, x_ref, top, bottom, left, right, cot, w_ref, bias, gain, shift, we, be, wr, scale,
    g_ref, kept, sent, taps, acc_ref, gpad, pad, wide, u_ref, nhat_ref, rstd_ref, normed, normed_t, go, go_t, hid, dz, dn,
):
    step = pl.program_id(0)
    rows, cols, chans = cot.shape
    hidden = we.shape[1]
    chunk = 256

    @pl.when(step == 0)
    def _():
        spread_weights(w_ref, wide, False)
        fill(pad, x_ref, top, bottom, left, right)
        acc_ref[...] = jnp.zeros_like(acc_ref)
        for h in range(2):
            for i in range(3):
                gpad[h, i] = jnp.zeros((cols, LANES), F32)
                gpad[h, x_ref.shape[0] + 3 + i] = jnp.zeros((cols, LANES), F32)

    ng = cols // (8 * CB)
    for h in range(2):

        def conv(n, _):
            row, col = (n // ng) * RG, (n % ng) * (8 * CB)
            acc = stencil(pad, wide, h, step * rows + row, col)
            for i in range(RG):
                for c in range(CB):
                    at = pl.multiple_of((row + i) * cols + col + c * 8, 8)
                    u_ref[pl.ds(at, 8), half(h)] = acc[i][c] + bias[0:1, half(h)]
            return 0

        lax.fori_loop(0, (rows // RG) * ng, conv, 0)

    tiles = cols // TILE
    for c in range(tiles):
        keep = tissue[step, c].astype(F32)
        part = cot[:, c * TILE : (c + 1) * TILE, :].astype(F32) * (scale[0:1, :] * keep)
        for i in range(rows):
            go[i * cols + c * TILE : i * cols + (c + 1) * TILE, :] = part[i].astype(BF16)

    def norm(i, _):
        at = pl.ds(pl.multiple_of(i * cols, cols), cols)
        u = u_ref[at, :]
        center = u - jnp.sum(u, axis=-1, keepdims=True) * (1.0 / chans)
        var = jnp.sum(center * center, axis=-1, keepdims=True) * (1.0 / chans)
        rstd = lax.rsqrt(var + 1e-06)
        nhat = center * rstd
        nhat_ref[at, :] = nhat
        rstd_ref[at, :] = jnp.broadcast_to(rstd, (cols, LANES))
        normed[at, :] = (nhat * gain[0:1, :] + shift[0:1, :]).astype(BF16)
        return 0

    lax.fori_loop(0, rows, norm, 0, unroll=4)
    normed_t[...] = normed[...].T
    go_t[...] = go[...].T

    for k in range(hidden // chunk):
        at = slice(k * chunk, (k + 1) * chunk)
        z = nn(normed[...], we[:, at]) + be[0:1, at]
        cdf = 0.5 * (1.0 + lax.erf(z * 0.7071067811865476))
        hid[:, at] = (z * cdf).astype(BF16)
        slope = cdf + z * jnp.exp(-0.5 * z * z) * 0.3989422804014327
        dz[:, at] = (nt(go[...], wr[at, :]) * slope).astype(BF16)
    dn[...] = nt(dz[...], we[...])
    acc_ref[0:chans, :] += nn(normed_t[...], dz[...])
    acc_ref[chans : 2 * chans, :] += nn(go_t[...], hid[...])

    def back(i, _):
        at = pl.ds(pl.multiple_of(i * cols, cols), cols)
        nhat = nhat_ref[at, :]
        d = dn[at, :] * gain[0:1, :]
        first = jnp.sum(d, axis=-1, keepdims=True) * (1.0 / chans)
        second = jnp.sum(d * nhat, axis=-1, keepdims=True) * (1.0 / chans)
        rstd = rstd_ref[at, :]
        g = (jnp.concatenate([rstd, rstd], axis=1) * (d - first - nhat * second)).astype(BF16)
        g_ref[i] = g
        for h in range(2):
            gpad[h, step * rows + i + 3] = g[:, half(h)].astype(F32)
        return 0

    lax.fori_loop(0, rows, back, 0, unroll=4)

    @pl.when(step == pl.num_programs(0) - 1)
    def _():
        filter_sums(pad, gpad, taps)
        blocks = hidden // LANES
        side = upper[0]
        for e in range(blocks):
            cut = half(e)
            other = acc_ref[chans : 2 * chans, cut].T
            piece = [acc_ref[0:chans, cut], other[:, :LANES], other[:, LANES:]]
            piece = jnp.concatenate(piece, axis=0)
            size = piece.shape[0]
            at = pl.ds((e % (blocks // 2)) * size, size)
            mine = side == e // (blocks // 2)

            @pl.when(mine)
            def _(piece=piece, at=at):
                kept[at, :] = piece

            @pl.when(jnp.logical_not(mine))
            def _(piece=piece, at=at):
                sent[at, :] = piece.astype(BF16)


def branch(x, halo, cot, tissue, upper, w, bias, gain, shift, we, be, wr, scale):
    rows, cols, chans = x.shape
    hidden = we.shape[1]
    pix = TILE * cols
    block = pl.BlockSpec((TILE, cols, chans), lambda s, t, u: (s, 0, 0))
    whole = lambda *shape: pl.BlockSpec(shape, lambda s, t, u: (0, 0))
    size = 2 * chans * hidden // LANES // 2
    grid = pltpu.PrefetchScalarGridSpec(
        num_scalar_prefetch=2,
        grid=(rows // TILE,),
        in_specs=[VMEM] * 5 + [block] + [VMEM] * 8,
        out_specs=[block, whole(size, LANES), whole(size, LANES), whole(2 * TAPS, LANES)],
        scratch_shapes=[
            pltpu.VMEM((2 * chans, hidden), F32),
            pltpu.VMEM((2, rows + 6, cols, LANES), F32),
            pltpu.VMEM((2, rows + 6, cols + 16, LANES), F32),
            pltpu.VMEM((2, 49, 8, LANES), F32),
            pltpu.VMEM((pix, chans), F32),
            pltpu.VMEM((pix, chans), F32),
            pltpu.VMEM((pix, LANES), F32),
            pltpu.VMEM((pix, chans), BF16),
            pltpu.VMEM((chans, pix), BF16),
            pltpu.VMEM((pix, chans), BF16),
            pltpu.VMEM((chans, pix), BF16),
            pltpu.VMEM((pix, hidden), BF16),
            pltpu.VMEM((pix, hidden), BF16),
            pltpu.VMEM((pix, chans), F32),
        ],
    )
    return pl.pallas_call(
        branch_kernel,
        grid_spec=grid,
        out_shape=(
            jax.ShapeDtypeStruct(x.shape, BF16),
            jax.ShapeDtypeStruct((size, LANES), F32),
            jax.ShapeDtypeStruct((size, LANES), BF16),
            jax.ShapeDtypeStruct((2 * TAPS, LANES), F32),
        ),
        compiler_params=pltpu.CompilerParams(**PARAMS),
        cost_estimate=cost(42),
        name="branch",
    )(tissue, upper, x, *halo, cot, w, bias, gain, shift, we, be, wr, scale)


def cost(us):
    return pl.CostEstimate(flops=0, transcendentals=0, bytes_accessed=int(us * 3.69e6))


def input_kernel(g_ref, top, bottom, left, right, cot, w_ref, o_ref, pad, wide, out):
    step = pl.program_id(0)
    rows, cols, _ = cot.shape

    @pl.when(step == 0)
    def _():
        spread_weights(w_ref, wide, True, (0,))
        fill(pad, g_ref, top, bottom, left, right, (0,))

    ng = cols // (8 * CB)

    def conv(n, _):
        row, col = (n // ng) * RG, (n % ng) * (8 * CB)
        acc = stencil(pad, wide, 0, step * rows + row, col)
        for i in range(RG):
            for c in range(CB):
                at = pl.ds(pl.multiple_of(col + c * 8, 8), 8)
                out[row + i, at, :] = acc[i][c]
        return 0

    lax.fori_loop(0, (rows // RG) * ng, conv, 0)

    def last(i, _):
        o_ref[i] = (cot[i].astype(F32) + out[i]).astype(BF16)
        return 0

    lax.fori_loop(0, rows, last, 0, unroll=4)


def input_grad(g, halo, cot, w, h):
    rows, cols, _ = g.shape
    flat = lambda a: pl.BlockSpec((a.shape[0], LANES), lambda s, h=h: (0, h))
    block = pl.BlockSpec((TILE, cols, LANES), lambda s, h=h: (s, 0, h))
    return pl.pallas_call(
        input_kernel,
        grid=(rows // TILE,),
        out_shape=jax.ShapeDtypeStruct((rows, cols, LANES), BF16),
        in_specs=[pl.BlockSpec((rows, cols, LANES), lambda s, h=h: (0, 0, h))]
        + [flat(a) for a in halo]
        + [block, flat(w)],
        out_specs=pl.BlockSpec((TILE, cols, LANES), lambda s: (s, 0, 0)),
        scratch_shapes=[
            pltpu.VMEM((1, rows + 6, cols + 16, LANES), F32),
            pltpu.VMEM((1, 49, 8, LANES), F32),
            pltpu.VMEM((TILE, cols, LANES), F32),
        ],
        compiler_params=pltpu.CompilerParams(**PARAMS),
        cost_estimate=cost(7),
        name="input_grad",
    )(g, *halo, cot, w)


def shifts(count):
    forward = [(i, i + 1) for i in range(count - 1)]
    return forward, [(b, a) for a, b in forward]


def halo_of(block, sizes):
    rows, cols, chans = block.shape
    forward, backward = shifts(sizes[0])
    top = lax.ppermute(block[rows - 3 :].reshape(-1, chans), TY, forward)
    bottom = lax.ppermute(block[:3].reshape(-1, chans), TY, backward)

    def edge(at):
        parts = []
        for j in range(3):
            column = lambda flat: [flat[i * cols + at + j][None] for i in range(3)]
            parts += column(top) + [block[:, at + j]] + column(bottom)
            parts.append(jnp.zeros((SPAN - rows - 6, chans), BF16))
        return jnp.concatenate(parts)

    forward, backward = shifts(sizes[1])
    left = lax.ppermute(edge(cols - 3), TX, forward)
    right = lax.ppermute(edge(0), TX, backward)
    return top, bottom, left, right


AXES = ("y", "x_hi", "core", "z", "x_lo")
SIZES = (4, 2, 2, 8, 2)
TY, TX = AXES[:3], AXES[3:]
PAIRS = ("core", "x_lo", "x_hi")
REST = ("y", "z")


def swap(value, axis):
    at = AXES.index(axis)
    index = np.arange(math.prod(SIZES)).reshape(SIZES)
    other = np.flip(index, axis=at)
    pairs = [(int(a), int(b)) for a, b in zip(index.ravel(), other.ravel())]
    return lax.ppermute(value, AXES, pairs)


def scatter(kept, sent):
    for n, axis in enumerate(PAIRS):
        kept = kept + swap(sent, axis).astype(F32)
        if n + 1 < len(PAIRS):
            upper = lax.axis_index(PAIRS[n + 1]) == 1
            size = kept.shape[0] // 2
            low, high = kept[:size], kept[size:]
            sent = jnp.where(upper, low, high).astype(BF16)
            kept = jnp.where(upper, high, low)
    return kept


def exchange(value, taps):
    count = math.prod(SIZES[AXES.index(a)] for a in REST)
    blocks = [value.reshape(count, -1, LANES), taps.reshape(count, -1, LANES)]
    rows = blocks[0].shape[1]
    split = jnp.concatenate([b.astype(BF16) for b in blocks], axis=1)
    split = lax.all_to_all(split, REST, 0, 0, tiled=True)
    mine = jnp.sum(split.astype(F32), axis=0).astype(BF16)
    out = lax.all_to_all(jnp.broadcast_to(mine, split.shape), REST, 0, 0, tiled=True)
    return out[:, :rows].reshape(value.shape), out[:, rows:].reshape(taps.shape).astype(F32)


def gather(out, taps):
    for axis in reversed(PAIRS):
        upper = lax.axis_index(axis) == 1
        rows = out.shape[0]
        got = swap(jnp.concatenate([out, taps.astype(BF16)]), axis)
        other = got[:rows]
        taps = taps + got[rows:].astype(F32)
        out = jnp.concatenate([jnp.where(upper, other, out), jnp.where(upper, out, other)])
    return out, taps


def body(x, cot, tissue, w, bias, gain, shift, we, be, wr, scale):
    rows, cols, chans = x.shape
    line = lambda v: v.reshape(1, -1)
    sizes = (math.prod(SIZES[:3]), math.prod(SIZES[3:]))
    factor = 1.0 / math.sqrt(rows * sizes[0] * cols * sizes[1])
    halo = halo_of(x, sizes)
    upper = lax.axis_index(PAIRS[0]).astype(jnp.int32).reshape(1)
    rest = (w, line(bias), line(gain), line(shift), we, line(be), wr, line(scale))
    g, kept, sent, taps = branch(x, halo, cot, tissue, upper, *rest)
    ghalo = halo_of(g, sizes)
    out, taps = exchange(scatter(kept, sent), taps)
    result = []
    for h in range(2):
        result.append(input_grad(g, ghalo, cot, w, h))
    out, taps = gather(out, taps)
    out = out.reshape(-1, 2 * chans, LANES)
    expand = out[:, :chans].transpose(1, 0, 2).reshape(chans, -1)
    reduce = out[:, chans:].reshape(-1, 2, LANES, LANES).transpose(0, 2, 1, 3).reshape(-1, chans)
    taps = jnp.concatenate([taps[:TAPS], taps[TAPS:]], axis=1)[: w.shape[0]]
    scaled = [v.astype(F32) * factor for v in (taps, expand, reduce)]
    return (jnp.concatenate(result, axis=2), *scaled)


def solution(mesh):
    fine = Mesh(mesh.devices.reshape(SIZES), AXES)
    pixels = P(TY, TX, None)
    return jax.shard_map(
        body,
        mesh=fine,
        in_specs=(pixels, pixels, P(TY, TX)) + (P(),) * 8,
        out_specs=(pixels, P(), P(), P()),
        check_vma=False,
    )
```

time: 186 us -> 190 us (1.022)
  the two profiles are of different devices: /device:TPU:2 before, /device:TPU:11 now
where the time goes in v3:
time: 190 us
  Pallas kernels  65.5 us (34%)
  starting transfers between devices  37.8 us (20%)
  waiting for transfers between devices  35.1 us (18%)
  blocking collectives  33 us (17%)
  local copies, waits for them, and re-layouts  11.8 us (6%)
  other arithmetic  5.37 us (3%)
    pallas_call x1, Pallas kernels, branch(): pl.pallas_call(branch_kernel, grid_spec=grid, out_shape=(jax.ShapeDtypeSt...  44.4 us
    pallas_call x2, Pallas kernels, input_grad(): pl.pallas_call(input_kernel, grid=(rows // TILE,), out_shape=jax.ShapeDty...  21.1 us
    all_to_all x1, blocking collectives, exchange(): split = lax.all_to_all(split, REST, 0, 0, tiled=True)  19.4 us
    ppermute x6, waiting for transfers between devices, swap(): return lax.ppermute(value, AXES, pairs)  18.3 us
    ppermute x2, starting transfers between devices, halo_of(): top = lax.ppermute(block[rows - 3:].reshape(-1, chans), TY, forward)  14.8 us
    all_to_all x1, blocking collectives, exchange(): lax.all_to_all(jnp.broadcast_to(mine, split.shape), REST, 0, 0, tiled=True)  13.5 us
    ppermute x2, waiting for transfers between devices, halo_of(): right = lax.ppermute(edge(0), TX, backward)  11.1 us
    ppermute x2, starting transfers between devices, halo_of(): left = lax.ppermute(edge(cols - 3), TX, forward)  8.99 us
  transfers between devices with their start and end apart: 14, of which 8 were waited for; matrix products, arithmetic and copies ran while one was open for 4% of the time, Pallas kernels for 11%

profile of v3, /device:TPU:11, one launch (start us, length us, event | category | flops | bytes accessed | tf_op | source)
XLA Modules:
  0.0 189.6 jit_solution(4043540791015532045)
XLA Ops:
  1.6 4.3 %collective-permute-start = (bf16[144,256]{1,0:T(8,128)(2,1)S(1)}, bf16[144,256]{1,0:T(8,128)(2,1)S(1)}, u32[]{:S(2)}, u32[]{:S(2)}) collective-permute-start(bf16[144,256]{1,0:T(8,128)(2,1)S(1)} %bitcast.73), channel_id=1, source_target_pairs={{0,16},{16,32},{32,48},{48,64},{64,80},{80,96},{96,112},{112,128},... | collective-permute-start | bytes 221192 | tf_op jit(solution)/shard_map/ppermute | solution.py:330
  5.9 1.9 %collective-permute-start.1 = (bf16[144,256]{1,0:T(8,128)(2,1)S(1)}, bf16[144,256]{1,0:T(8,128)(2,1)S(1)}, u32[]{:S(2)}, u32[]{:S(2)}) collective-permute-start(bf16[144,256]{1,0:T(8,128)(2,1)S(1)} %bitcast.71), channel_id=1, source_target_pairs={{16,0},{32,16},{48,32},{64,48},{80,64},{96,80},{112,96},{128,112},... | collective-permute-start | bytes 221192 | tf_op jit(solution)/shard_map/ppermute | solution.py:331
  7.8 1.9 %fusion.4 = (bf16[64,1,256]{2,1,0:T(2,128)(2,1)S(1)}, bf16[64,1,256]{2,1,0:T(2,128)(2,1)S(1)}, bf16[64,1,256]{2,1,0:T(2,128)(2,1)S(1)}, bf16[64,1,256]{2,1,0:T(2...) fusion(bf16[64,48,256]{2,1,0:T(8,128)(2,1)} %x_ref.1), kind=kLoop, calls=%fused_computation.43 | loop fusion | bytes 393216 | tf_op jit(solution)/shard_map/slice | solution.py:337
  9.9 3.2 %collective-permute-done.1.bottom = bf16[144,256]{1,0:T(8,128)(2,1)S(1)} collective-permute-done((bf16[144,256]{1,0:T(8,128)(2,1)S(1)}, bf16[144,256]{1,0:T(8,128)(2,1)S(1)}, u32[]{:S(2)}, u32[]{:S(2)}) %collective-permute-start.1) | collective-permute-done | bytes 73760 | tf_op jit(solution)/shard_map/ppermute | solution.py:331
  13.1 1.0 concatenate.41
  14.1 4.4 %collective-permute-start.2 = (bf16[240,256]{1,0:T(8,128)(2,1)S(1)}, bf16[240,256]{1,0:T(8,128)(2,1)S(1)}, u32[]{:S(2)}, u32[]{:S(2)}) collective-permute-start(bf16[240,256]{1,0:T(8,128)(2,1)S(1)} %concatenate.41), channel_id=1, source_target_pairs={{0,1},{1,2},{2,3},{3,4},{4,5},{5,6},{6,7},{7,8},{8,9},{9,10},{10,1... | collective-permute-start | bytes 368648 | tf_op jit(solution)/shard_map/ppermute | solution.py:342
  18.5 1.0 concatenate.42
  19.5 1.9 %collective-permute-start.3 = (bf16[240,256]{1,0:T(8,128)(2,1)S(1)}, bf16[240,256]{1,0:T(8,128)(2,1)S(1)}, u32[]{:S(2)}, u32[]{:S(2)}) collective-permute-start(bf16[240,256]{1,0:T(8,128)(2,1)S(1)} %concatenate.42), channel_id=1, source_target_pairs={{1,0},{2,1},{3,2},{4,3},{5,4},{6,5},{7,6},{8,7},{9,8},{10,9},{11,1... | collective-permute-start | bytes 368648 | tf_op jit(solution)/shard_map/ppermute | solution.py:343
  21.4 5.0 %collective-permute-done.3.right = bf16[240,256]{1,0:T(8,128)(2,1)S(1)} collective-permute-done((bf16[240,256]{1,0:T(8,128)(2,1)S(1)}, bf16[240,256]{1,0:T(8,128)(2,1)S(1)}, u32[]{:S(2)}, u32[]{:S(2)}) %collective-permute-start.3) | collective-permute-done | bytes 122912 | tf_op jit(solution)/shard_map/ppermute | solution.py:343
  27.1 44.4 %branch.1 = (bf16[64,48,256]{2,1,0:T(8,128)(2,1)}, f32[2048,128]{1,0:T(8,128)}, bf16[2048,128]{1,0:T(8,128)(2,1)}, f32[128,128]{1,0:T(8,128)}) custom-call(s32[4,3]{1,0:T(4,128)} %tissue.1, s32[1]{0:T(128)} %bitcast.upper, bf16[64,48,256]{2,1,0:T(8,128)(2,1)} %x_ref.1, bf16[144,256]{1,0:T(8,128)(2,1)} %copy-done.8, bf16[144,256]{1,0:T(8,128)(2,1)} %copy-done.9, ...), custom_call_target="tpu_custom_call" | custom-call | bytes 154980000 | tf_op jit(solution)/shard_map/branch/pallas_call | solution.py:251
  71.6 2.1 %collective-permute-done.8 = bf16[2048,128]{1,0:T(8,128)(2,1)S(1)} collective-permute-done((bf16[2048,128]{1,0:T(8,128)(2,1)}, bf16[2048,128]{1,0:T(8,128)(2,1)S(1)}, u32[]{:S(2)}, u32[]{:S(2)}) %collective-permute-start.8) | collective-permute-done | bytes 524320 | tf_op jit(solution)/shard_map/ppermute | solution.py:359
  73.7 1.3 convert_add_fusion
  75.2 7.7 %collective-permute-done.9 = bf16[1024,128]{1,0:T(8,128)(2,1)S(1)} collective-permute-done((bf16[1024,128]{1,0:T(8,128)(2,1)S(1)}, bf16[1024,128]{1,0:T(8,128)(2,1)S(1)}, u32[]{:S(2)}, u32[]{:S(2)}) %collective-permute-start.9) | collective-permute-done | bytes 262176 | tf_op jit(solution)/shard_map/ppermute | solution.py:359
  83.0 1.3 collective-permute-start.10
  84.3 4.1 %collective-permute-done.10 = bf16[512,128]{1,0:T(8,128)(2,1)S(1)} collective-permute-done((bf16[512,128]{1,0:T(8,128)(2,1)S(1)}, bf16[512,128]{1,0:T(8,128)(2,1)S(1)}, u32[]{:S(2)}, u32[]{:S(2)}) %collective-permute-start.10) | collective-permute-done | bytes 131104 | tf_op jit(solution)/shard_map/ppermute | solution.py:359
  88.5 19.4 %all_to_all.10 = bf16[32,20,128]{2,1,0:T(8,128)(2,1)S(1)} all-to-all(bf16[32,20,128]{2,1,0:T(8,128)(2,1)S(1)} %pad_maximum_fusion.6), channel_id=1, replica_groups=mesh['y'=4,'x_hi'=2,'core'=2,'z'=8,'x_lo'=2] {'y','z'}, dimensions={0} | all-to-all | bytes 327680 | tf_op jit(solution)/shard_map/all_to_all | solution.py:379
  108.0 13.5 %all_to_all.11 = bf16[32,20,128]{2,1,0:T(8,128)(2,1)S(1)} all-to-all(bf16[32,20,128]{2,1,0:T(8,128)(2,1)S(1)} %broadcast_in_dim.3), channel_id=1, replica_groups=mesh['y'=4,'x_hi'=2,'core'=2,'z'=8,'x_lo'=2] {'y','z'}, dimensions={0} | all-to-all | bytes 327680 | tf_op jit(solution)/shard_map/all_to_all | solution.py:381
  121.6 1.3 collective-permute-start.11
  122.9 4.4 %collective-permute-done.11 = bf16[640,128]{1,0:T(8,128)(2,1)S(1)} collective-permute-done((bf16[640,128]{1,0:T(8,128)(2,1)S(1)}, bf16[640,128]{1,0:T(8,128)(2,1)S(1)}, u32[]{:S(2)}, u32[]{:S(2)}) %collective-permute-start.11) | collective-permute-done | bytes 163872 | tf_op jit(solution)/shard_map/ppermute | solution.py:359
  128.8 10.5 %collective-permute-start.4 = (bf16[144,256]{1,0:T(8,128)(2,1)S(1)}, bf16[144,256]{1,0:T(8,128)(2,1)S(1)}, u32[]{:S(2)}, u32[]{:S(2)}) collective-permute-start(bf16[144,256]{1,0:T(8,128)(2,1)S(1)} %bitcast.72), channel_id=1, source_target_pairs={{0,16},{16,32},{32,48},{48,64},{64,80},{80,96},{96,112},{112,128},... | collective-permute-start | bytes 221192 | tf_op jit(solution)/shard_map/ppermute | solution.py:330
  139.3 2.1 %collective-permute-start.5 = (bf16[144,256]{1,0:T(8,128)(2,1)S(1)}, bf16[144,256]{1,0:T(8,128)(2,1)S(1)}, u32[]{:S(2)}, u32[]{:S(2)}) collective-permute-start(bf16[144,256]{1,0:T(8,128)(2,1)S(1)} %bitcast.70), channel_id=1, source_target_pairs={{16,0},{32,16},{48,32},{64,48},{80,64},{96,80},{112,96},{128,112},... | collective-permute-start | bytes 221192 | tf_op jit(solution)/shard_map/ppermute | solution.py:331
  141.6 2.5 %collective-permute-start.13 = (bf16[2176,128]{1,0:T(8,128)(2,1)S(1)}, bf16[2176,128]{1,0:T(8,128)(2,1)S(1)}, u32[]{:S(2)}, u32[]{:S(2)}) collective-permute-start(bf16[2176,128]{1,0:T(8,128)(2,1)S(1)} %pad_maximum_fusion.2), channel_id=1, source_target_pairs={{0,16},{1,17},{2,18},{3,19},{4,20},{5,21},{6,22},{7,23},{8,24},{9,... | collective-permute-start | bytes 1671176 | tf_op jit(solution)/shard_map/ppermute | solution.py:359
  144.2 2.5 %collective-permute-done.5.bottom = bf16[144,256]{1,0:T(8,128)(2,1)S(1)} collective-permute-done((bf16[144,256]{1,0:T(8,128)(2,1)S(1)}, bf16[144,256]{1,0:T(8,128)(2,1)S(1)}, u32[]{:S(2)}, u32[]{:S(2)}) %collective-permute-start.5) | collective-permute-done | bytes 73760 | tf_op jit(solution)/shard_map/ppermute | solution.py:331
  146.7 1.0 concatenate.43
  147.7 4.6 %collective-permute-start.6 = (bf16[240,256]{1,0:T(8,128)(2,1)S(1)}, bf16[240,256]{1,0:T(8,128)(2,1)S(1)}, u32[]{:S(2)}, u32[]{:S(2)}) collective-permute-start(bf16[240,256]{1,0:T(8,128)(2,1)S(1)} %concatenate.43), channel_id=1, source_target_pairs={{0,1},{1,2},{2,3},{3,4},{4,5},{5,6},{6,7},{7,8},{8,9},{9,10},{10,1... | collective-permute-start | bytes 368648 | tf_op jit(solution)/shard_map/ppermute | solution.py:342
  153.2 1.9 %collective-permute-start.7 = (bf16[240,256]{1,0:T(8,128)(2,1)S(1)}, bf16[240,256]{1,0:T(8,128)(2,1)S(1)}, u32[]{:S(2)}, u32[]{:S(2)}) collective-permute-start(bf16[240,256]{1,0:T(8,128)(2,1)S(1)} %concatenate.44), channel_id=1, source_target_pairs={{1,0},{2,1},{3,2},{4,3},{5,4},{6,5},{7,6},{8,7},{9,8},{10,9},{11,1... | collective-permute-start | bytes 368648 | tf_op jit(solution)/shard_map/ppermute | solution.py:343
  155.2 6.1 %collective-permute-done.7.right = bf16[240,256]{1,0:T(8,128)(2,1)S(1)} collective-permute-done((bf16[240,256]{1,0:T(8,128)(2,1)S(1)}, bf16[240,256]{1,0:T(8,128)(2,1)S(1)}, u32[]{:S(2)}, u32[]{:S(2)}) %collective-permute-start.7) | collective-permute-done | bytes 122912 | tf_op jit(solution)/shard_map/ppermute | solution.py:343
  162.0 10.5 %input_grad.3 = bf16[64,48,128]{2,1,0:T(8,128)(2,1)} custom-call(bf16[64,48,256]{2,1,0:T(8,128)(2,1)} %get-tuple-element.8.g_ref, bf16[144,256]{1,0:T(8,128)(2,1)} %copy-done.4, bf16[144,256]{1,0:T(8,128)(2,1)} %copy-done.5, bf16[240,256]{1,0:T(8,128)(2,1)} %copy-done.2, bf16[240,256]{1,0:T(8,128)(2,1)} %copy-done.3, bf16[64,48,256]{2,1,0:T(8,128)(2,1)} %cot.5, ...), custom_call_target="tpu_custom_call" | custom-call | bytes 25830000 | tf_op jit(solution)/shard_map/input_grad/pallas_call | solution.py:303
  172.5 10.6 %input_grad.2 = bf16[64,48,128]{2,1,0:T(8,128)(2,1)} custom-call(bf16[64,48,256]{2,1,0:T(8,128)(2,1)} %get-tuple-element.8.g_ref, bf16[144,256]{1,0:T(8,128)(2,1)} %copy-done.4, bf16[144,256]{1,0:T(8,128)(2,1)} %copy-done.5, bf16[240,256]{1,0:T(8,128)(2,1)} %copy-done.2, bf16[240,256]{1,0:T(8,128)(2,1)} %copy-done.3, bf16[64,48,256]{2,1,0:T(8,128)(2,1)} %cot.5, ...), custom_call_target="tpu_custom_call" | custom-call | bytes 25830000 | tf_op jit(solution)/shard_map/input_grad/pallas_call | solution.py:303
  183.1 2.4 %pad_maximum_fusion = bf16[64,48,256]{2,1,0:T(8,128)(2,1)} fusion(bf16[64,48,128]{2,1,0:T(8,128)(2,1)S(1)} %copy-done.1, bf16[64,48,128]{2,1,0:T(8,128)(2,1)} %input_grad.2), kind=kLoop, calls=%fused_computation | loop fusion | flops 3145728 | bytes 3145728 | tf_op jit(solution)/shard_map/concatenate | solution.py:416
  186.1 1.1 copy.46
  188.0 1.0 copy.45
  (69 shorter events, 7.4 us)
Async XLA Ops:
  1.6 8.3 %collective-permute-start = (bf16[144,256]{1,0:T(8,128)(2,1)S(1)}, bf16[144,256]{1,0:T(8,128)(2,1)S(1)}, u32[]{:S(2)}, u32[]{:S(2)}) collective-permute-start(bf16[144,256]{1,0:T(8,128)(2,1)S(1)} %bitcast.73), channel_id=1, source_target_pairs={{0,16},{16,32},{32,48},{48,64},{64,80},{80,96},{96,112},{112,128},... | collective-permute-start | bytes 221192 | tf_op jit(solution)/shard_map/ppermute | solution.py:330
  5.9 7.2 %collective-permute-start.1 = (bf16[144,256]{1,0:T(8,128)(2,1)S(1)}, bf16[144,256]{1,0:T(8,128)(2,1)S(1)}, u32[]{:S(2)}, u32[]{:S(2)}) collective-permute-start(bf16[144,256]{1,0:T(8,128)(2,1)S(1)} %bitcast.71), channel_id=1, source_target_pairs={{16,0},{32,16},{48,32},{64,48},{80,64},{96,80},{112,96},{128,112},... | collective-permute-start | bytes 221192 | tf_op jit(solution)/shard_map/ppermute | solution.py:331
  9.8 16.6 %copy-start.8 = (bf16[144,256]{1,0:T(8,128)(2,1)}, bf16[144,256]{1,0:T(8,128)(2,1)S(1)}, u32[]{:S(2)}) copy-start(bf16[144,256]{1,0:T(8,128)(2,1)S(1)} %collective-permute-done.top) | copy-start | bytes 221188
  13.1 13.4 %copy-start.9 = (bf16[144,256]{1,0:T(8,128)(2,1)}, bf16[144,256]{1,0:T(8,128)(2,1)S(1)}, u32[]{:S(2)}) copy-start(bf16[144,256]{1,0:T(8,128)(2,1)S(1)} %collective-permute-done.1.bottom) | copy-start | bytes 221188
  14.1 7.3 %collective-permute-start.2 = (bf16[240,256]{1,0:T(8,128)(2,1)S(1)}, bf16[240,256]{1,0:T(8,128)(2,1)S(1)}, u32[]{:S(2)}, u32[]{:S(2)}) collective-permute-start(bf16[240,256]{1,0:T(8,128)(2,1)S(1)} %concatenate.41), channel_id=1, source_target_pairs={{0,1},{1,2},{2,3},{3,4},{4,5},{5,6},{6,7},{7,8},{8,9},{9,10},{10,1... | collective-permute-start | bytes 368648 | tf_op jit(solution)/shard_map/ppermute | solution.py:342
  19.5 6.9 %collective-permute-start.3 = (bf16[240,256]{1,0:T(8,128)(2,1)S(1)}, bf16[240,256]{1,0:T(8,128)(2,1)S(1)}, u32[]{:S(2)}, u32[]{:S(2)}) collective-permute-start(bf16[240,256]{1,0:T(8,128)(2,1)S(1)} %concatenate.42), channel_id=1, source_target_pairs={{1,0},{2,1},{3,2},{4,3},{5,4},{6,5},{7,6},{8,7},{9,8},{10,9},{11,1... | collective-permute-start | bytes 368648 | tf_op jit(solution)/shard_map/ppermute | solution.py:343
  21.4 5.0 %copy-start.6 = (bf16[240,256]{1,0:T(8,128)(2,1)}, bf16[240,256]{1,0:T(8,128)(2,1)S(1)}, u32[]{:S(2)}) copy-start(bf16[240,256]{1,0:T(8,128)(2,1)S(1)} %collective-permute-done.2.left) | copy-start | bytes 368644
  26.4 0.6 copy-start.7
  71.5 2.2 %collective-permute-start.8 = (bf16[2048,128]{1,0:T(8,128)(2,1)}, bf16[2048,128]{1,0:T(8,128)(2,1)S(1)}, u32[]{:S(2)}, u32[]{:S(2)}) collective-permute-start(bf16[2048,128]{1,0:T(8,128)(2,1)} %get-tuple-element.10), channel_id=1, source_target_pairs={{0,16},{1,17},{2,18},{3,19},{4,20},{5,21},{6,22},{7,23},{8,24},{9,... | collective-permute-start | bytes 1572872 | tf_op jit(solution)/shard_map/ppermute | solution.py:359
  75.0 9.3 %copy-start.10 = (f32[128,128]{1,0:T(8,128)S(1)}, f32[128,128]{1,0:T(8,128)}, u32[]{:S(2)}) copy-start(f32[128,128]{1,0:T(8,128)} %get-tuple-element.11) | copy-start | bytes 196612
  75.1 7.8 %collective-permute-start.9 = (bf16[1024,128]{1,0:T(8,128)(2,1)S(1)}, bf16[1024,128]{1,0:T(8,128)(2,1)S(1)}, u32[]{:S(2)}, u32[]{:S(2)}) collective-permute-start(bf16[1024,128]{1,0:T(8,128)(2,1)S(1)} %select_convert_fusion), channel_id=1, source_target_pairs={{0,1},{1,0},{2,3},{3,2},{4,5},{5,4},{6,7},{7,6},{8,9},{9,8},{10,11... | collective-permute-start | bytes 786440 | tf_op jit(solution)/shard_map/ppermute | solution.py:359
  83.0 5.4 %collective-permute-start.10 = (bf16[512,128]{1,0:T(8,128)(2,1)S(1)}, bf16[512,128]{1,0:T(8,128)(2,1)S(1)}, u32[]{:S(2)}, u32[]{:S(2)}) collective-permute-start(bf16[512,128]{1,0:T(8,128)(2,1)S(1)} %select_convert_fusion.1), channel_id=1, source_target_pairs={{0,32},{1,33},{2,34},{3,35},{4,36},{5,37},{6,38},{7,39},{8,40},{9,... | collective-permute-start | bytes 393224 | tf_op jit(solution)/shard_map/ppermute | solution.py:359
  88.5 39.8 %copy-start = (bf16[64,48,256]{2,1,0:T(8,128)(2,1)S(1)}, bf16[64,48,256]{2,1,0:T(8,128)(2,1)}, u32[]{:S(2)}) copy-start(bf16[64,48,256]{2,1,0:T(8,128)(2,1)} %get-tuple-element.8.g_ref) | copy-start | bytes 4718596
  121.6 5.8 %collective-permute-start.11 = (bf16[640,128]{1,0:T(8,128)(2,1)S(1)}, bf16[640,128]{1,0:T(8,128)(2,1)S(1)}, u32[]{:S(2)}, u32[]{:S(2)}) collective-permute-start(bf16[640,128]{1,0:T(8,128)(2,1)S(1)} %pad_maximum_fusion.7), channel_id=1, source_target_pairs={{0,32},{1,33},{2,34},{3,35},{4,36},{5,37},{6,38},{7,39},{8,40},{9,... | collective-permute-start | bytes 491528 | tf_op jit(solution)/shard_map/ppermute | solution.py:359
  127.4 14.0 %collective-permute-start.12 = (bf16[1152,128]{1,0:T(8,128)(2,1)S(1)}, bf16[1152,128]{1,0:T(8,128)(2,1)S(1)}, u32[]{:S(2)}, u32[]{:S(2)}) collective-permute-start(bf16[1152,128]{1,0:T(8,128)(2,1)S(1)} %pad_maximum_fusion.4), channel_id=1, source_target_pairs={{0,1},{1,0},{2,3},{3,2},{4,5},{5,4},{6,7},{7,6},{8,9},{9,8},{10,11... | collective-permute-start | bytes 884744 | tf_op jit(solution)/shard_map/ppermute | solution.py:359
  128.8 15.3 %collective-permute-start.4 = (bf16[144,256]{1,0:T(8,128)(2,1)S(1)}, bf16[144,256]{1,0:T(8,128)(2,1)S(1)}, u32[]{:S(2)}, u32[]{:S(2)}) collective-permute-start(bf16[144,256]{1,0:T(8,128)(2,1)S(1)} %bitcast.72), channel_id=1, source_target_pairs={{0,16},{16,32},{32,48},{48,64},{64,80},{80,96},{96,112},{112,128},... | collective-permute-start | bytes 221192 | tf_op jit(solution)/shard_map/ppermute | solution.py:330
  139.3 7.4 %collective-permute-start.5 = (bf16[144,256]{1,0:T(8,128)(2,1)S(1)}, bf16[144,256]{1,0:T(8,128)(2,1)S(1)}, u32[]{:S(2)}, u32[]{:S(2)}) collective-permute-start(bf16[144,256]{1,0:T(8,128)(2,1)S(1)} %bitcast.70), channel_id=1, source_target_pairs={{16,0},{32,16},{48,32},{64,48},{80,64},{96,80},{112,96},{128,112},... | collective-permute-start | bytes 221192 | tf_op jit(solution)/shard_map/ppermute | solution.py:331
  141.6 43.9 %collective-permute-start.13 = (bf16[2176,128]{1,0:T(8,128)(2,1)S(1)}, bf16[2176,128]{1,0:T(8,128)(2,1)S(1)}, u32[]{:S(2)}, u32[]{:S(2)}) collective-permute-start(bf16[2176,128]{1,0:T(8,128)(2,1)S(1)} %pad_maximum_fusion.2), channel_id=1, source_target_pairs={{0,16},{1,17},{2,18},{3,19},{4,20},{5,21},{6,22},{7,23},{8,24},{9,... | collective-permute-start | bytes 1671176 | tf_op jit(solution)/shard_map/ppermute | solution.py:359
  144.1 17.2 %copy-start.4 = (bf16[144,256]{1,0:T(8,128)(2,1)}, bf16[144,256]{1,0:T(8,128)(2,1)S(1)}, u32[]{:S(2)}) copy-start(bf16[144,256]{1,0:T(8,128)(2,1)S(1)} %collective-permute-done.4.top) | copy-start | bytes 221188
  146.7 14.6 %copy-start.5 = (bf16[144,256]{1,0:T(8,128)(2,1)}, bf16[144,256]{1,0:T(8,128)(2,1)S(1)}, u32[]{:S(2)}) copy-start(bf16[144,256]{1,0:T(8,128)(2,1)S(1)} %collective-permute-done.5.bottom) | copy-start | bytes 221188
  147.7 7.5 %collective-permute-start.6 = (bf16[240,256]{1,0:T(8,128)(2,1)S(1)}, bf16[240,256]{1,0:T(8,128)(2,1)S(1)}, u32[]{:S(2)}, u32[]{:S(2)}) collective-permute-start(bf16[240,256]{1,0:T(8,128)(2,1)S(1)} %concatenate.43), channel_id=1, source_target_pairs={{0,1},{1,2},{2,3},{3,4},{4,5},{5,6},{6,7},{7,8},{8,9},{9,10},{10,1... | collective-permute-start | bytes 368648 | tf_op jit(solution)/shard_map/ppermute | solution.py:342
  153.2 8.1 %collective-permute-start.7 = (bf16[240,256]{1,0:T(8,128)(2,1)S(1)}, bf16[240,256]{1,0:T(8,128)(2,1)S(1)}, u32[]{:S(2)}, u32[]{:S(2)}) collective-permute-start(bf16[240,256]{1,0:T(8,128)(2,1)S(1)} %concatenate.44), channel_id=1, source_target_pairs={{1,0},{2,1},{3,2},{4,3},{5,4},{6,5},{7,6},{8,7},{9,8},{10,9},{11,1... | collective-permute-start | bytes 368648 | tf_op jit(solution)/shard_map/ppermute | solution.py:343
  155.2 6.1 %copy-start.2 = (bf16[240,256]{1,0:T(8,128)(2,1)}, bf16[240,256]{1,0:T(8,128)(2,1)S(1)}, u32[]{:S(2)}) copy-start(bf16[240,256]{1,0:T(8,128)(2,1)S(1)} %collective-permute-done.6.left) | copy-start | bytes 368644
  161.3 0.7 copy-start.3
  172.5 10.6 %copy-start.1 = (bf16[64,48,128]{2,1,0:T(8,128)(2,1)S(1)}, bf16[64,48,128]{2,1,0:T(8,128)(2,1)}, u32[]{:S(2)}) copy-start(bf16[64,48,128]{2,1,0:T(8,128)(2,1)} %input_grad.3) | copy-start | bytes 2359300

commit v4 on v3

--- a/solution.py
+++ b/solution.py
@@ -15,7 +15,7 @@
 RG = 8
 CB = 3
 TAPS = 64
-SPAN = 80
+EXTRA = 32
 VMEM = pl.BlockSpec(memory_space=pltpu.VMEM)
 PARAMS = dict(vmem_limit_bytes=56 << 20)
 
@@ -41,7 +41,7 @@
 
 def fill(pad, core, top, bottom, left, right, halves=(0, 1)):
     rows, cols = core.shape[0], core.shape[1]
-    span = left.shape[0] // 3
+    ends = (5, 8 + cols)
     for k, h in enumerate(halves):
 
         def put(i, _):
@@ -49,27 +49,24 @@
             return 0
 
         lax.fori_loop(0, rows, put, 0, unroll=4)
-        for i in range(3):
-            pad[k, i, 8 : 8 + cols, :] = top[i * cols : (i + 1) * cols, half(h)].astype(F32)
-            pad[k, 3 + rows + i, 8 : 8 + cols, :] = bottom[
-                i * cols : (i + 1) * cols, half(h)
-            ].astype(F32)
-
-        def side(first, count):
-            for j in range(3):
-                at = pl.ds(pl.multiple_of(j * span + first, 8), 8)
-                lv = left[at, half(h)].astype(F32)
-                rv = right[at, half(h)].astype(F32)
-                for r in range(count):
-                    pad[k, first + r, 5 + j : 6 + j, :] = lv[r : r + 1]
-                    pad[k, first + r, 8 + cols + j : 9 + cols + j, :] = rv[r : r + 1]
-
-        def eight(i, _):
-            side(i * 8, 8)
+        for first, flat in ((0, top), (3 + rows, bottom)):
+            extra = flat[3 * cols : 3 * cols + 24, half(h)].astype(F32)
+            for i in range(3):
+                at = slice(i * cols, (i + 1) * cols)
+                pad[k, first + i, 8 : 8 + cols, :] = flat[at, half(h)].astype(F32)
+                for n, end in enumerate(ends):
+                    corner = extra[n * 9 + i * 3 : n * 9 + i * 3 + 3]
+                    pad[k, first + i, end : end + 3, :] = corner
+
+        def side(i, _):
+            at = pl.ds(pl.multiple_of(i * 24, 8), 24)
+            for end, flat in zip(ends, (left, right)):
+                v = flat[at, half(h)].astype(F32)
+                for r in range(8):
+                    pad[k, 3 + i * 8 + r, end : end + 3, :] = v[r * 3 : r * 3 + 3]
             return 0
 
-        lax.fori_loop(0, (rows + 6) // 8, eight, 0)
-        side((rows + 6) // 8 * 8, (rows + 6) % 8)
+        lax.fori_loop(0, rows // 8, side, 0)
 
 
 def stencil(pad, wide, h, row, col):
@@ -116,7 +113,7 @@
 
 def branch_kernel(
     tissue, upper, x_ref, top, bottom, left, right, cot, w_ref, bias, gain, shift, we, be, wr, scale,
-    g_ref, kept, sent, taps, acc_ref, gpad, pad, wide, u_ref, nhat_ref, rstd_ref, normed, normed_t, go, go_t, hid, dz, dn,
+    g_ref, g_left, g_right, g_top, g_bottom, kept, sent, taps, acc_ref, gpad, pad, wide, u_ref, nhat_ref, rstd_ref, normed, normed_t, go, go_t, hid, dz, dn,
 ):
     step = pl.program_id(0)
     rows, cols, chans = cot.shape
@@ -199,12 +196,28 @@
     @pl.when(step == pl.num_programs(0) - 1)
     def _():
         filter_sums(pad, gpad, taps)
+        high = gpad.shape[1] - 6
+        for h in range(2):
+            for first, flat in ((3, g_top), (high, g_bottom)):
+                for i in range(3):
+                    flat[i * cols : (i + 1) * cols, half(h)] = gpad[h, first + i].astype(BF16)
+            for col, flat in ((0, g_left), (cols - 3, g_right)):
+
+                def collect(i, _, col=col, flat=flat, h=h):
+                    v = [gpad[h, 3 + i * 16 + r, col : col + 3, :] for r in range(16)]
+                    at = pl.ds(pl.multiple_of(i * 48, 16), 48)
+                    flat[at, half(h)] = jnp.concatenate(v, axis=0).astype(BF16)
+                    return 0
+
+                lax.fori_loop(0, high // 16, collect, 0)
         blocks = hidden // LANES
         side = upper[0]
         for e in range(blocks):
             cut = half(e)
             other = acc_ref[chans : 2 * chans, cut].T
+            count = 2 * TAPS // blocks
             piece = [acc_ref[0:chans, cut], other[:, :LANES], other[:, LANES:]]
+            piece += [taps[e * count : (e + 1) * count, :], jnp.zeros((EXTRA - count, LANES), F32)]
             piece = jnp.concatenate(piece, axis=0)
             size = piece.shape[0]
             at = pl.ds((e % (blocks // 2)) * size, size)
@@ -225,13 +238,17 @@
     pix = TILE * cols
     block = pl.BlockSpec((TILE, cols, chans), lambda s, t, u: (s, 0, 0))
     whole = lambda *shape: pl.BlockSpec(shape, lambda s, t, u: (0, 0))
-    size = 2 * chans * hidden // LANES // 2
+    size = (2 * chans + EXTRA) * (hidden // LANES) // 2
     grid = pltpu.PrefetchScalarGridSpec(
         num_scalar_prefetch=2,
         grid=(rows // TILE,),
         in_specs=[VMEM] * 5 + [block] + [VMEM] * 8,
-        out_specs=[block, whole(size, LANES), whole(size, LANES), whole(2 * TAPS, LANES)],
+        out_specs=[block]
+        + [whole(3 * rows, chans)] * 2
+        + [whole(3 * cols, chans)] * 2
+        + [whole(size, LANES)] * 2,
         scratch_shapes=[
+            pltpu.VMEM((2 * TAPS, LANES), F32),
             pltpu.VMEM((2 * chans, hidden), F32),
             pltpu.VMEM((2, rows + 6, cols, LANES), F32),
             pltpu.VMEM((2, rows + 6, cols + 16, LANES), F32),
@@ -253,9 +270,12 @@
         grid_spec=grid,
         out_shape=(
             jax.ShapeDtypeStruct(x.shape, BF16),
+            jax.ShapeDtypeStruct((3 * rows, chans), BF16),
+            jax.ShapeDtypeStruct((3 * rows, chans), BF16),
+            jax.ShapeDtypeStruct((3 * cols, chans), BF16),
+            jax.ShapeDtypeStruct((3 * cols, chans), BF16),
             jax.ShapeDtypeStruct((size, LANES), F32),
             jax.ShapeDtypeStruct((size, LANES), BF16),
-            jax.ShapeDtypeStruct((2 * TAPS, LANES), F32),
         ),
         compiler_params=pltpu.CompilerParams(**PARAMS),
         cost_estimate=cost(42),
@@ -319,78 +339,81 @@
     )(g, *halo, cot, w)
 
 
-def shifts(count):
-    forward = [(i, i + 1) for i in range(count - 1)]
-    return forward, [(b, a) for a, b in forward]
-
-
-def halo_of(block, sizes):
-    rows, cols, chans = block.shape
-    forward, backward = shifts(sizes[0])
-    top = lax.ppermute(block[rows - 3 :].reshape(-1, chans), TY, forward)
-    bottom = lax.ppermute(block[:3].reshape(-1, chans), TY, backward)
-
-    def edge(at):
-        parts = []
-        for j in range(3):
-            column = lambda flat: [flat[i * cols + at + j][None] for i in range(3)]
-            parts += column(top) + [block[:, at + j]] + column(bottom)
-            parts.append(jnp.zeros((SPAN - rows - 6, chans), BF16))
-        return jnp.concatenate(parts)
-
-    forward, backward = shifts(sizes[1])
-    left = lax.ppermute(edge(cols - 3), TX, forward)
-    right = lax.ppermute(edge(0), TX, backward)
-    return top, bottom, left, right
-
-
 AXES = ("y", "x_hi", "core", "z", "x_lo")
 SIZES = (4, 2, 2, 8, 2)
 TY, TX = AXES[:3], AXES[3:]
-PAIRS = ("core", "x_lo", "x_hi")
-REST = ("y", "z")
-
-
-def swap(value, axis):
-    at = AXES.index(axis)
+
+
+def beside(value, axes, odd):
+    count = math.prod(SIZES[AXES.index(a)] for a in axes)
+    pairs = [(i, i + 1) for i in range(odd, count - 1, 2)]
+    return lax.ppermute(value, axes, pairs + [(b, a) for a, b in pairs])
+
+
+def both_sides(low, high, axes):
+    odd = lax.axis_index(axes) % 2 == 1
+    first = beside(jnp.where(odd, low, high), axes, 0)
+    second = beside(jnp.where(odd, high, low), axes, 1)
+    return jnp.where(odd, first, second), jnp.where(odd, second, first)
+
+
+def halo_of(left, right, top, bottom):
+    chans = left.shape[1]
+    left, right = both_sides(left, right, TX)
+    filler = jnp.zeros((14, chans), BF16)
+    top = jnp.concatenate([top, left[:9], right[:9], filler])
+    bottom = jnp.concatenate([bottom, left[-9:], right[-9:], filler])
+    top, bottom = both_sides(top, bottom, TY)
+    return top, bottom, left, right
+
+
+SWAPS = {
+    "core": (("core",), ("core",)),
+    "x_near": (("x_lo",), ("x_lo", "x_hi")),
+    "x_far": (("x_lo", "x_hi"), ("x_hi",)),
+    "y_near": ((("y", 1),), (("y", 1), ("y", 2))),
+    "y_far": ((("y", 3),), (("y", 2),)),
+}
+
+
+def keeps_upper(name):
+    bit = 0
+    for item in SWAPS[name][1]:
+        axis, mask = item if isinstance(item, tuple) else (item, 1)
+        bit = bit + (lax.axis_index(axis) // mask) % 2
+    return bit % 2
+
+
+def swap(value, name):
     index = np.arange(math.prod(SIZES)).reshape(SIZES)
-    other = np.flip(index, axis=at)
+    where = np.indices(SIZES)
+    for item in SWAPS[name][0]:
+        axis, mask = item if isinstance(item, tuple) else (item, 1)
+        where[AXES.index(axis)] ^= mask
+    other = index[tuple(where)]
     pairs = [(int(a), int(b)) for a, b in zip(index.ravel(), other.ravel())]
     return lax.ppermute(value, AXES, pairs)
 
 
-def scatter(kept, sent):
-    for n, axis in enumerate(PAIRS):
-        kept = kept + swap(sent, axis).astype(F32)
-        if n + 1 < len(PAIRS):
-            upper = lax.axis_index(PAIRS[n + 1]) == 1
+def total(kept, sent):
+    names = list(SWAPS)
+    for n, name in enumerate(names):
+        kept = kept + swap(sent, name).astype(F32)
+        if n + 1 < len(names):
+            upper = keeps_upper(names[n + 1]) == 1
             size = kept.shape[0] // 2
             low, high = kept[:size], kept[size:]
             sent = jnp.where(upper, low, high).astype(BF16)
             kept = jnp.where(upper, high, low)
-    return kept
-
-
-def exchange(value, taps):
-    count = math.prod(SIZES[AXES.index(a)] for a in REST)
-    blocks = [value.reshape(count, -1, LANES), taps.reshape(count, -1, LANES)]
-    rows = blocks[0].shape[1]
-    split = jnp.concatenate([b.astype(BF16) for b in blocks], axis=1)
-    split = lax.all_to_all(split, REST, 0, 0, tiled=True)
-    mine = jnp.sum(split.astype(F32), axis=0).astype(BF16)
-    out = lax.all_to_all(jnp.broadcast_to(mine, split.shape), REST, 0, 0, tiled=True)
-    return out[:, :rows].reshape(value.shape), out[:, rows:].reshape(taps.shape).astype(F32)
-
-
-def gather(out, taps):
-    for axis in reversed(PAIRS):
-        upper = lax.axis_index(axis) == 1
-        rows = out.shape[0]
-        got = swap(jnp.concatenate([out, taps.astype(BF16)]), axis)
-        other = got[:rows]
-        taps = taps + got[rows:].astype(F32)
+    count = SIZES[AXES.index("z")]
+    copies = jnp.broadcast_to(kept.astype(BF16)[None], (count, *kept.shape))
+    copies = lax.all_to_all(copies, "z", 0, 0, tiled=True)
+    out = jnp.sum(copies.astype(F32), axis=0).astype(BF16)
+    for name in reversed(names):
+        upper = keeps_upper(name) == 1
+        other = swap(out, name)
         out = jnp.concatenate([jnp.where(upper, other, out), jnp.where(upper, out, other)])
-    return out, taps
+    return out
 
 
 def body(x, cot, tissue, w, bias, gain, shift, we, be, wr, scale):
@@ -398,20 +421,21 @@
     line = lambda v: v.reshape(1, -1)
     sizes = (math.prod(SIZES[:3]), math.prod(SIZES[3:]))
     factor = 1.0 / math.sqrt(rows * sizes[0] * cols * sizes[1])
-    halo = halo_of(x, sizes)
-    upper = lax.axis_index(PAIRS[0]).astype(jnp.int32).reshape(1)
+    edges = (x[:, :3], x[:, cols - 3 :], x[:3], x[rows - 3 :])
+    halo = halo_of(*(v.reshape(-1, chans) for v in edges))
+    upper = keeps_upper("core").astype(jnp.int32).reshape(1)
     rest = (w, line(bias), line(gain), line(shift), we, line(be), wr, line(scale))
-    g, kept, sent, taps = branch(x, halo, cot, tissue, upper, *rest)
-    ghalo = halo_of(g, sizes)
-    out, taps = exchange(scatter(kept, sent), taps)
+    g, *edges, kept, sent = branch(x, halo, cot, tissue, upper, *rest)
+    ghalo = halo_of(*edges)
     result = []
     for h in range(2):
         result.append(input_grad(g, ghalo, cot, w, h))
-    out, taps = gather(out, taps)
-    out = out.reshape(-1, 2 * chans, LANES)
+    out = total(kept, sent).reshape(-1, 2 * chans + EXTRA, LANES)
     expand = out[:, :chans].transpose(1, 0, 2).reshape(chans, -1)
-    reduce = out[:, chans:].reshape(-1, 2, LANES, LANES).transpose(0, 2, 1, 3).reshape(-1, chans)
-    taps = jnp.concatenate([taps[:TAPS], taps[TAPS:]], axis=1)[: w.shape[0]]
+    reduce = out[:, chans : 2 * chans].reshape(-1, 2, LANES, LANES)
+    reduce = reduce.transpose(0, 2, 1, 3).reshape(-1, chans)
+    taps = out[:, 2 * chans : 2 * chans + 2 * TAPS // out.shape[0]].reshape(2, TAPS, LANES)
+    taps = taps.transpose(1, 0, 2).reshape(TAPS, chans)[: w.shape[0]]
     scaled = [v.astype(F32) * factor for v in (taps, expand, reduce)]
     return (jnp.concatenate(result, axis=2), *scaled)
 

time: 190 us -> 175 us (0.921)
  the two profiles are of different devices: /device:TPU:11 before, /device:TPU:7 now
where the time goes in v4:
time: 175 us
  Pallas kernels  65.7 us (38%)
  waiting for transfers between devices  49.1 us (28%)
  starting transfers between devices  28.3 us (16%)
  blocking collectives  17.9 us (10%)
  other arithmetic  7.81 us (4%)
  local copies, waits for them, and re-layouts  4.92 us (3%)
    pallas_call x1, Pallas kernels, branch(): pl.pallas_call(branch_kernel, grid_spec=grid, out_shape=(jax.ShapeDtypeSt...  44.6 us
    ppermute x10, waiting for transfers between devices, swap(): return lax.ppermute(value, AXES, pairs)  31.4 us
    pallas_call x2, Pallas kernels, input_grad(): pl.pallas_call(input_kernel, grid=(rows // TILE,), out_shape=jax.ShapeDty...  21 us
    all_to_all x1, blocking collectives, total(): copies = lax.all_to_all(copies, 'z', 0, 0, tiled=True)  17.9 us
    ppermute x8, waiting for transfers between devices, beside(): return lax.ppermute(value, axes, pairs + [(b, a) for a, b in pairs])  17.7 us
    ppermute x8, starting transfers between devices, beside(): return lax.ppermute(value, axes, pairs + [(b, a) for a, b in pairs])  14.4 us
    ppermute x10, starting transfers between devices, swap(): return lax.ppermute(value, AXES, pairs)  13.9 us
  transfers between devices with their start and end apart: 18, of which 13 were waited for; matrix products, arithmetic and copies ran while one was open for 3% of the time, Pallas kernels for 12%

profile of v4, /device:TPU:7, one launch (start us, length us, event | category | flops | bytes accessed | tf_op | source)
XLA Modules:
  0.0 175.0 jit_solution(5658342669535836650)
XLA Ops:
  0.6 1.2 broadcast_select_fusion.7
  1.9 3.8 %collective-permute-start.1 = (bf16[192,256]{1,0:T(8,128)(2,1)S(1)}, bf16[192,256]{1,0:T(8,128)(2,1)S(1)}, u32[]{:S(2)}, u32[]{:S(2)}) collective-permute-start(bf16[192,256]{1,0:T(8,128)(2,1)S(1)} %select_n.290), channel_id=1, source_target_pairs={{1,2},{3,4},{5,6},{7,8},{9,10},{11,12},{13,14},{2,1},{4,3},{6,5},{... | collective-permute-start | bytes 294920 | tf_op jit(solution)/shard_map/ppermute | solution.py:350
  5.9 0.9 fusion
  7.0 1.2 collective-permute-done.1
  8.2 3.1 %collective-permute-done = bf16[192,256]{1,0:T(8,128)(2,1)S(1)} collective-permute-done((bf16[192,256]{1,0:T(8,128)(2,1)S(1)}, bf16[192,256]{1,0:T(8,128)(2,1)S(1)}, u32[]{:S(2)}, u32[]{:S(2)}) %collective-permute-start) | collective-permute-done | bytes 98336 | tf_op jit(solution)/shard_map/ppermute | solution.py:350
  11.5 4.7 %collective-permute-start.3 = (bf16[176,256]{1,0:T(8,128)(2,1)S(1)}, bf16[176,256]{1,0:T(8,128)(2,1)S(1)}, u32[]{:S(2)}, u32[]{:S(2)}) collective-permute-start(bf16[176,256]{1,0:T(8,128)(2,1)S(1)} %get-tuple-element.38), channel_id=1, source_target_pairs={{16,32},{48,64},{80,96},{112,128},{144,160},{176,192},{208,224},{3... | collective-permute-start | bytes 270344 | tf_op jit(solution)/shard_map/ppermute | solution.py:350
  16.3 4.1 %collective-permute-done.3 = bf16[176,256]{1,0:T(8,128)(2,1)S(1)} collective-permute-done((bf16[176,256]{1,0:T(8,128)(2,1)S(1)}, bf16[176,256]{1,0:T(8,128)(2,1)S(1)}, u32[]{:S(2)}, u32[]{:S(2)}) %collective-permute-start.3) | collective-permute-done | bytes 90144 | tf_op jit(solution)/shard_map/ppermute | solution.py:350
  21.1 44.6 %branch.1 = (bf16[64,48,256]{2,1,0:T(8,128)(2,1)}, bf16[192,256]{1,0:T(8,128)(2,1)}, bf16[192,256]{1,0:T(8,128)(2,1)}, bf16[144,256]{1,0:T(8,128)(2,1)}, bf16[14...) custom-call(s32[4,3]{1,0:T(4,128)} %tissue.1, s32[1]{0:T(128)} %bitcast.upper, ...), custom_call_target="tpu_custom_call" | custom-call | bytes 154980000 | tf_op jit(solution)/shard_map/branch/pallas_call | solution.py:268
  65.9 2.1 %collective-permute-done.8 = bf16[2176,128]{1,0:T(8,128)(2,1)S(1)} collective-permute-done((bf16[2176,128]{1,0:T(8,128)(2,1)}, bf16[2176,128]{1,0:T(8,128)(2,1)S(1)}, u32[]{:S(2)}, u32[]{:S(2)}) %collective-permute-start.8) | collective-permute-done | bytes 557088 | tf_op jit(solution)/shard_map/ppermute | solution.py:395
  68.0 1.3 convert_add_fusion
  69.6 8.0 %collective-permute-done.9 = bf16[1088,128]{1,0:T(8,128)(2,1)S(1)} collective-permute-done((bf16[1088,128]{1,0:T(8,128)(2,1)S(1)}, bf16[1088,128]{1,0:T(8,128)(2,1)S(1)}, u32[]{:S(2)}, u32[]{:S(2)}) %collective-permute-start.9) | collective-permute-done | bytes 278560 | tf_op jit(solution)/shard_map/ppermute | solution.py:395
  77.9 5.4 %collective-permute-done.10 = bf16[544,128]{1,0:T(8,128)(2,1)S(1)} collective-permute-done((bf16[544,128]{1,0:T(8,128)(2,1)S(1)}, bf16[544,128]{1,0:T(8,128)(2,1)S(1)}, u32[]{:S(2)}, u32[]{:S(2)}) %collective-permute-start.10) | collective-permute-done | bytes 139296 | tf_op jit(solution)/shard_map/ppermute | solution.py:395
  83.3 1.4 collective-permute-start.11
  84.7 1.9 %collective-permute-done.11 = bf16[272,128]{1,0:T(8,128)(2,1)S(1)} collective-permute-done((bf16[272,128]{1,0:T(8,128)(2,1)S(1)}, bf16[272,128]{1,0:T(8,128)(2,1)S(1)}, u32[]{:S(2)}, u32[]{:S(2)}) %collective-permute-start.11) | collective-permute-done | bytes 69664 | tf_op jit(solution)/shard_map/ppermute | solution.py:395
  86.6 2.0 %collective-permute-start.12 = (bf16[136,128]{1,0:T(8,128)(2,1)S(1)}, bf16[136,128]{1,0:T(8,128)(2,1)S(1)}, u32[]{:S(2)}, u32[]{:S(2)}) collective-permute-start(bf16[136,128]{1,0:T(8,128)(2,1)S(1)} %select_convert_fusion.3), channel_id=1, source_target_pairs={{0,192},{1,193},{2,194},{3,195},{4,196},{5,197},{6,198},{7,199},{8... | collective-permute-start | bytes 104456 | tf_op jit(solution)/shard_map/ppermute | solution.py:395
  88.7 2.0 %collective-permute-done.12 = bf16[136,128]{1,0:T(8,128)(2,1)S(1)} collective-permute-done((bf16[136,128]{1,0:T(8,128)(2,1)S(1)}, bf16[136,128]{1,0:T(8,128)(2,1)S(1)}, u32[]{:S(2)}, u32[]{:S(2)}) %collective-permute-start.12) | collective-permute-done | bytes 34848 | tf_op jit(solution)/shard_map/ppermute | solution.py:395
  90.8 17.9 %all_to_all.5 = bf16[8,136,128]{2,1,0:T(8,128)(2,1)S(1)} all-to-all(bf16[8,136,128]{2,1,0:T(8,128)(2,1)S(1)} %broadcast_in_dim.2), channel_id=1, replica_groups=mesh['y'=4,'x_hi'=2,'core'=2,'z'=8,'x_lo'=2] {'z'}, dimensions={0} | all-to-all | bytes 557056 | tf_op jit(solution)/shard_map/all_to_all | solution.py:410
  108.7 1.5 collective-permute-start.13
  110.3 2.8 %collective-permute-done.13 = bf16[136,128]{1,0:T(8,128)(2,1)S(1)} collective-permute-done((bf16[136,128]{1,0:T(8,128)(2,1)S(1)}, bf16[136,128]{1,0:T(8,128)(2,1)S(1)}, u32[]{:S(2)}, u32[]{:S(2)}) %collective-permute-start.13) | collective-permute-done | bytes 34848 | tf_op jit(solution)/shard_map/ppermute | solution.py:395
  113.6 3.4 %collective-permute-start.5 = (bf16[192,256]{1,0:T(8,128)(2,1)S(1)}, bf16[192,256]{1,0:T(8,128)(2,1)S(1)}, u32[]{:S(2)}, u32[]{:S(2)}) collective-permute-start(bf16[192,256]{1,0:T(8,128)(2,1)S(1)} %get-tuple-element.33), channel_id=1, source_target_pairs={{1,2},{3,4},{5,6},{7,8},{9,10},{11,12},{13,14},{2,1},{4,3},{6,5},{... | collective-permute-start | bytes 294920 | tf_op jit(solution)/shard_map/ppermute | solution.py:350
  117.2 2.7 %collective-permute-done.5 = bf16[192,256]{1,0:T(8,128)(2,1)S(1)} collective-permute-done((bf16[192,256]{1,0:T(8,128)(2,1)S(1)}, bf16[192,256]{1,0:T(8,128)(2,1)S(1)}, u32[]{:S(2)}, u32[]{:S(2)}) %collective-permute-start.5) | collective-permute-done | bytes 98336 | tf_op jit(solution)/shard_map/ppermute | solution.py:350
  119.9 2.4 %collective-permute-done.15 = bf16[544,128]{1,0:T(8,128)(2,1)S(1)} collective-permute-done((bf16[544,128]{1,0:T(8,128)(2,1)S(1)}, bf16[544,128]{1,0:T(8,128)(2,1)S(1)}, u32[]{:S(2)}, u32[]{:S(2)}) %collective-permute-start.15) | collective-permute-done | bytes 139296 | tf_op jit(solution)/shard_map/ppermute | solution.py:395
  122.5 6.7 %collective-permute-done.16 = bf16[1088,128]{1,0:T(8,128)(2,1)S(1)} collective-permute-done((bf16[1088,128]{1,0:T(8,128)(2,1)S(1)}, bf16[1088,128]{1,0:T(8,128)(2,1)S(1)}, u32[]{:S(2)}, u32[]{:S(2)}) %collective-permute-start.16) | collective-permute-done | bytes 278560 | tf_op jit(solution)/shard_map/ppermute | solution.py:395
  129.4 8.2 %collective-permute-start.17 = (bf16[2176,128]{1,0:T(8,128)(2,1)S(1)}, bf16[2176,128]{1,0:T(8,128)(2,1)S(1)}, u32[]{:S(2)}, u32[]{:S(2)}) collective-permute-start(bf16[2176,128]{1,0:T(8,128)(2,1)S(1)} %pad_maximum_fusion.2), channel_id=1, source_target_pairs={{0,16},{1,17},{2,18},{3,19},{4,20},{5,21},{6,22},{7,23},{8,24},{9,... | collective-permute-start | bytes 1671176 | tf_op jit(solution)/shard_map/ppermute | solution.py:395
  137.7 2.2 %collective-permute-start.7 = (bf16[176,256]{1,0:T(8,128)(2,1)S(1)}, bf16[176,256]{1,0:T(8,128)(2,1)S(1)}, u32[]{:S(2)}, u32[]{:S(2)}) collective-permute-start(bf16[176,256]{1,0:T(8,128)(2,1)S(1)} %get-tuple-element.36), channel_id=1, source_target_pairs={{16,32},{48,64},{80,96},{112,128},{144,160},{176,192},{208,224},{3... | collective-permute-start | bytes 270344 | tf_op jit(solution)/shard_map/ppermute | solution.py:350
  140.0 6.6 %collective-permute-done.7 = bf16[176,256]{1,0:T(8,128)(2,1)S(1)} collective-permute-done((bf16[176,256]{1,0:T(8,128)(2,1)S(1)}, bf16[176,256]{1,0:T(8,128)(2,1)S(1)}, u32[]{:S(2)}, u32[]{:S(2)}) %collective-permute-start.7) | collective-permute-done | bytes 90144 | tf_op jit(solution)/shard_map/ppermute | solution.py:350
  147.3 10.5 %input_grad.3 = bf16[64,48,128]{2,1,0:T(8,128)(2,1)} custom-call(bf16[64,48,256]{2,1,0:T(8,128)(2,1)} %get-tuple-element.11.g_ref, bf16[176,256]{1,0:T(8,128)(2,1)} %get-tuple-element.41.top, bf16[176,256]{1,0:T(8,128)(2,1)} %get-tuple-element.40.bottom, bf16[192,256]{1,0:T(8,128)(2,1)} %copy-done.1, bf16[192,256]{1,0:T(8,128)(2,1)} %copy-done.2, ...), custom_call_target="tpu_custom_call" | custom-call | bytes 25830000 | tf_op jit(solution)/shard_map/input_grad/pallas_call | solution.py:323
  157.7 10.5 %input_grad.2 = bf16[64,48,128]{2,1,0:T(8,128)(2,1)} custom-call(bf16[64,48,256]{2,1,0:T(8,128)(2,1)} %get-tuple-element.11.g_ref, bf16[176,256]{1,0:T(8,128)(2,1)} %get-tuple-element.41.top, bf16[176,256]{1,0:T(8,128)(2,1)} %get-tuple-element.40.bottom, bf16[192,256]{1,0:T(8,128)(2,1)} %copy-done.1, bf16[192,256]{1,0:T(8,128)(2,1)} %copy-done.2, ...), custom_call_target="tpu_custom_call" | custom-call | bytes 25830000 | tf_op jit(solution)/shard_map/input_grad/pallas_call | solution.py:323
  168.3 2.4 %pad_maximum_fusion = bf16[64,48,256]{2,1,0:T(8,128)(2,1)} fusion(bf16[64,48,128]{2,1,0:T(8,128)(2,1)S(1)} %copy-done, bf16[64,48,128]{2,1,0:T(8,128)(2,1)} %input_grad.2), kind=kLoop, calls=%fused_computation | loop fusion | flops 3145728 | bytes 3145728 | tf_op jit(solution)/shard_map/concatenate | solution.py:440
  172.0 0.8 copy.23
  172.8 1.0 copy.30
  173.9 1.1 copy.31
  (73 shorter events, 5.0 us)
Async XLA Ops:
  1.9 6.3 %collective-permute-start.1 = (bf16[192,256]{1,0:T(8,128)(2,1)S(1)}, bf16[192,256]{1,0:T(8,128)(2,1)S(1)}, u32[]{:S(2)}, u32[]{:S(2)}) collective-permute-start(bf16[192,256]{1,0:T(8,128)(2,1)S(1)} %select_n.290), channel_id=1, source_target_pairs={{1,2},{3,4},{5,6},{7,8},{9,10},{11,12},{13,14},{2,1},{4,3},{6,5},{... | collective-permute-start | bytes 294920 | tf_op jit(solution)/shard_map/ppermute | solution.py:350
  5.8 5.5 %collective-permute-start = (bf16[192,256]{1,0:T(8,128)(2,1)S(1)}, bf16[192,256]{1,0:T(8,128)(2,1)S(1)}, u32[]{:S(2)}, u32[]{:S(2)}) collective-permute-start(bf16[192,256]{1,0:T(8,128)(2,1)S(1)} %select_n.288), channel_id=1, source_target_pairs={{0,1},{2,3},{4,5},{6,7},{8,9},{10,11},{12,13},{14,15},{1,0},{3,2},... | collective-permute-start | bytes 294920 | tf_op jit(solution)/shard_map/ppermute | solution.py:350
  11.3 9.8 %copy-start.3 = (bf16[192,256]{1,0:T(8,128)(2,1)}, bf16[192,256]{1,0:T(8,128)(2,1)S(1)}, u32[]{:S(2)}) copy-start(bf16[192,256]{1,0:T(8,128)(2,1)S(1)} %get-tuple-element.34.left) | copy-start | bytes 294916
  11.3 9.8 %copy-start.4 = (bf16[192,256]{1,0:T(8,128)(2,1)}, bf16[192,256]{1,0:T(8,128)(2,1)S(1)}, u32[]{:S(2)}) copy-start(bf16[192,256]{1,0:T(8,128)(2,1)S(1)} %get-tuple-element.35.right) | copy-start | bytes 294916
  11.5 9.0 %collective-permute-start.3 = (bf16[176,256]{1,0:T(8,128)(2,1)S(1)}, bf16[176,256]{1,0:T(8,128)(2,1)S(1)}, u32[]{:S(2)}, u32[]{:S(2)}) collective-permute-start(bf16[176,256]{1,0:T(8,128)(2,1)S(1)} %get-tuple-element.38), channel_id=1, source_target_pairs={{16,32},{48,64},{80,96},{112,128},{144,160},{176,192},{208,224},{3... | collective-permute-start | bytes 270344 | tf_op jit(solution)/shard_map/ppermute | solution.py:350
  16.2 4.3 %collective-permute-start.2 = (bf16[176,256]{1,0:T(8,128)(2,1)S(1)}, bf16[176,256]{1,0:T(8,128)(2,1)S(1)}, u32[]{:S(2)}, u32[]{:S(2)}) collective-permute-start(bf16[176,256]{1,0:T(8,128)(2,1)S(1)} %get-tuple-element.39), channel_id=1, source_target_pairs={{0,16},{32,48},{64,80},{96,112},{128,144},{160,176},{192,208},{224... | collective-permute-start | bytes 270344 | tf_op jit(solution)/shard_map/ppermute | solution.py:350
  65.8 2.3 %collective-permute-start.8 = (bf16[2176,128]{1,0:T(8,128)(2,1)}, bf16[2176,128]{1,0:T(8,128)(2,1)S(1)}, u32[]{:S(2)}, u32[]{:S(2)}) collective-permute-start(bf16[2176,128]{1,0:T(8,128)(2,1)} %get-tuple-element.17), channel_id=1, source_target_pairs={{0,16},{1,17},{2,18},{3,19},{4,20},{5,21},{6,22},{7,23},{8,24},{9,... | collective-permute-start | bytes 1671176 | tf_op jit(solution)/shard_map/ppermute | solution.py:395
  69.5 8.2 %collective-permute-start.9 = (bf16[1088,128]{1,0:T(8,128)(2,1)S(1)}, bf16[1088,128]{1,0:T(8,128)(2,1)S(1)}, u32[]{:S(2)}, u32[]{:S(2)}) collective-permute-start(bf16[1088,128]{1,0:T(8,128)(2,1)S(1)} %select_convert_fusion), channel_id=1, source_target_pairs={{0,1},{1,0},{2,3},{3,2},{4,5},{5,4},{6,7},{7,6},{8,9},{9,8},{10,11... | collective-permute-start | bytes 835592 | tf_op jit(solution)/shard_map/ppermute | solution.py:395
  77.7 5.5 %collective-permute-start.10 = (bf16[544,128]{1,0:T(8,128)(2,1)S(1)}, bf16[544,128]{1,0:T(8,128)(2,1)S(1)}, u32[]{:S(2)}, u32[]{:S(2)}) collective-permute-start(bf16[544,128]{1,0:T(8,128)(2,1)S(1)} %select_convert_fusion.1), channel_id=1, source_target_pairs={{0,33},{1,32},{2,35},{3,34},{4,37},{5,36},{6,39},{7,38},{8,41},{9,... | collective-permute-start | bytes 417800 | tf_op jit(solution)/shard_map/ppermute | solution.py:395
  83.3 3.2 %collective-permute-start.11 = (bf16[272,128]{1,0:T(8,128)(2,1)S(1)}, bf16[272,128]{1,0:T(8,128)(2,1)S(1)}, u32[]{:S(2)}, u32[]{:S(2)}) collective-permute-start(bf16[272,128]{1,0:T(8,128)(2,1)S(1)} %select_convert_fusion.2), channel_id=1, source_target_pairs={{0,64},{1,65},{2,66},{3,67},{4,68},{5,69},{6,70},{7,71},{8,72},{9,... | collective-permute-start | bytes 208904 | tf_op jit(solution)/shard_map/ppermute | solution.py:395
  84.7 28.7 %copy-start.5 = (bf16[192,256]{1,0:T(8,128)(2,1)S(1)}, bf16[192,256]{1,0:T(8,128)(2,1)}, u32[]{:S(2)}) copy-start(bf16[192,256]{1,0:T(8,128)(2,1)} %get-tuple-element.13) | copy-start | bytes 294916
  84.7 28.7 %copy-start.6 = (bf16[192,256]{1,0:T(8,128)(2,1)S(1)}, bf16[192,256]{1,0:T(8,128)(2,1)}, u32[]{:S(2)}) copy-start(bf16[192,256]{1,0:T(8,128)(2,1)} %get-tuple-element.14) | copy-start | bytes 294916
  86.6 4.1 %collective-permute-start.12 = (bf16[136,128]{1,0:T(8,128)(2,1)S(1)}, bf16[136,128]{1,0:T(8,128)(2,1)S(1)}, u32[]{:S(2)}, u32[]{:S(2)}) collective-permute-start(bf16[136,128]{1,0:T(8,128)(2,1)S(1)} %select_convert_fusion.3), channel_id=1, source_target_pairs={{0,192},{1,193},{2,194},{3,195},{4,196},{5,197},{6,198},{7,199},{8... | collective-permute-start | bytes 104456 | tf_op jit(solution)/shard_map/ppermute | solution.py:395
  108.7 4.4 %collective-permute-start.13 = (bf16[136,128]{1,0:T(8,128)(2,1)S(1)}, bf16[136,128]{1,0:T(8,128)(2,1)S(1)}, u32[]{:S(2)}, u32[]{:S(2)}) collective-permute-start(bf16[136,128]{1,0:T(8,128)(2,1)S(1)} %reduce_sum.12), channel_id=1, source_target_pairs={{0,192},{1,193},{2,194},{3,195},{4,196},{5,197},{6,198},{7,199},{8... | collective-permute-start | bytes 104456 | tf_op jit(solution)/shard_map/ppermute | solution.py:395
  113.2 3.8 %collective-permute-start.14 = (bf16[272,128]{1,0:T(8,128)(2,1)S(1)}, bf16[272,128]{1,0:T(8,128)(2,1)S(1)}, u32[]{:S(2)}, u32[]{:S(2)}) collective-permute-start(bf16[272,128]{1,0:T(8,128)(2,1)S(1)} %pad_maximum_fusion.5), channel_id=1, source_target_pairs={{0,64},{1,65},{2,66},{3,67},{4,68},{5,69},{6,70},{7,71},{8,72},{9,... | collective-permute-start | bytes 208904 | tf_op jit(solution)/shard_map/ppermute | solution.py:395
  113.5 3.7 %collective-permute-start.4 = (bf16[192,256]{1,0:T(8,128)(2,1)S(1)}, bf16[192,256]{1,0:T(8,128)(2,1)S(1)}, u32[]{:S(2)}, u32[]{:S(2)}) collective-permute-start(bf16[192,256]{1,0:T(8,128)(2,1)S(1)} %get-tuple-element.32), channel_id=1, source_target_pairs={{0,1},{2,3},{4,5},{6,7},{8,9},{10,11},{12,13},{14,15},{1,0},{3,2},... | collective-permute-start | bytes 294920 | tf_op jit(solution)/shard_map/ppermute | solution.py:350
  113.6 6.3 %collective-permute-start.5 = (bf16[192,256]{1,0:T(8,128)(2,1)S(1)}, bf16[192,256]{1,0:T(8,128)(2,1)S(1)}, u32[]{:S(2)}, u32[]{:S(2)}) collective-permute-start(bf16[192,256]{1,0:T(8,128)(2,1)S(1)} %get-tuple-element.33), channel_id=1, source_target_pairs={{1,2},{3,4},{5,6},{7,8},{9,10},{11,12},{13,14},{2,1},{4,3},{6,5},{... | collective-permute-start | bytes 294920 | tf_op jit(solution)/shard_map/ppermute | solution.py:350
  117.1 5.2 %collective-permute-start.15 = (bf16[544,128]{1,0:T(8,128)(2,1)S(1)}, bf16[544,128]{1,0:T(8,128)(2,1)S(1)}, u32[]{:S(2)}, u32[]{:S(2)}) collective-permute-start(bf16[544,128]{1,0:T(8,128)(2,1)S(1)} %pad_maximum_fusion.4), channel_id=1, source_target_pairs={{0,33},{1,32},{2,35},{3,34},{4,37},{5,36},{6,39},{7,38},{8,41},{9,... | collective-permute-start | bytes 417800 | tf_op jit(solution)/shard_map/ppermute | solution.py:395
  119.9 9.4 %copy-start.1 = (bf16[192,256]{1,0:T(8,128)(2,1)}, bf16[192,256]{1,0:T(8,128)(2,1)S(1)}, u32[]{:S(2)}) copy-start(bf16[192,256]{1,0:T(8,128)(2,1)S(1)} %get-tuple-element.30.left) | copy-start | bytes 294916
  119.9 9.4 %copy-start.2 = (bf16[192,256]{1,0:T(8,128)(2,1)}, bf16[192,256]{1,0:T(8,128)(2,1)S(1)}, u32[]{:S(2)}) copy-start(bf16[192,256]{1,0:T(8,128)(2,1)S(1)} %get-tuple-element.31.right) | copy-start | bytes 294916
  122.3 6.8 %collective-permute-start.16 = (bf16[1088,128]{1,0:T(8,128)(2,1)S(1)}, bf16[1088,128]{1,0:T(8,128)(2,1)S(1)}, u32[]{:S(2)}, u32[]{:S(2)}) collective-permute-start(bf16[1088,128]{1,0:T(8,128)(2,1)S(1)} %pad_maximum_fusion.3), channel_id=1, source_target_pairs={{0,1},{1,0},{2,3},{3,2},{4,5},{5,4},{6,7},{7,6},{8,9},{9,8},{10,11... | collective-permute-start | bytes 835592 | tf_op jit(solution)/shard_map/ppermute | solution.py:395
  122.5 15.1 %copy-start.7 = (bf16[144,256]{1,0:T(8,128)(2,1)S(1)}, bf16[144,256]{1,0:T(8,128)(2,1)}, u32[]{:S(2)}) copy-start(bf16[144,256]{1,0:T(8,128)(2,1)} %get-tuple-element.12) | copy-start | bytes 221188
  122.5 15.1 %copy-start.8 = (bf16[144,256]{1,0:T(8,128)(2,1)S(1)}, bf16[144,256]{1,0:T(8,128)(2,1)}, u32[]{:S(2)}) copy-start(bf16[144,256]{1,0:T(8,128)(2,1)} %get-tuple-element.15) | copy-start | bytes 221188
  129.4 41.3 %collective-permute-start.17 = (bf16[2176,128]{1,0:T(8,128)(2,1)S(1)}, bf16[2176,128]{1,0:T(8,128)(2,1)S(1)}, u32[]{:S(2)}, u32[]{:S(2)}) collective-permute-start(bf16[2176,128]{1,0:T(8,128)(2,1)S(1)} %pad_maximum_fusion.2), channel_id=1, source_target_pairs={{0,16},{1,17},{2,18},{3,19},{4,20},{5,21},{6,22},{7,23},{8,24},{9,... | collective-permute-start | bytes 1671176 | tf_op jit(solution)/shard_map/ppermute | solution.py:395
  137.7 8.9 %collective-permute-start.7 = (bf16[176,256]{1,0:T(8,128)(2,1)S(1)}, bf16[176,256]{1,0:T(8,128)(2,1)S(1)}, u32[]{:S(2)}, u32[]{:S(2)}) collective-permute-start(bf16[176,256]{1,0:T(8,128)(2,1)S(1)} %get-tuple-element.36), channel_id=1, source_target_pairs={{16,32},{48,64},{80,96},{112,128},{144,160},{176,192},{208,224},{3... | collective-permute-start | bytes 270344 | tf_op jit(solution)/shard_map/ppermute | solution.py:350
  139.9 6.7 %collective-permute-start.6 = (bf16[176,256]{1,0:T(8,128)(2,1)S(1)}, bf16[176,256]{1,0:T(8,128)(2,1)S(1)}, u32[]{:S(2)}, u32[]{:S(2)}) collective-permute-start(bf16[176,256]{1,0:T(8,128)(2,1)S(1)} %get-tuple-element.37), channel_id=1, source_target_pairs={{0,16},{32,48},{64,80},{96,112},{128,144},{160,176},{192,208},{224... | collective-permute-start | bytes 270344 | tf_op jit(solution)/shard_map/ppermute | solution.py:350
  157.7 10.5 %copy-start = (bf16[64,48,128]{2,1,0:T(8,128)(2,1)S(1)}, bf16[64,48,128]{2,1,0:T(8,128)(2,1)}, u32[]{:S(2)}) copy-start(bf16[64,48,128]{2,1,0:T(8,128)(2,1)} %input_grad.3) | copy-start | bytes 2359300

commit v5 on v4

--- a/solution.py
+++ b/solution.py
@@ -1,3 +1,4 @@
+import functools
 import math
 
 import jax
@@ -15,9 +16,9 @@
 RG = 8
 CB = 3
 TAPS = 64
+PART = 16
 EXTRA = 32
 VMEM = pl.BlockSpec(memory_space=pltpu.VMEM)
-PARAMS = dict(vmem_limit_bytes=56 << 20)
 
 
 def nn(a, b):
@@ -39,34 +40,48 @@
             wide[k, t] = jnp.broadcast_to(w_ref[s : s + 1, half(h)], (8, LANES))
 
 
-def fill(pad, core, top, bottom, left, right, halves=(0, 1)):
+def fill(pad, core, top, bottom, left, right, base=0, count=None):
     rows, cols = core.shape[0], core.shape[1]
+    count = rows if count is None else count
     ends = (5, 8 + cols)
-    for k, h in enumerate(halves):
+    first, stop = max(base - 3, 0), min(base + count + 3, rows)
+    edges = []
+    if base == 0:
+        edges.append((0, top))
+    if base + count == rows:
+        edges.append((3 + count, bottom))
+    for h in range(2):
 
         def put(i, _):
-            pad[k, 3 + i, 8 : 8 + cols, :] = core[i, :, half(h)].astype(F32)
+            pad[h, i - base + 3, 8 : 8 + cols, :] = core[i, :, half(h)].astype(F32)
             return 0
 
-        lax.fori_loop(0, rows, put, 0, unroll=4)
-        for first, flat in ((0, top), (3 + rows, bottom)):
+        lax.fori_loop(first, stop, put, 0, unroll=4 if (stop - first) % 4 == 0 else 1)
+        for at, flat in edges:
             extra = flat[3 * cols : 3 * cols + 24, half(h)].astype(F32)
             for i in range(3):
-                at = slice(i * cols, (i + 1) * cols)
-                pad[k, first + i, 8 : 8 + cols, :] = flat[at, half(h)].astype(F32)
+                line = flat[i * cols : (i + 1) * cols, half(h)].astype(F32)
+                pad[h, at + i, 8 : 8 + cols, :] = line
                 for n, end in enumerate(ends):
                     corner = extra[n * 9 + i * 3 : n * 9 + i * 3 + 3]
-                    pad[k, first + i, end : end + 3, :] = corner
-
-        def side(i, _):
-            at = pl.ds(pl.multiple_of(i * 24, 8), 24)
+                    pad[h, at + i, end : end + 3, :] = corner
+
+        def side(start, lines):
+            at = pl.ds(pl.multiple_of(start * 3, 8), 24)
             for end, flat in zip(ends, (left, right)):
                 v = flat[at, half(h)].astype(F32)
-                for r in range(8):
-                    pad[k, 3 + i * 8 + r, end : end + 3, :] = v[r * 3 : r * 3 + 3]
+                for r in lines:
+                    pad[h, 3 - base + start + r, end : end + 3, :] = v[r * 3 : r * 3 + 3]
+
+        def eight(i, _):
+            side(base + i * 8, range(8))
             return 0
 
-        lax.fori_loop(0, rows // 8, side, 0)
+        lax.fori_loop(0, count // 8, eight, 0)
+        if first < base:
+            side(base - 8, range(8 - (base - first), 8))
+        if stop > base + count:
+            side(base + count, range(stop - base - count))
 
 
 def stencil(pad, wide, h, row, col):
@@ -186,7 +201,7 @@
         second = jnp.sum(d * nhat, axis=-1, keepdims=True) * (1.0 / chans)
         rstd = rstd_ref[at, :]
         g = (jnp.concatenate([rstd, rstd], axis=1) * (d - first - nhat * second)).astype(BF16)
-        g_ref[i] = g
+        g_ref[step * rows + i] = g
         for h in range(2):
             gpad[h, step * rows + i + 3] = g[:, half(h)].astype(F32)
         return 0
@@ -237,16 +252,12 @@
     hidden = we.shape[1]
     pix = TILE * cols
     block = pl.BlockSpec((TILE, cols, chans), lambda s, t, u: (s, 0, 0))
-    whole = lambda *shape: pl.BlockSpec(shape, lambda s, t, u: (0, 0))
     size = (2 * chans + EXTRA) * (hidden // LANES) // 2
     grid = pltpu.PrefetchScalarGridSpec(
         num_scalar_prefetch=2,
         grid=(rows // TILE,),
         in_specs=[VMEM] * 5 + [block] + [VMEM] * 8,
-        out_specs=[block]
-        + [whole(3 * rows, chans)] * 2
-        + [whole(3 * cols, chans)] * 2
-        + [whole(size, LANES)] * 2,
+        out_specs=[VMEM] * 7,
         scratch_shapes=[
             pltpu.VMEM((2 * TAPS, LANES), F32),
             pltpu.VMEM((2 * chans, hidden), F32),
@@ -277,7 +288,7 @@
             jax.ShapeDtypeStruct((size, LANES), F32),
             jax.ShapeDtypeStruct((size, LANES), BF16),
         ),
-        compiler_params=pltpu.CompilerParams(**PARAMS),
+        compiler_params=pltpu.CompilerParams(vmem_limit_bytes=40 << 20),
         cost_estimate=cost(42),
         name="branch",
     )(tissue, upper, x, *halo, cot, w, bias, gain, shift, we, be, wr, scale)
@@ -287,56 +298,103 @@
     return pl.CostEstimate(flops=0, transcendentals=0, bytes_accessed=int(us * 3.69e6))
 
 
-def input_kernel(g_ref, top, bottom, left, right, cot, w_ref, o_ref, pad, wide, out):
-    step = pl.program_id(0)
-    rows, cols, _ = cot.shape
-
-    @pl.when(step == 0)
-    def _():
-        spread_weights(w_ref, wide, True, (0,))
-        fill(pad, g_ref, top, bottom, left, right, (0,))
-
+def input_kernel(part, g_ref, top, bottom, left, right, cot, w_ref, *rest):
+    o_ref, pad, wide, out = rest[-4:]
+    rows, cols, _ = out.shape
+    base = part * rows
+    spread_weights(w_ref, wide, True)
+    fill(pad, g_ref, top, bottom, left, right, base, rows)
     ng = cols // (8 * CB)
-
-    def conv(n, _):
-        row, col = (n // ng) * RG, (n % ng) * (8 * CB)
-        acc = stencil(pad, wide, 0, step * rows + row, col)
-        for i in range(RG):
-            for c in range(CB):
-                at = pl.ds(pl.multiple_of(col + c * 8, 8), 8)
-                out[row + i, at, :] = acc[i][c]
+    for h in range(2):
+
+        def conv(n, _):
+            row, col = (n // ng) * RG, (n % ng) * (8 * CB)
+            acc = stencil(pad, wide, h, row, col)
+            for i in range(RG):
+                for c in range(CB):
+                    at = pl.ds(pl.multiple_of(col + c * 8, 8), 8)
+                    out[row + i, at, half(h)] = acc[i][c]
+            return 0
+
+        lax.fori_loop(0, (rows // RG) * ng, conv, 0)
+
+    def last(i, _):
+        o_ref[i] = (cot[base + i].astype(F32) + out[i]).astype(BF16)
         return 0
 
-    lax.fori_loop(0, (rows // RG) * ng, conv, 0)
-
-    def last(i, _):
-        o_ref[i] = (cot[i].astype(F32) + out[i]).astype(BF16)
-        return 0
-
     lax.fori_loop(0, rows, last, 0, unroll=4)
 
 
-def input_grad(g, halo, cot, w, h):
-    rows, cols, _ = g.shape
-    flat = lambda a: pl.BlockSpec((a.shape[0], LANES), lambda s, h=h: (0, h))
-    block = pl.BlockSpec((TILE, cols, LANES), lambda s, h=h: (s, 0, h))
+def input_grad(g, halo, cot, w, so_far, part):
+    _, cols, chans = g.shape
+    arrays = (g, *halo, cot, w)
+    specs = [VMEM] * len(arrays)
+    alias = {}
+    if so_far is not None:
+        alias = {len(arrays): 0}
+        arrays += (so_far,)
+        specs.append(pl.BlockSpec(memory_space=pl.ANY))
     return pl.pallas_call(
-        input_kernel,
-        grid=(rows // TILE,),
-        out_shape=jax.ShapeDtypeStruct((rows, cols, LANES), BF16),
-        in_specs=[pl.BlockSpec((rows, cols, LANES), lambda s, h=h: (0, 0, h))]
-        + [flat(a) for a in halo]
-        + [block, flat(w)],
-        out_specs=pl.BlockSpec((TILE, cols, LANES), lambda s: (s, 0, 0)),
+        functools.partial(input_kernel, part),
+        grid=(1,),
+        out_shape=jax.ShapeDtypeStruct(g.shape, BF16),
+        in_specs=specs,
+        out_specs=pl.BlockSpec((PART, cols, chans), lambda s: (part, 0, 0)),
         scratch_shapes=[
-            pltpu.VMEM((1, rows + 6, cols + 16, LANES), F32),
-            pltpu.VMEM((1, 49, 8, LANES), F32),
-            pltpu.VMEM((TILE, cols, LANES), F32),
+            pltpu.VMEM((2, PART + 6, cols + 16, LANES), F32),
+            pltpu.VMEM((2, 49, 8, LANES), F32),
+            pltpu.VMEM((PART, cols, chans), F32),
         ],
-        compiler_params=pltpu.CompilerParams(**PARAMS),
-        cost_estimate=cost(7),
+        input_output_aliases=alias,
+        compiler_params=pltpu.CompilerParams(vmem_limit_bytes=16 << 20),
+        cost_estimate=cost(4),
         name="input_grad",
-    )(g, *halo, cot, w)
+    )(*arrays)
+
+
+def spread_kernel(upper, mine, other, taps_ref, expand, reduce, *, factor):
+    chans = expand.shape[0]
+    blocks = expand.shape[1] // LANES
+    size = 2 * chans + EXTRA
+    count = 2 * TAPS // blocks
+    for e in range(blocks):
+        at = pl.ds((e % (blocks // 2)) * size, size)
+        here = upper[0] == e // (blocks // 2)
+
+        def write(flat, e=e, at=at):
+            v = flat[at, :].astype(F32) * factor
+            expand[:, half(e)] = v[:chans]
+            for h in range(2):
+                reduce[half(e), half(h)] = v[chans + h * LANES : chans + (h + 1) * LANES]
+            h, first = e * count // TAPS, e * count % TAPS
+            taps_ref[first : first + count, half(h)] = v[2 * chans : 2 * chans + count]
+
+        pl.when(here)(functools.partial(write, mine))
+        pl.when(jnp.logical_not(here))(functools.partial(write, other))
+
+
+def spread(upper, mine, other, chans, hidden, factor):
+    grid = pltpu.PrefetchScalarGridSpec(
+        num_scalar_prefetch=1,
+        grid=(1,),
+        in_specs=[VMEM] * 2,
+        out_specs=[
+            pl.BlockSpec(shape, lambda s, u: (0, 0))
+            for shape in ((TAPS, chans), (chans, hidden), (hidden, chans))
+        ],
+    )
+    return pl.pallas_call(
+        functools.partial(spread_kernel, factor=factor),
+        grid_spec=grid,
+        out_shape=(
+            jax.ShapeDtypeStruct((TAPS, chans), F32),
+            jax.ShapeDtypeStruct((chans, hidden), F32),
+            jax.ShapeDtypeStruct((hidden, chans), F32),
+        ),
+        compiler_params=pltpu.CompilerParams(vmem_limit_bytes=12 << 20),
+        cost_estimate=cost(2),
+        name="spread",
+    )(upper, mine, other)
 
 
 AXES = ("y", "x_hi", "core", "z", "x_lo")
@@ -412,8 +470,9 @@
     for name in reversed(names):
         upper = keeps_upper(name) == 1
         other = swap(out, name)
+        if name == "core":
+            return out, other
         out = jnp.concatenate([jnp.where(upper, other, out), jnp.where(upper, out, other)])
-    return out
 
 
 def body(x, cot, tissue, w, bias, gain, shift, we, be, wr, scale):
@@ -427,17 +486,12 @@
     rest = (w, line(bias), line(gain), line(shift), we, line(be), wr, line(scale))
     g, *edges, kept, sent = branch(x, halo, cot, tissue, upper, *rest)
     ghalo = halo_of(*edges)
-    result = []
-    for h in range(2):
-        result.append(input_grad(g, ghalo, cot, w, h))
-    out = total(kept, sent).reshape(-1, 2 * chans + EXTRA, LANES)
-    expand = out[:, :chans].transpose(1, 0, 2).reshape(chans, -1)
-    reduce = out[:, chans : 2 * chans].reshape(-1, 2, LANES, LANES)
-    reduce = reduce.transpose(0, 2, 1, 3).reshape(-1, chans)
-    taps = out[:, 2 * chans : 2 * chans + 2 * TAPS // out.shape[0]].reshape(2, TAPS, LANES)
-    taps = taps.transpose(1, 0, 2).reshape(TAPS, chans)[: w.shape[0]]
-    scaled = [v.astype(F32) * factor for v in (taps, expand, reduce)]
-    return (jnp.concatenate(result, axis=2), *scaled)
+    result = None
+    for part in range(rows // PART):
+        result = input_grad(g, ghalo, cot, w, result, part)
+    mine, other = total(kept, sent)
+    taps, expand, reduce = spread(upper, mine, other, chans, we.shape[1], factor)
+    return result, taps[: w.shape[0]], expand, reduce
 
 
 def solution(mesh):

time: 175 us -> 176 us (level)
  the two profiles are of different devices: /device:TPU:7 before, /device:TPU:1 now
where the time goes in v5:
time: 176 us; the launch traced here: 175 us
  Pallas kernels  59.1 us (34%)
  starting transfers between devices  38.9 us (22%)
  waiting for transfers between devices  36.9 us (21%)
  blocking collectives  19.4 us (11%)
  local copies, waits for them, and re-layouts  10.8 us (6%)
  other arithmetic  9.24 us (5%)
    pallas_call x1, Pallas kernels, branch(): pl.pallas_call(branch_kernel, grid_spec=grid, out_shape=(jax.ShapeDtypeSt...  42.3 us
    ppermute x10, waiting for transfers between devices, swap(): return lax.ppermute(value, AXES, pairs)  29.3 us
    ppermute x10, starting transfers between devices, swap(): return lax.ppermute(value, AXES, pairs)  26.6 us
    all_to_all x1, blocking collectives, total(): copies = lax.all_to_all(copies, 'z', 0, 0, tiled=True)  19.4 us
    pallas_call x4, Pallas kernels, input_grad(): pl.pallas_call(functools.partial(input_kernel, part), grid=(1,), out_shap...  15.2 us
    ppermute x8, starting transfers between devices, beside(): return lax.ppermute(value, axes, pairs + [(b, a) for a, b in pairs])  12.4 us
    unnamed x42, local copies, waits for them, and re-layouts  8.92 us
    ppermute x8, waiting for transfers between devices, beside(): return lax.ppermute(value, axes, pairs + [(b, a) for a, b in pairs])  7.54 us
  transfers between devices with their start and end apart: 18, of which 12 were waited for; matrix products, arithmetic and copies ran while one was open for 1% of the time, Pallas kernels for 9%

profile of v5, /device:TPU:1, one launch (start us, length us, event | category | flops | bytes accessed | tf_op | source)
XLA Modules:
  0.0 175.4 jit_solution(12013985251690066892)
XLA Ops:
  0.6 1.2 broadcast_select_fusion.5
  2.0 2.1 %collective-permute-start = (bf16[192,256]{1,0:T(8,128)(2,1)S(1)}, bf16[192,256]{1,0:T(8,128)(2,1)S(1)}, u32[]{:S(2)}, u32[]{:S(2)}) collective-permute-start(bf16[192,256]{1,0:T(8,128)(2,1)S(1)} %select_n.271), channel_id=1, source_target_pairs={{0,1},{2,3},{4,5},{6,7},{8,9},{10,11},{12,13},{14,15},{1,0},{3,2},... | collective-permute-start | bytes 294920 | tf_op jit(solution)/shard_map/ppermute | solution.py:408
  6.3 6.6 %collective-permute-start.3 = (bf16[176,256]{1,0:T(8,128)(2,1)S(1)}, bf16[176,256]{1,0:T(8,128)(2,1)S(1)}, u32[]{:S(2)}, u32[]{:S(2)}) collective-permute-start(bf16[176,256]{1,0:T(8,128)(2,1)S(1)} %get-tuple-element.40), channel_id=1, source_target_pairs={{16,32},{48,64},{80,96},{112,128},{144,160},{176,192},{208,224},{3... | collective-permute-start | bytes 270344 | tf_op jit(solution)/shard_map/ppermute | solution.py:408
  13.0 2.1 %collective-permute-done.3 = bf16[176,256]{1,0:T(8,128)(2,1)S(1)} collective-permute-done((bf16[176,256]{1,0:T(8,128)(2,1)S(1)}, bf16[176,256]{1,0:T(8,128)(2,1)S(1)}, u32[]{:S(2)}, u32[]{:S(2)}) %collective-permute-start.3) | collective-permute-done | bytes 90144 | tf_op jit(solution)/shard_map/ppermute | solution.py:408
  15.3 1.4 copy-done.1
  18.7 42.3 %branch.1 = (bf16[64,48,256]{2,1,0:T(8,128)(2,1)S(1)}, bf16[192,256]{1,0:T(8,128)(2,1)S(1)}, bf16[192,256]{1,0:T(8,128)(2,1)S(1)}, bf16[144,256]{1,0:T(8,128)(2,...) custom-call(s32[4,3]{1,0:T(4,128)S(1)} %copy-done.13, s32[1]{0:T(128)} %bitcast.upper, ...), custom_call_target="tpu_custom_call" | custom-call | bytes 154980000 | tf_op jit(solution)/shard_map/branch/pallas_call | solution.py:279
  64.0 2.3 %collective-permute-done.8 = bf16[2176,128]{1,0:T(8,128)(2,1)} collective-permute-done((bf16[2176,128]{1,0:T(8,128)(2,1)}, bf16[2176,128]{1,0:T(8,128)(2,1)}, u32[]{:S(2)}, u32[]{:S(2)}) %collective-permute-start.8) | collective-permute-done | bytes 557088 | tf_op jit(solution)/shard_map/ppermute | solution.py:453
  66.3 1.5 convert_add_fusion
  69.5 4.0 %collective-permute-start.9 = (bf16[1088,128]{1,0:T(8,128)(2,1)}, bf16[1088,128]{1,0:T(8,128)(2,1)}, u32[]{:S(2)}, u32[]{:S(2)}) collective-permute-start(bf16[1088,128]{1,0:T(8,128)(2,1)} %select_convert_fusion), channel_id=1, source_target_pairs={{0,1},{1,0},{2,3},{3,2},{4,5},{5,4},{6,7},{7,6},{8,9},{9,8},{10,11... | collective-permute-start | bytes 835592 | tf_op jit(solution)/shard_map/ppermute | solution.py:453
  73.5 7.2 %collective-permute-done.9 = bf16[1088,128]{1,0:T(8,128)(2,1)} collective-permute-done((bf16[1088,128]{1,0:T(8,128)(2,1)}, bf16[1088,128]{1,0:T(8,128)(2,1)}, u32[]{:S(2)}, u32[]{:S(2)}) %collective-permute-start.9) | collective-permute-done | bytes 278560 | tf_op jit(solution)/shard_map/ppermute | solution.py:453
  80.7 1.4 convert_add_fusion.1
  83.6 3.4 %collective-permute-start.10 = (bf16[544,128]{1,0:T(8,128)(2,1)}, bf16[544,128]{1,0:T(8,128)(2,1)S(1)}, u32[]{:S(2)}, u32[]{:S(2)}) collective-permute-start(bf16[544,128]{1,0:T(8,128)(2,1)} %select_convert_fusion.1), channel_id=1, source_target_pairs={{0,33},{1,32},{2,35},{3,34},{4,37},{5,36},{6,39},{7,38},{8,41},{9,... | collective-permute-start | bytes 417800 | tf_op jit(solution)/shard_map/ppermute | solution.py:453
  86.9 3.0 %collective-permute-done.10 = bf16[544,128]{1,0:T(8,128)(2,1)S(1)} collective-permute-done((bf16[544,128]{1,0:T(8,128)(2,1)}, bf16[544,128]{1,0:T(8,128)(2,1)S(1)}, u32[]{:S(2)}, u32[]{:S(2)}) %collective-permute-start.10) | collective-permute-done | bytes 139296 | tf_op jit(solution)/shard_map/ppermute | solution.py:453
  90.0 1.1 convert_add_fusion.2
  91.8 2.2 %collective-permute-start.11 = (bf16[272,128]{1,0:T(8,128)(2,1)S(1)}, bf16[272,128]{1,0:T(8,128)(2,1)S(1)}, u32[]{:S(2)}, u32[]{:S(2)}) collective-permute-start(bf16[272,128]{1,0:T(8,128)(2,1)S(1)} %select_convert_fusion.2), channel_id=1, source_target_pairs={{0,64},{1,65},{2,66},{3,67},{4,68},{5,69},{6,70},{7,71},{8,72},{9,... | collective-permute-start | bytes 208904 | tf_op jit(solution)/shard_map/ppermute | solution.py:453
  94.0 1.7 collective-permute-done.11
  96.7 3.0 %collective-permute-start.12 = (bf16[136,128]{1,0:T(8,128)(2,1)S(1)}, bf16[136,128]{1,0:T(8,128)(2,1)S(1)}, u32[]{:S(2)}, u32[]{:S(2)}) collective-permute-start(bf16[136,128]{1,0:T(8,128)(2,1)S(1)} %select_convert_fusion.3), channel_id=1, source_target_pairs={{0,192},{1,193},{2,194},{3,195},{4,196},{5,197},{6,198},{7,199},{8... | collective-permute-start | bytes 104456 | tf_op jit(solution)/shard_map/ppermute | solution.py:453
  99.7 1.3 collective-permute-done.12
  101.1 19.4 %all_to_all.5 = bf16[8,136,128]{2,1,0:T(8,128)(2,1)} all-to-all(bf16[8,136,128]{2,1,0:T(8,128)(2,1)S(1)} %broadcast_in_dim.2), channel_id=1, replica_groups=mesh['y'=4,'x_hi'=2,'core'=2,'z'=8,'x_lo'=2] {'z'}, dimensions={0} | all-to-all | bytes 557056 | tf_op jit(solution)/shard_map/all_to_all | solution.py:468
  121.5 2.8 %collective-permute-start.13 = (bf16[136,128]{1,0:T(8,128)(2,1)S(1)}, bf16[136,128]{1,0:T(8,128)(2,1)S(1)}, u32[]{:S(2)}, u32[]{:S(2)}) collective-permute-start(bf16[136,128]{1,0:T(8,128)(2,1)S(1)} %reduce_sum.12), channel_id=1, source_target_pairs={{0,192},{1,193},{2,194},{3,195},{4,196},{5,197},{6,198},{7,199},{8... | collective-permute-start | bytes 104456 | tf_op jit(solution)/shard_map/ppermute | solution.py:453
  124.3 1.7 collective-permute-done.13
  126.2 3.1 %collective-permute-done.14 = bf16[272,128]{1,0:T(8,128)(2,1)S(1)} collective-permute-done((bf16[272,128]{1,0:T(8,128)(2,1)S(1)}, bf16[272,128]{1,0:T(8,128)(2,1)S(1)}, u32[]{:S(2)}, u32[]{:S(2)}) %collective-permute-start.14) | collective-permute-done | bytes 69664 | tf_op jit(solution)/shard_map/ppermute | solution.py:453
  131.0 3.7 %collective-permute-done.15 = bf16[544,128]{1,0:T(8,128)(2,1)S(1)} collective-permute-done((bf16[544,128]{1,0:T(8,128)(2,1)S(1)}, bf16[544,128]{1,0:T(8,128)(2,1)S(1)}, u32[]{:S(2)}, u32[]{:S(2)}) %collective-permute-start.15) | collective-permute-done | bytes 139296 | tf_op jit(solution)/shard_map/ppermute | solution.py:453
  134.9 5.3 %collective-permute-done.16 = bf16[1088,128]{1,0:T(8,128)(2,1)S(1)} collective-permute-done((bf16[1088,128]{1,0:T(8,128)(2,1)S(1)}, bf16[1088,128]{1,0:T(8,128)(2,1)S(1)}, u32[]{:S(2)}, u32[]{:S(2)}) %collective-permute-start.16) | collective-permute-done | bytes 278560 | tf_op jit(solution)/shard_map/ppermute | solution.py:453
  140.4 10.2 %collective-permute-start.17 = (bf16[2176,128]{1,0:T(8,128)(2,1)S(1)}, bf16[2176,128]{1,0:T(8,128)(2,1)S(1)}, u32[]{:S(2)}, u32[]{:S(2)}) collective-permute-start(bf16[2176,128]{1,0:T(8,128)(2,1)S(1)} %pad_maximum_fusion.mine), channel_id=1, source_target_pairs={{0,16},{1,17},{2,18},{3,19},{4,20},{5,21},{6,22},{7,23},{8,24},{9,... | collective-permute-start | bytes 1671176 | tf_op jit(solution)/shard_map/ppermute | solution.py:453
  150.7 2.0 %collective-permute-start.7 = (bf16[176,256]{1,0:T(8,128)(2,1)S(1)}, bf16[176,256]{1,0:T(8,128)(2,1)S(1)}, u32[]{:S(2)}, u32[]{:S(2)}) collective-permute-start(bf16[176,256]{1,0:T(8,128)(2,1)S(1)} %get-tuple-element.38), channel_id=1, source_target_pairs={{16,32},{48,64},{80,96},{112,128},{144,160},{176,192},{208,224},{3... | collective-permute-start | bytes 270344 | tf_op jit(solution)/shard_map/ppermute | solution.py:408
  152.8 5.2 %collective-permute-done.7 = bf16[176,256]{1,0:T(8,128)(2,1)S(1)} collective-permute-done((bf16[176,256]{1,0:T(8,128)(2,1)S(1)}, bf16[176,256]{1,0:T(8,128)(2,1)S(1)}, u32[]{:S(2)}, u32[]{:S(2)}) %collective-permute-start.7) | collective-permute-done | bytes 90144 | tf_op jit(solution)/shard_map/ppermute | solution.py:408
  158.1 3.8 %input_grad.4.rest_0_ = bf16[64,48,256]{2,1,0:T(8,128)(2,1)} custom-call(bf16[64,48,256]{2,1,0:T(8,128)(2,1)S(1)} %get-tuple-element.14.g_ref, bf16[176,256]{1,0:T(8,128)(2,1)S(1)} %get-tuple-element.43.top, bf16[176,256]{1,0:T(8,128)(2,1)S(1)} %get-tuple-element.42.bottom, bf16[192,256]{1,0:T(8,128)(2,1)S(1)} %get-tuple-element.32.left, ...), custom_call_target="tpu_custom_call" | custom-call | bytes 14760000 | tf_op jit(solution)/shard_map/input_grad/pallas_call | solution.py:337
  161.8 3.8 %input_grad.5.rest_0_ = bf16[64,48,256]{2,1,0:T(8,128)(2,1)} custom-call(bf16[64,48,256]{2,1,0:T(8,128)(2,1)S(1)} %get-tuple-element.14.g_ref, bf16[176,256]{1,0:T(8,128)(2,1)S(1)} %get-tuple-element.43.top, bf16[176,256]{1,0:T(8,128)(2,1)S(1)} %get-tuple-element.42.bottom, ...), custom_call_target="tpu_custom_call", output_to_operand_aliasing={{}: (7, {})} | custom-call | bytes 14760000 | tf_op jit(solution)/shard_map/input_grad/pallas_call | solution.py:337
  165.7 3.8 %input_grad.6.rest_0_ = bf16[64,48,256]{2,1,0:T(8,128)(2,1)} custom-call(bf16[64,48,256]{2,1,0:T(8,128)(2,1)S(1)} %get-tuple-element.14.g_ref, bf16[176,256]{1,0:T(8,128)(2,1)S(1)} %get-tuple-element.43.top, bf16[176,256]{1,0:T(8,128)(2,1)S(1)} %get-tuple-element.42.bottom, ...), custom_call_target="tpu_custom_call", output_to_operand_aliasing={{}: (7, {})} | custom-call | bytes 14760000 | tf_op jit(solution)/shard_map/input_grad/pallas_call | solution.py:337
  169.5 3.8 %input_grad.7 = bf16[64,48,256]{2,1,0:T(8,128)(2,1)} custom-call(bf16[64,48,256]{2,1,0:T(8,128)(2,1)S(1)} %get-tuple-element.14.g_ref, bf16[176,256]{1,0:T(8,128)(2,1)S(1)} %get-tuple-element.43.top, bf16[176,256]{1,0:T(8,128)(2,1)S(1)} %get-tuple-element.42.bottom, bf16[192,256]{1,0:T(8,128)(2,1)S(1)} %get-tuple-element.32.left, ...), custom_call_target="tpu_custom_call", output_to_operand_aliasing={{}: (7, {})} | custom-call | bytes 14760000 | tf_op jit(solution)/shard_map/input_grad/pallas_call | solution.py:337
  173.2 1.6 spread.1
  (89 shorter events, 16.4 us)
Async XLA Ops:
  1.8 13.3 %copy-start = (bf16[64,48,256]{2,1,0:T(8,128)(2,1)S(1)}, bf16[64,48,256]{2,1,0:T(8,128)(2,1)}, u32[]{:S(2)}) copy-start(bf16[64,48,256]{2,1,0:T(8,128)(2,1)} %cot.9) | copy-start | bytes 4718596
  1.8 13.3 %copy-start.2 = (f32[49,256]{1,0:T(8,128)S(1)}, f32[49,256]{1,0:T(8,128)}, u32[]{:S(2)}) copy-start(f32[49,256]{1,0:T(8,128)} %w_ref.9) | copy-start | bytes 150532
  1.9 13.3 %copy-start.12 = (f32[1024]{0:T(1024)S(1)}, f32[1024]{0:T(1024)}, u32[]{:S(2)}) copy-start(f32[1024]{0:T(1024)} %param.19) | copy-start | bytes 12292
  1.9 13.3 %copy-start.13 = (s32[4,3]{1,0:T(4,128)S(1)}, s32[4,3]{1,0:T(4,128)}, u32[]{:S(2)}) copy-start(s32[4,3]{1,0:T(4,128)} %tissue.1) | copy-start | bytes 148
  1.9 13.3 %copy-start.14 = (f32[256]{0:T(256)S(1)}, f32[256]{0:T(256)}, u32[]{:S(2)}) copy-start(f32[256]{0:T(256)} %param.15) | copy-start | bytes 3076
  1.9 13.3 %copy-start.15 = (f32[256]{0:T(256)S(1)}, f32[256]{0:T(256)}, u32[]{:S(2)}) copy-start(f32[256]{0:T(256)} %param.16) | copy-start | bytes 3076
  1.9 13.3 %copy-start.16 = (f32[256]{0:T(256)S(1)}, f32[256]{0:T(256)}, u32[]{:S(2)}) copy-start(f32[256]{0:T(256)} %param.17) | copy-start | bytes 3076
  1.9 13.3 %copy-start.17 = (f32[256]{0:T(256)S(1)}, f32[256]{0:T(256)}, u32[]{:S(2)}) copy-start(f32[256]{0:T(256)} %param.21) | copy-start | bytes 3076
  2.0 4.1 %collective-permute-start = (bf16[192,256]{1,0:T(8,128)(2,1)S(1)}, bf16[192,256]{1,0:T(8,128)(2,1)S(1)}, u32[]{:S(2)}, u32[]{:S(2)}) collective-permute-start(bf16[192,256]{1,0:T(8,128)(2,1)S(1)} %select_n.271), channel_id=1, source_target_pairs={{0,1},{2,3},{4,5},{6,7},{8,9},{10,11},{12,13},{14,15},{1,0},{3,2},... | collective-permute-start | bytes 294920 | tf_op jit(solution)/shard_map/ppermute | solution.py:408
  4.2 1.9 %collective-permute-start.1 = (bf16[192,256]{1,0:T(8,128)(2,1)S(1)}, bf16[192,256]{1,0:T(8,128)(2,1)S(1)}, u32[]{:S(2)}, u32[]{:S(2)}) collective-permute-start(bf16[192,256]{1,0:T(8,128)(2,1)S(1)} %select_n.273), channel_id=1, source_target_pairs={{1,2},{3,4},{5,6},{7,8},{9,10},{11,12},{13,14},{2,1},{4,3},{6,5},{... | collective-permute-start | bytes 294920 | tf_op jit(solution)/shard_map/ppermute | solution.py:408
  6.3 8.8 %collective-permute-start.3 = (bf16[176,256]{1,0:T(8,128)(2,1)S(1)}, bf16[176,256]{1,0:T(8,128)(2,1)S(1)}, u32[]{:S(2)}, u32[]{:S(2)}) collective-permute-start(bf16[176,256]{1,0:T(8,128)(2,1)S(1)} %get-tuple-element.40), channel_id=1, source_target_pairs={{16,32},{48,64},{80,96},{112,128},{144,160},{176,192},{208,224},{3... | collective-permute-start | bytes 270344 | tf_op jit(solution)/shard_map/ppermute | solution.py:408
  12.9 2.2 %collective-permute-start.2 = (bf16[176,256]{1,0:T(8,128)(2,1)S(1)}, bf16[176,256]{1,0:T(8,128)(2,1)S(1)}, u32[]{:S(2)}, u32[]{:S(2)}) collective-permute-start(bf16[176,256]{1,0:T(8,128)(2,1)S(1)} %get-tuple-element.41), channel_id=1, source_target_pairs={{0,16},{32,48},{64,80},{96,112},{128,144},{160,176},{192,208},{224... | collective-permute-start | bytes 270344 | tf_op jit(solution)/shard_map/ppermute | solution.py:408
  15.2 1.4 copy-start.1
  16.7 1.0 copy-start.4
  17.7 1.0 copy-start.5
  64.0 2.3 %collective-permute-start.8 = (bf16[2176,128]{1,0:T(8,128)(2,1)}, bf16[2176,128]{1,0:T(8,128)(2,1)}, u32[]{:S(2)}, u32[]{:S(2)}) collective-permute-start(bf16[2176,128]{1,0:T(8,128)(2,1)} %get-tuple-element.20), channel_id=1, source_target_pairs={{0,16},{1,17},{2,18},{3,19},{4,20},{5,21},{6,22},{7,23},{8,24},{9,... | collective-permute-start | bytes 1671176 | tf_op jit(solution)/shard_map/ppermute | solution.py:453
  69.5 11.2 %collective-permute-start.9 = (bf16[1088,128]{1,0:T(8,128)(2,1)}, bf16[1088,128]{1,0:T(8,128)(2,1)}, u32[]{:S(2)}, u32[]{:S(2)}) collective-permute-start(bf16[1088,128]{1,0:T(8,128)(2,1)} %select_convert_fusion), channel_id=1, source_target_pairs={{0,1},{1,0},{2,3},{3,2},{4,5},{5,4},{6,7},{7,6},{8,9},{9,8},{10,11... | collective-permute-start | bytes 835592 | tf_op jit(solution)/shard_map/ppermute | solution.py:453
  83.6 6.4 %collective-permute-start.10 = (bf16[544,128]{1,0:T(8,128)(2,1)}, bf16[544,128]{1,0:T(8,128)(2,1)S(1)}, u32[]{:S(2)}, u32[]{:S(2)}) collective-permute-start(bf16[544,128]{1,0:T(8,128)(2,1)} %select_convert_fusion.1), channel_id=1, source_target_pairs={{0,33},{1,32},{2,35},{3,34},{4,37},{5,36},{6,39},{7,38},{8,41},{9,... | collective-permute-start | bytes 417800 | tf_op jit(solution)/shard_map/ppermute | solution.py:453
  91.8 3.9 %collective-permute-start.11 = (bf16[272,128]{1,0:T(8,128)(2,1)S(1)}, bf16[272,128]{1,0:T(8,128)(2,1)S(1)}, u32[]{:S(2)}, u32[]{:S(2)}) collective-permute-start(bf16[272,128]{1,0:T(8,128)(2,1)S(1)} %select_convert_fusion.2), channel_id=1, source_target_pairs={{0,64},{1,65},{2,66},{3,67},{4,68},{5,69},{6,70},{7,71},{8,72},{9,... | collective-permute-start | bytes 208904 | tf_op jit(solution)/shard_map/ppermute | solution.py:453
  96.7 33.5 %copy-start.7 = (bf16[192,256]{1,0:T(8,128)(2,1)S(1)}, bf16[192,256]{1,0:T(8,128)(2,1)}, u32[]{:S(2)}) copy-start(bf16[192,256]{1,0:T(8,128)(2,1)} %copy-done.6) | copy-start | bytes 294916
  96.7 4.3 %collective-permute-start.12 = (bf16[136,128]{1,0:T(8,128)(2,1)S(1)}, bf16[136,128]{1,0:T(8,128)(2,1)S(1)}, u32[]{:S(2)}, u32[]{:S(2)}) collective-permute-start(bf16[136,128]{1,0:T(8,128)(2,1)S(1)} %select_convert_fusion.3), channel_id=1, source_target_pairs={{0,192},{1,193},{2,194},{3,195},{4,196},{5,197},{6,198},{7,199},{8... | collective-permute-start | bytes 104456 | tf_op jit(solution)/shard_map/ppermute | solution.py:453
  121.5 4.4 %collective-permute-start.13 = (bf16[136,128]{1,0:T(8,128)(2,1)S(1)}, bf16[136,128]{1,0:T(8,128)(2,1)S(1)}, u32[]{:S(2)}, u32[]{:S(2)}) collective-permute-start(bf16[136,128]{1,0:T(8,128)(2,1)S(1)} %reduce_sum.12), channel_id=1, source_target_pairs={{0,192},{1,193},{2,194},{3,195},{4,196},{5,197},{6,198},{7,199},{8... | collective-permute-start | bytes 104456 | tf_op jit(solution)/shard_map/ppermute | solution.py:453
  126.0 3.4 %collective-permute-start.14 = (bf16[272,128]{1,0:T(8,128)(2,1)S(1)}, bf16[272,128]{1,0:T(8,128)(2,1)S(1)}, u32[]{:S(2)}, u32[]{:S(2)}) collective-permute-start(bf16[272,128]{1,0:T(8,128)(2,1)S(1)} %pad_maximum_fusion.3), channel_id=1, source_target_pairs={{0,64},{1,65},{2,66},{3,67},{4,68},{5,69},{6,70},{7,71},{8,72},{9,... | collective-permute-start | bytes 208904 | tf_op jit(solution)/shard_map/ppermute | solution.py:453
  129.4 5.2 %collective-permute-start.15 = (bf16[544,128]{1,0:T(8,128)(2,1)S(1)}, bf16[544,128]{1,0:T(8,128)(2,1)S(1)}, u32[]{:S(2)}, u32[]{:S(2)}) collective-permute-start(bf16[544,128]{1,0:T(8,128)(2,1)S(1)} %pad_maximum_fusion.2), channel_id=1, source_target_pairs={{0,33},{1,32},{2,35},{3,34},{4,37},{5,36},{6,39},{7,38},{8,41},{9,... | collective-permute-start | bytes 417800 | tf_op jit(solution)/shard_map/ppermute | solution.py:453
  130.2 4.6 %collective-permute-start.4 = (bf16[192,256]{1,0:T(8,128)(2,1)S(1)}, bf16[192,256]{1,0:T(8,128)(2,1)S(1)}, u32[]{:S(2)}, u32[]{:S(2)}) collective-permute-start(bf16[192,256]{1,0:T(8,128)(2,1)S(1)} %get-tuple-element.34), channel_id=1, source_target_pairs={{0,1},{2,3},{4,5},{6,7},{8,9},{10,11},{12,13},{14,15},{1,0},{3,2},... | collective-permute-start | bytes 294920 | tf_op jit(solution)/shard_map/ppermute | solution.py:408
  130.3 4.5 %collective-permute-start.5 = (bf16[192,256]{1,0:T(8,128)(2,1)S(1)}, bf16[192,256]{1,0:T(8,128)(2,1)S(1)}, u32[]{:S(2)}, u32[]{:S(2)}) collective-permute-start(bf16[192,256]{1,0:T(8,128)(2,1)S(1)} %get-tuple-element.35), channel_id=1, source_target_pairs={{1,2},{3,4},{5,6},{7,8},{9,10},{11,12},{13,14},{2,1},{4,3},{6,5},{... | collective-permute-start | bytes 294920 | tf_op jit(solution)/shard_map/ppermute | solution.py:408
  134.7 5.5 %collective-permute-start.16 = (bf16[1088,128]{1,0:T(8,128)(2,1)S(1)}, bf16[1088,128]{1,0:T(8,128)(2,1)S(1)}, u32[]{:S(2)}, u32[]{:S(2)}) collective-permute-start(bf16[1088,128]{1,0:T(8,128)(2,1)S(1)} %pad_maximum_fusion.1), channel_id=1, source_target_pairs={{0,1},{1,0},{2,3},{3,2},{4,5},{5,4},{6,7},{7,6},{8,9},{9,8},{10,11... | collective-permute-start | bytes 835592 | tf_op jit(solution)/shard_map/ppermute | solution.py:453
  134.9 15.7 %copy-start.9 = (bf16[144,256]{1,0:T(8,128)(2,1)S(1)}, bf16[144,256]{1,0:T(8,128)(2,1)}, u32[]{:S(2)}) copy-start(bf16[144,256]{1,0:T(8,128)(2,1)} %copy-done.8) | copy-start | bytes 221188
  134.9 15.7 %copy-start.11 = (bf16[144,256]{1,0:T(8,128)(2,1)S(1)}, bf16[144,256]{1,0:T(8,128)(2,1)}, u32[]{:S(2)}) copy-start(bf16[144,256]{1,0:T(8,128)(2,1)} %copy-done.10) | copy-start | bytes 221188
  140.4 32.8 %collective-permute-start.17 = (bf16[2176,128]{1,0:T(8,128)(2,1)S(1)}, bf16[2176,128]{1,0:T(8,128)(2,1)S(1)}, u32[]{:S(2)}, u32[]{:S(2)}) collective-permute-start(bf16[2176,128]{1,0:T(8,128)(2,1)S(1)} %pad_maximum_fusion.mine), channel_id=1, source_target_pairs={{0,16},{1,17},{2,18},{3,19},{4,20},{5,21},{6,22},{7,23},{8,24},{9,... | collective-permute-start | bytes 1671176 | tf_op jit(solution)/shard_map/ppermute | solution.py:453
  150.7 7.4 %collective-permute-start.7 = (bf16[176,256]{1,0:T(8,128)(2,1)S(1)}, bf16[176,256]{1,0:T(8,128)(2,1)S(1)}, u32[]{:S(2)}, u32[]{:S(2)}) collective-permute-start(bf16[176,256]{1,0:T(8,128)(2,1)S(1)} %get-tuple-element.38), channel_id=1, source_target_pairs={{16,32},{48,64},{80,96},{112,128},{144,160},{176,192},{208,224},{3... | collective-permute-start | bytes 270344 | tf_op jit(solution)/shard_map/ppermute | solution.py:408
  152.7 5.3 %collective-permute-start.6 = (bf16[176,256]{1,0:T(8,128)(2,1)S(1)}, bf16[176,256]{1,0:T(8,128)(2,1)S(1)}, u32[]{:S(2)}, u32[]{:S(2)}) collective-permute-start(bf16[176,256]{1,0:T(8,128)(2,1)S(1)} %get-tuple-element.39), channel_id=1, source_target_pairs={{0,16},{32,48},{64,80},{96,112},{128,144},{160,176},{192,208},{224... | collective-permute-start | bytes 270344 | tf_op jit(solution)/shard_map/ppermute | solution.py:408
  (7 other events, 5.4 us)

commit v6 on v5

--- a/solution.py
+++ b/solution.py
@@ -252,12 +252,16 @@
     hidden = we.shape[1]
     pix = TILE * cols
     block = pl.BlockSpec((TILE, cols, chans), lambda s, t, u: (s, 0, 0))
+    whole = lambda *shape: pl.BlockSpec(shape, lambda s, t, u: (0, 0))
     size = (2 * chans + EXTRA) * (hidden // LANES) // 2
     grid = pltpu.PrefetchScalarGridSpec(
         num_scalar_prefetch=2,
         grid=(rows // TILE,),
         in_specs=[VMEM] * 5 + [block] + [VMEM] * 8,
-        out_specs=[VMEM] * 7,
+        out_specs=[pl.BlockSpec((rows, cols, chans), lambda s, t, u: (0, 0, 0))]
+        + [whole(3 * rows, chans)] * 2
+        + [whole(3 * cols, chans)] * 2
+        + [whole(size, LANES)] * 2,
         scratch_shapes=[
             pltpu.VMEM((2 * TAPS, LANES), F32),
             pltpu.VMEM((2 * chans, hidden), F32),
@@ -288,7 +292,7 @@
             jax.ShapeDtypeStruct((size, LANES), F32),
             jax.ShapeDtypeStruct((size, LANES), BF16),
         ),
-        compiler_params=pltpu.CompilerParams(vmem_limit_bytes=40 << 20),
+        compiler_params=pltpu.CompilerParams(vmem_limit_bytes=56 << 20),
         cost_estimate=cost(42),
         name="branch",
     )(tissue, upper, x, *halo, cot, w, bias, gain, shift, we, be, wr, scale)

time: 176 us -> 164 us (0.932)
  local copies, waits for them, and re-layouts: 10.8 us -> 1.91 us
  other arithmetic: 9.24 us -> 4.11 us
  Pallas kernels: 59.1 us -> 61.5 us
    unnamed x42 -> x18, local copies, waits for them, and re-layouts: 8.92 us -> 0.05 us
    add x4, other arithmetic: 4.95 us -> 1.47 us  [total(): kept = kept + swap(sent, name).astype(F32)]
    pallas_call x1, Pallas kernels: 42.3 us -> 45 us  [branch(): pl.pallas_call(branch_kernel, grid_spec=grid, out_shape=(jax.ShapeDtypeSt...]
where the time goes in v6:
time: 164 us; the launch traced here: 163 us
  Pallas kernels  61.5 us (38%)
  starting transfers between devices  39.6 us (24%)
  waiting for transfers between devices  35.6 us (22%)
  blocking collectives  19.3 us (12%)
  other arithmetic  4.11 us (3%)
  local copies, waits for them, and re-layouts  1.91 us (1%)
    pallas_call x1, Pallas kernels, branch(): pl.pallas_call(branch_kernel, grid_spec=grid, out_shape=(jax.ShapeDtypeSt...  45 us
    ppermute x10, waiting for transfers between devices, swap(): return lax.ppermute(value, AXES, pairs)  28.2 us
    ppermute x10, starting transfers between devices, swap(): return lax.ppermute(value, AXES, pairs)  27.1 us
    all_to_all x1, blocking collectives, total(): copies = lax.all_to_all(copies, 'z', 0, 0, tiled=True)  19.3 us
    pallas_call x4, Pallas kernels, input_grad(): pl.pallas_call(functools.partial(input_kernel, part), grid=(1,), out_shap...  15 us
    ppermute x8, starting transfers between devices, beside(): return lax.ppermute(value, axes, pairs + [(b, a) for a, b in pairs])  12.5 us
    ppermute x8, waiting for transfers between devices, beside(): return lax.ppermute(value, axes, pairs + [(b, a) for a, b in pairs])  7.4 us
  transfers between devices with their start and end apart: 18, of which 12 were waited for; matrix products, arithmetic and copies ran while one was open for 1% of the time, Pallas kernels for 9%

profile of v6, /device:TPU:1, one launch (start us, length us, event | category | flops | bytes accessed | tf_op | source)
XLA Modules:
  0.0 163.2 jit_solution(17997920333932190666)
XLA Ops:
  0.6 1.2 broadcast_select_fusion.5
  1.9 2.1 %collective-permute-start = (bf16[192,256]{1,0:T(8,128)(2,1)S(1)}, bf16[192,256]{1,0:T(8,128)(2,1)S(1)}, u32[]{:S(2)}, u32[]{:S(2)}) collective-permute-start(bf16[192,256]{1,0:T(8,128)(2,1)S(1)} %select_n.271), channel_id=1, source_target_pairs={{0,1},{2,3},{4,5},{6,7},{8,9},{10,11},{12,13},{14,15},{1,0},{3,2},... | collective-permute-start | bytes 294920 | tf_op jit(solution)/shard_map/ppermute | solution.py:412
  4.8 0.9 fusion
  6.2 6.6 %collective-permute-start.3 = (bf16[176,256]{1,0:T(8,128)(2,1)S(1)}, bf16[176,256]{1,0:T(8,128)(2,1)S(1)}, u32[]{:S(2)}, u32[]{:S(2)}) collective-permute-start(bf16[176,256]{1,0:T(8,128)(2,1)S(1)} %get-tuple-element.40), channel_id=1, source_target_pairs={{16,32},{48,64},{80,96},{112,128},{144,160},{176,192},{208,224},{3... | collective-permute-start | bytes 270344 | tf_op jit(solution)/shard_map/ppermute | solution.py:412
  13.0 2.1 %collective-permute-done.3 = bf16[176,256]{1,0:T(8,128)(2,1)S(1)} collective-permute-done((bf16[176,256]{1,0:T(8,128)(2,1)S(1)}, bf16[176,256]{1,0:T(8,128)(2,1)S(1)}, u32[]{:S(2)}, u32[]{:S(2)}) %collective-permute-start.3) | collective-permute-done | bytes 90144 | tf_op jit(solution)/shard_map/ppermute | solution.py:412
  15.1 0.7 broadcast_select_fusion.16
  15.8 45.0 %branch.1 = (bf16[64,48,256]{2,1,0:T(8,128)(2,1)}, bf16[192,256]{1,0:T(8,128)(2,1)}, bf16[192,256]{1,0:T(8,128)(2,1)}, bf16[144,256]{1,0:T(8,128)(2,1)}, bf16[14...) custom-call(s32[4,3]{1,0:T(4,128)} %tissue.1, s32[1]{0:T(128)} %bitcast.upper, ...), custom_call_target="tpu_custom_call" | custom-call | bytes 154980000 | tf_op jit(solution)/shard_map/branch/pallas_call | solution.py:283
  60.8 2.1 %collective-permute-done.8 = bf16[2176,128]{1,0:T(8,128)(2,1)S(1)} collective-permute-done((bf16[2176,128]{1,0:T(8,128)(2,1)}, bf16[2176,128]{1,0:T(8,128)(2,1)S(1)}, u32[]{:S(2)}, u32[]{:S(2)}) %collective-permute-start.8) | collective-permute-done | bytes 557088 | tf_op jit(solution)/shard_map/ppermute | solution.py:457
  62.9 1.3 convert_add_fusion
  64.3 4.1 %collective-permute-start.9 = (bf16[1088,128]{1,0:T(8,128)(2,1)S(1)}, bf16[1088,128]{1,0:T(8,128)(2,1)S(1)}, u32[]{:S(2)}, u32[]{:S(2)}) collective-permute-start(bf16[1088,128]{1,0:T(8,128)(2,1)S(1)} %select_convert_fusion), channel_id=1, source_target_pairs={{0,1},{1,0},{2,3},{3,2},{4,5},{5,4},{6,7},{7,6},{8,9},{9,8},{10,11... | collective-permute-start | bytes 835592 | tf_op jit(solution)/shard_map/ppermute | solution.py:457
  68.4 6.9 %collective-permute-done.9 = bf16[1088,128]{1,0:T(8,128)(2,1)S(1)} collective-permute-done((bf16[1088,128]{1,0:T(8,128)(2,1)S(1)}, bf16[1088,128]{1,0:T(8,128)(2,1)S(1)}, u32[]{:S(2)}, u32[]{:S(2)}) %collective-permute-start.9) | collective-permute-done | bytes 278560 | tf_op jit(solution)/shard_map/ppermute | solution.py:457
  75.4 3.4 %collective-permute-start.10 = (bf16[544,128]{1,0:T(8,128)(2,1)S(1)}, bf16[544,128]{1,0:T(8,128)(2,1)S(1)}, u32[]{:S(2)}, u32[]{:S(2)}) collective-permute-start(bf16[544,128]{1,0:T(8,128)(2,1)S(1)} %select_convert_fusion.1), channel_id=1, source_target_pairs={{0,33},{1,32},{2,35},{3,34},{4,37},{5,36},{6,39},{7,38},{8,41},{9,... | collective-permute-start | bytes 417800 | tf_op jit(solution)/shard_map/ppermute | solution.py:457
  78.8 2.8 %collective-permute-done.10 = bf16[544,128]{1,0:T(8,128)(2,1)S(1)} collective-permute-done((bf16[544,128]{1,0:T(8,128)(2,1)S(1)}, bf16[544,128]{1,0:T(8,128)(2,1)S(1)}, u32[]{:S(2)}, u32[]{:S(2)}) %collective-permute-start.10) | collective-permute-done | bytes 139296 | tf_op jit(solution)/shard_map/ppermute | solution.py:457
  81.7 2.2 %collective-permute-start.11 = (bf16[272,128]{1,0:T(8,128)(2,1)S(1)}, bf16[272,128]{1,0:T(8,128)(2,1)S(1)}, u32[]{:S(2)}, u32[]{:S(2)}) collective-permute-start(bf16[272,128]{1,0:T(8,128)(2,1)S(1)} %select_convert_fusion.2), channel_id=1, source_target_pairs={{0,64},{1,65},{2,66},{3,67},{4,68},{5,69},{6,70},{7,71},{8,72},{9,... | collective-permute-start | bytes 208904 | tf_op jit(solution)/shard_map/ppermute | solution.py:457
  83.9 1.7 %collective-permute-done.11 = bf16[272,128]{1,0:T(8,128)(2,1)S(1)} collective-permute-done((bf16[272,128]{1,0:T(8,128)(2,1)S(1)}, bf16[272,128]{1,0:T(8,128)(2,1)S(1)}, u32[]{:S(2)}, u32[]{:S(2)}) %collective-permute-start.11) | collective-permute-done | bytes 69664 | tf_op jit(solution)/shard_map/ppermute | solution.py:457
  85.7 3.0 %collective-permute-start.12 = (bf16[136,128]{1,0:T(8,128)(2,1)S(1)}, bf16[136,128]{1,0:T(8,128)(2,1)S(1)}, u32[]{:S(2)}, u32[]{:S(2)}) collective-permute-start(bf16[136,128]{1,0:T(8,128)(2,1)S(1)} %select_convert_fusion.3), channel_id=1, source_target_pairs={{0,192},{1,193},{2,194},{3,195},{4,196},{5,197},{6,198},{7,199},{8... | collective-permute-start | bytes 104456 | tf_op jit(solution)/shard_map/ppermute | solution.py:457
  88.7 1.3 collective-permute-done.12
  90.1 19.3 %all_to_all.5 = bf16[8,136,128]{2,1,0:T(8,128)(2,1)S(1)} all-to-all(bf16[8,136,128]{2,1,0:T(8,128)(2,1)S(1)} %broadcast_in_dim.2), channel_id=1, replica_groups=mesh['y'=4,'x_hi'=2,'core'=2,'z'=8,'x_lo'=2] {'z'}, dimensions={0} | all-to-all | bytes 557056 | tf_op jit(solution)/shard_map/all_to_all | solution.py:472
  109.4 2.8 %collective-permute-start.13 = (bf16[136,128]{1,0:T(8,128)(2,1)S(1)}, bf16[136,128]{1,0:T(8,128)(2,1)S(1)}, u32[]{:S(2)}, u32[]{:S(2)}) collective-permute-start(bf16[136,128]{1,0:T(8,128)(2,1)S(1)} %reduce_sum.12), channel_id=1, source_target_pairs={{0,192},{1,193},{2,194},{3,195},{4,196},{5,197},{6,198},{7,199},{8... | collective-permute-start | bytes 104456 | tf_op jit(solution)/shard_map/ppermute | solution.py:457
  112.2 1.6 collective-permute-done.13
  114.1 3.1 %collective-permute-done.14 = bf16[272,128]{1,0:T(8,128)(2,1)S(1)} collective-permute-done((bf16[272,128]{1,0:T(8,128)(2,1)S(1)}, bf16[272,128]{1,0:T(8,128)(2,1)S(1)}, u32[]{:S(2)}, u32[]{:S(2)}) %collective-permute-start.14) | collective-permute-done | bytes 69664 | tf_op jit(solution)/shard_map/ppermute | solution.py:457
  117.3 1.1 collective-permute-start.15
  119.2 3.3 %collective-permute-done.15 = bf16[544,128]{1,0:T(8,128)(2,1)S(1)} collective-permute-done((bf16[544,128]{1,0:T(8,128)(2,1)S(1)}, bf16[544,128]{1,0:T(8,128)(2,1)S(1)}, u32[]{:S(2)}, u32[]{:S(2)}) %collective-permute-start.15) | collective-permute-done | bytes 139296 | tf_op jit(solution)/shard_map/ppermute | solution.py:457
  122.8 5.3 %collective-permute-done.16 = bf16[1088,128]{1,0:T(8,128)(2,1)S(1)} collective-permute-done((bf16[1088,128]{1,0:T(8,128)(2,1)S(1)}, bf16[1088,128]{1,0:T(8,128)(2,1)S(1)}, u32[]{:S(2)}, u32[]{:S(2)}) %collective-permute-start.16) | collective-permute-done | bytes 278560 | tf_op jit(solution)/shard_map/ppermute | solution.py:457
  128.3 10.2 %collective-permute-start.17 = (bf16[2176,128]{1,0:T(8,128)(2,1)S(1)}, bf16[2176,128]{1,0:T(8,128)(2,1)S(1)}, u32[]{:S(2)}, u32[]{:S(2)}) collective-permute-start(bf16[2176,128]{1,0:T(8,128)(2,1)S(1)} %pad_maximum_fusion.mine), channel_id=1, source_target_pairs={{0,16},{1,17},{2,18},{3,19},{4,20},{5,21},{6,22},{7,23},{8,24},{9,... | collective-permute-start | bytes 1671176 | tf_op jit(solution)/shard_map/ppermute | solution.py:457
  138.6 2.2 %collective-permute-start.7 = (bf16[176,256]{1,0:T(8,128)(2,1)S(1)}, bf16[176,256]{1,0:T(8,128)(2,1)S(1)}, u32[]{:S(2)}, u32[]{:S(2)}) collective-permute-start(bf16[176,256]{1,0:T(8,128)(2,1)S(1)} %get-tuple-element.38), channel_id=1, source_target_pairs={{16,32},{48,64},{80,96},{112,128},{144,160},{176,192},{208,224},{3... | collective-permute-start | bytes 270344 | tf_op jit(solution)/shard_map/ppermute | solution.py:412
  140.9 5.1 %collective-permute-done.7 = bf16[176,256]{1,0:T(8,128)(2,1)S(1)} collective-permute-done((bf16[176,256]{1,0:T(8,128)(2,1)S(1)}, bf16[176,256]{1,0:T(8,128)(2,1)S(1)}, u32[]{:S(2)}, u32[]{:S(2)}) %collective-permute-start.7) | collective-permute-done | bytes 90144 | tf_op jit(solution)/shard_map/ppermute | solution.py:412
  146.1 3.7 %input_grad.4.rest_0_ = bf16[64,48,256]{2,1,0:T(8,128)(2,1)} custom-call(bf16[64,48,256]{2,1,0:T(8,128)(2,1)S(1)} %copy-done.1, bf16[176,256]{1,0:T(8,128)(2,1)S(1)} %get-tuple-element.43.top, bf16[176,256]{1,0:T(8,128)(2,1)S(1)} %get-tuple-element.42.bottom, bf16[192,256]{1,0:T(8,128)(2,1)S(1)} %get-tuple-element.32.left, ...), custom_call_target="tpu_custom_call" | custom-call | bytes 14760000 | tf_op jit(solution)/shard_map/input_grad/pallas_call | solution.py:341
  149.8 3.8 %input_grad.5.rest_0_ = bf16[64,48,256]{2,1,0:T(8,128)(2,1)} custom-call(bf16[64,48,256]{2,1,0:T(8,128)(2,1)S(1)} %copy-done.1, bf16[176,256]{1,0:T(8,128)(2,1)S(1)} %get-tuple-element.43.top, bf16[176,256]{1,0:T(8,128)(2,1)S(1)} %get-tuple-element.42.bottom, bf16[192,256]{1,0:T(8,128)(2,1)S(1)} %get-tuple-element.32.left, ...), custom_call_target="tpu_custom_call", output_to_operand_aliasing={{}: (7, {})} | custom-call | bytes 14760000 | tf_op jit(solution)/shard_map/input_grad/pallas_call | solution.py:341
  153.5 3.8 %input_grad.6.rest_0_ = bf16[64,48,256]{2,1,0:T(8,128)(2,1)} custom-call(bf16[64,48,256]{2,1,0:T(8,128)(2,1)S(1)} %copy-done.1, bf16[176,256]{1,0:T(8,128)(2,1)S(1)} %get-tuple-element.43.top, bf16[176,256]{1,0:T(8,128)(2,1)S(1)} %get-tuple-element.42.bottom, bf16[192,256]{1,0:T(8,128)(2,1)S(1)} %get-tuple-element.32.left, ...), custom_call_target="tpu_custom_call", output_to_operand_aliasing={{}: (7, {})} | custom-call | bytes 14760000 | tf_op jit(solution)/shard_map/input_grad/pallas_call | solution.py:341
  157.3 3.7 %input_grad.7 = bf16[64,48,256]{2,1,0:T(8,128)(2,1)} custom-call(bf16[64,48,256]{2,1,0:T(8,128)(2,1)S(1)} %copy-done.1, bf16[176,256]{1,0:T(8,128)(2,1)S(1)} %get-tuple-element.43.top, bf16[176,256]{1,0:T(8,128)(2,1)S(1)} %get-tuple-element.42.bottom, bf16[192,256]{1,0:T(8,128)(2,1)S(1)} %get-tuple-element.32.left, ...), custom_call_target="tpu_custom_call", output_to_operand_aliasing={{}: (7, {})} | custom-call | bytes 14760000 | tf_op jit(solution)/shard_map/input_grad/pallas_call | solution.py:341
  161.0 1.6 spread.1
  (65 shorter events, 4.1 us)
Async XLA Ops:
  1.9 4.1 %collective-permute-start = (bf16[192,256]{1,0:T(8,128)(2,1)S(1)}, bf16[192,256]{1,0:T(8,128)(2,1)S(1)}, u32[]{:S(2)}, u32[]{:S(2)}) collective-permute-start(bf16[192,256]{1,0:T(8,128)(2,1)S(1)} %select_n.271), channel_id=1, source_target_pairs={{0,1},{2,3},{4,5},{6,7},{8,9},{10,11},{12,13},{14,15},{1,0},{3,2},... | collective-permute-start | bytes 294920 | tf_op jit(solution)/shard_map/ppermute | solution.py:412
  4.1 1.9 %collective-permute-start.1 = (bf16[192,256]{1,0:T(8,128)(2,1)S(1)}, bf16[192,256]{1,0:T(8,128)(2,1)S(1)}, u32[]{:S(2)}, u32[]{:S(2)}) collective-permute-start(bf16[192,256]{1,0:T(8,128)(2,1)S(1)} %select_n.273), channel_id=1, source_target_pairs={{1,2},{3,4},{5,6},{7,8},{9,10},{11,12},{13,14},{2,1},{4,3},{6,5},{... | collective-permute-start | bytes 294920 | tf_op jit(solution)/shard_map/ppermute | solution.py:412
  6.1 9.7 %copy-start.3 = (bf16[192,256]{1,0:T(8,128)(2,1)}, bf16[192,256]{1,0:T(8,128)(2,1)S(1)}, u32[]{:S(2)}) copy-start(bf16[192,256]{1,0:T(8,128)(2,1)S(1)} %get-tuple-element.36.left) | copy-start | bytes 294916
  6.1 9.7 %copy-start.4 = (bf16[192,256]{1,0:T(8,128)(2,1)}, bf16[192,256]{1,0:T(8,128)(2,1)S(1)}, u32[]{:S(2)}) copy-start(bf16[192,256]{1,0:T(8,128)(2,1)S(1)} %get-tuple-element.37.right) | copy-start | bytes 294916
  6.2 8.8 %collective-permute-start.3 = (bf16[176,256]{1,0:T(8,128)(2,1)S(1)}, bf16[176,256]{1,0:T(8,128)(2,1)S(1)}, u32[]{:S(2)}, u32[]{:S(2)}) collective-permute-start(bf16[176,256]{1,0:T(8,128)(2,1)S(1)} %get-tuple-element.40), channel_id=1, source_target_pairs={{16,32},{48,64},{80,96},{112,128},{144,160},{176,192},{208,224},{3... | collective-permute-start | bytes 270344 | tf_op jit(solution)/shard_map/ppermute | solution.py:412
  12.8 2.2 %collective-permute-start.2 = (bf16[176,256]{1,0:T(8,128)(2,1)S(1)}, bf16[176,256]{1,0:T(8,128)(2,1)S(1)}, u32[]{:S(2)}, u32[]{:S(2)}) collective-permute-start(bf16[176,256]{1,0:T(8,128)(2,1)S(1)} %get-tuple-element.41), channel_id=1, source_target_pairs={{0,16},{32,48},{64,80},{96,112},{128,144},{160,176},{192,208},{224... | collective-permute-start | bytes 270344 | tf_op jit(solution)/shard_map/ppermute | solution.py:412
  60.8 2.2 %collective-permute-start.8 = (bf16[2176,128]{1,0:T(8,128)(2,1)}, bf16[2176,128]{1,0:T(8,128)(2,1)S(1)}, u32[]{:S(2)}, u32[]{:S(2)}) collective-permute-start(bf16[2176,128]{1,0:T(8,128)(2,1)} %get-tuple-element.20), channel_id=1, source_target_pairs={{0,16},{1,17},{2,18},{3,19},{4,20},{5,21},{6,22},{7,23},{8,24},{9,... | collective-permute-start | bytes 1671176 | tf_op jit(solution)/shard_map/ppermute | solution.py:457
  64.3 11.0 %collective-permute-start.9 = (bf16[1088,128]{1,0:T(8,128)(2,1)S(1)}, bf16[1088,128]{1,0:T(8,128)(2,1)S(1)}, u32[]{:S(2)}, u32[]{:S(2)}) collective-permute-start(bf16[1088,128]{1,0:T(8,128)(2,1)S(1)} %select_convert_fusion), channel_id=1, source_target_pairs={{0,1},{1,0},{2,3},{3,2},{4,5},{5,4},{6,7},{7,6},{8,9},{9,8},{10,11... | collective-permute-start | bytes 835592 | tf_op jit(solution)/shard_map/ppermute | solution.py:457
  75.4 6.3 %collective-permute-start.10 = (bf16[544,128]{1,0:T(8,128)(2,1)S(1)}, bf16[544,128]{1,0:T(8,128)(2,1)S(1)}, u32[]{:S(2)}, u32[]{:S(2)}) collective-permute-start(bf16[544,128]{1,0:T(8,128)(2,1)S(1)} %select_convert_fusion.1), channel_id=1, source_target_pairs={{0,33},{1,32},{2,35},{3,34},{4,37},{5,36},{6,39},{7,38},{8,41},{9,... | collective-permute-start | bytes 417800 | tf_op jit(solution)/shard_map/ppermute | solution.py:457
  81.7 3.9 %collective-permute-start.11 = (bf16[272,128]{1,0:T(8,128)(2,1)S(1)}, bf16[272,128]{1,0:T(8,128)(2,1)S(1)}, u32[]{:S(2)}, u32[]{:S(2)}) collective-permute-start(bf16[272,128]{1,0:T(8,128)(2,1)S(1)} %select_convert_fusion.2), channel_id=1, source_target_pairs={{0,64},{1,65},{2,66},{3,67},{4,68},{5,69},{6,70},{7,71},{8,72},{9,... | collective-permute-start | bytes 208904 | tf_op jit(solution)/shard_map/ppermute | solution.py:457
  85.7 32.7 %copy-start.5 = (bf16[192,256]{1,0:T(8,128)(2,1)S(1)}, bf16[192,256]{1,0:T(8,128)(2,1)}, u32[]{:S(2)}) copy-start(bf16[192,256]{1,0:T(8,128)(2,1)} %get-tuple-element.16) | copy-start | bytes 294916
  85.7 32.7 %copy-start.6 = (bf16[192,256]{1,0:T(8,128)(2,1)S(1)}, bf16[192,256]{1,0:T(8,128)(2,1)}, u32[]{:S(2)}) copy-start(bf16[192,256]{1,0:T(8,128)(2,1)} %get-tuple-element.17) | copy-start | bytes 294916
  85.7 4.3 %collective-permute-start.12 = (bf16[136,128]{1,0:T(8,128)(2,1)S(1)}, bf16[136,128]{1,0:T(8,128)(2,1)S(1)}, u32[]{:S(2)}, u32[]{:S(2)}) collective-permute-start(bf16[136,128]{1,0:T(8,128)(2,1)S(1)} %select_convert_fusion.3), channel_id=1, source_target_pairs={{0,192},{1,193},{2,194},{3,195},{4,196},{5,197},{6,198},{7,199},{8... | collective-permute-start | bytes 104456 | tf_op jit(solution)/shard_map/ppermute | solution.py:457
  109.4 4.4 %collective-permute-start.13 = (bf16[136,128]{1,0:T(8,128)(2,1)S(1)}, bf16[136,128]{1,0:T(8,128)(2,1)S(1)}, u32[]{:S(2)}, u32[]{:S(2)}) collective-permute-start(bf16[136,128]{1,0:T(8,128)(2,1)S(1)} %reduce_sum.12), channel_id=1, source_target_pairs={{0,192},{1,193},{2,194},{3,195},{4,196},{5,197},{6,198},{7,199},{8... | collective-permute-start | bytes 104456 | tf_op jit(solution)/shard_map/ppermute | solution.py:457
  113.8 3.4 %collective-permute-start.14 = (bf16[272,128]{1,0:T(8,128)(2,1)S(1)}, bf16[272,128]{1,0:T(8,128)(2,1)S(1)}, u32[]{:S(2)}, u32[]{:S(2)}) collective-permute-start(bf16[272,128]{1,0:T(8,128)(2,1)S(1)} %pad_maximum_fusion.3), channel_id=1, source_target_pairs={{0,64},{1,65},{2,66},{3,67},{4,68},{5,69},{6,70},{7,71},{8,72},{9,... | collective-permute-start | bytes 208904 | tf_op jit(solution)/shard_map/ppermute | solution.py:457
  117.3 5.2 %collective-permute-start.15 = (bf16[544,128]{1,0:T(8,128)(2,1)S(1)}, bf16[544,128]{1,0:T(8,128)(2,1)S(1)}, u32[]{:S(2)}, u32[]{:S(2)}) collective-permute-start(bf16[544,128]{1,0:T(8,128)(2,1)S(1)} %pad_maximum_fusion.2), channel_id=1, source_target_pairs={{0,33},{1,32},{2,35},{3,34},{4,37},{5,36},{6,39},{7,38},{8,41},{9,... | collective-permute-start | bytes 417800 | tf_op jit(solution)/shard_map/ppermute | solution.py:457
  118.4 4.3 %collective-permute-start.4 = (bf16[192,256]{1,0:T(8,128)(2,1)S(1)}, bf16[192,256]{1,0:T(8,128)(2,1)S(1)}, u32[]{:S(2)}, u32[]{:S(2)}) collective-permute-start(bf16[192,256]{1,0:T(8,128)(2,1)S(1)} %get-tuple-element.34), channel_id=1, source_target_pairs={{0,1},{2,3},{4,5},{6,7},{8,9},{10,11},{12,13},{14,15},{1,0},{3,2},... | collective-permute-start | bytes 294920 | tf_op jit(solution)/shard_map/ppermute | solution.py:412
  118.5 4.2 %collective-permute-start.5 = (bf16[192,256]{1,0:T(8,128)(2,1)S(1)}, bf16[192,256]{1,0:T(8,128)(2,1)S(1)}, u32[]{:S(2)}, u32[]{:S(2)}) collective-permute-start(bf16[192,256]{1,0:T(8,128)(2,1)S(1)} %get-tuple-element.35), channel_id=1, source_target_pairs={{1,2},{3,4},{5,6},{7,8},{9,10},{11,12},{13,14},{2,1},{4,3},{6,5},{... | collective-permute-start | bytes 294920 | tf_op jit(solution)/shard_map/ppermute | solution.py:412
  122.6 5.5 %collective-permute-start.16 = (bf16[1088,128]{1,0:T(8,128)(2,1)S(1)}, bf16[1088,128]{1,0:T(8,128)(2,1)S(1)}, u32[]{:S(2)}, u32[]{:S(2)}) collective-permute-start(bf16[1088,128]{1,0:T(8,128)(2,1)S(1)} %pad_maximum_fusion.1), channel_id=1, source_target_pairs={{0,1},{1,0},{2,3},{3,2},{4,5},{5,4},{6,7},{7,6},{8,9},{9,8},{10,11... | collective-permute-start | bytes 835592 | tf_op jit(solution)/shard_map/ppermute | solution.py:457
  122.7 23.3 %copy-start.1 = (bf16[64,48,256]{2,1,0:T(8,128)(2,1)S(1)}, bf16[64,48,256]{2,1,0:T(8,128)(2,1)}, u32[]{:S(2)}) copy-start(bf16[64,48,256]{2,1,0:T(8,128)(2,1)} %get-tuple-element.14.g_ref) | copy-start | bytes 4718596
  122.8 15.7 %copy-start.7 = (bf16[144,256]{1,0:T(8,128)(2,1)S(1)}, bf16[144,256]{1,0:T(8,128)(2,1)}, u32[]{:S(2)}) copy-start(bf16[144,256]{1,0:T(8,128)(2,1)} %get-tuple-element.15) | copy-start | bytes 221188
  122.8 15.7 %copy-start.8 = (bf16[144,256]{1,0:T(8,128)(2,1)S(1)}, bf16[144,256]{1,0:T(8,128)(2,1)}, u32[]{:S(2)}) copy-start(bf16[144,256]{1,0:T(8,128)(2,1)} %get-tuple-element.18) | copy-start | bytes 221188
  128.2 17.8 %copy-start = (bf16[64,48,256]{2,1,0:T(8,128)(2,1)S(1)}, bf16[64,48,256]{2,1,0:T(8,128)(2,1)}, u32[]{:S(2)}) copy-start(bf16[64,48,256]{2,1,0:T(8,128)(2,1)} %cot.9) | copy-start | bytes 4718596
  128.2 17.8 %copy-start.2 = (f32[49,256]{1,0:T(8,128)S(1)}, f32[49,256]{1,0:T(8,128)}, u32[]{:S(2)}) copy-start(f32[49,256]{1,0:T(8,128)} %w_ref.9) | copy-start | bytes 150532
  128.3 32.7 %collective-permute-start.17 = (bf16[2176,128]{1,0:T(8,128)(2,1)S(1)}, bf16[2176,128]{1,0:T(8,128)(2,1)S(1)}, u32[]{:S(2)}, u32[]{:S(2)}) collective-permute-start(bf16[2176,128]{1,0:T(8,128)(2,1)S(1)} %pad_maximum_fusion.mine), channel_id=1, source_target_pairs={{0,16},{1,17},{2,18},{3,19},{4,20},{5,21},{6,22},{7,23},{8,24},{9,... | collective-permute-start | bytes 1671176 | tf_op jit(solution)/shard_map/ppermute | solution.py:457
  138.6 7.4 %collective-permute-start.7 = (bf16[176,256]{1,0:T(8,128)(2,1)S(1)}, bf16[176,256]{1,0:T(8,128)(2,1)S(1)}, u32[]{:S(2)}, u32[]{:S(2)}) collective-permute-start(bf16[176,256]{1,0:T(8,128)(2,1)S(1)} %get-tuple-element.38), channel_id=1, source_target_pairs={{16,32},{48,64},{80,96},{112,128},{144,160},{176,192},{208,224},{3... | collective-permute-start | bytes 270344 | tf_op jit(solution)/shard_map/ppermute | solution.py:412
  140.8 5.2 %collective-permute-start.6 = (bf16[176,256]{1,0:T(8,128)(2,1)S(1)}, bf16[176,256]{1,0:T(8,128)(2,1)S(1)}, u32[]{:S(2)}, u32[]{:S(2)}) collective-permute-start(bf16[176,256]{1,0:T(8,128)(2,1)S(1)} %get-tuple-element.39), channel_id=1, source_target_pairs={{0,16},{32,48},{64,80},{96,112},{128,144},{160,176},{192,208},{224... | collective-permute-start | bytes 270344 | tf_op jit(solution)/shard_map/ppermute | solution.py:412

commit v7 on v6

--- a/solution.py
+++ b/solution.py
@@ -371,27 +371,28 @@
             for h in range(2):
                 reduce[half(e), half(h)] = v[chans + h * LANES : chans + (h + 1) * LANES]
             h, first = e * count // TAPS, e * count % TAPS
-            taps_ref[first : first + count, half(h)] = v[2 * chans : 2 * chans + count]
+            lines = min(count, taps_ref.shape[0] - first)
+            taps_ref[first : first + lines, half(h)] = v[2 * chans : 2 * chans + lines]
 
         pl.when(here)(functools.partial(write, mine))
         pl.when(jnp.logical_not(here))(functools.partial(write, other))
 
 
-def spread(upper, mine, other, chans, hidden, factor):
+def spread(upper, mine, other, taps, chans, hidden, factor):
     grid = pltpu.PrefetchScalarGridSpec(
         num_scalar_prefetch=1,
         grid=(1,),
         in_specs=[VMEM] * 2,
         out_specs=[
             pl.BlockSpec(shape, lambda s, u: (0, 0))
-            for shape in ((TAPS, chans), (chans, hidden), (hidden, chans))
+            for shape in ((taps, chans), (chans, hidden), (hidden, chans))
         ],
     )
     return pl.pallas_call(
         functools.partial(spread_kernel, factor=factor),
         grid_spec=grid,
         out_shape=(
-            jax.ShapeDtypeStruct((TAPS, chans), F32),
+            jax.ShapeDtypeStruct((taps, chans), F32),
             jax.ShapeDtypeStruct((chans, hidden), F32),
             jax.ShapeDtypeStruct((hidden, chans), F32),
         ),
@@ -494,8 +495,8 @@
     for part in range(rows // PART):
         result = input_grad(g, ghalo, cot, w, result, part)
     mine, other = total(kept, sent)
-    taps, expand, reduce = spread(upper, mine, other, chans, we.shape[1], factor)
-    return result, taps[: w.shape[0]], expand, reduce
+    sums = spread(upper, mine, other, w.shape[0], chans, we.shape[1], factor)
+    return (result, *sums)
 
 
 def solution(mesh):

time: 164 us -> 163 us (level)
  no operation moved by 1% of the time
where the time goes in v7:
time: 163 us
  Pallas kernels  61.6 us (38%)
  starting transfers between devices  39.6 us (24%)
  waiting for transfers between devices  35.6 us (22%)
  blocking collectives  19.3 us (12%)
  other arithmetic  4.11 us (3%)
    pallas_call x1, Pallas kernels, branch(): pl.pallas_call(branch_kernel, grid_spec=grid, out_shape=(jax.ShapeDtypeSt...  45 us
    ppermute x10, waiting for transfers between devices, swap(): return lax.ppermute(value, AXES, pairs)  28.2 us
    ppermute x10, starting transfers between devices, swap(): return lax.ppermute(value, AXES, pairs)  27.1 us
    all_to_all x1, blocking collectives, total(): copies = lax.all_to_all(copies, 'z', 0, 0, tiled=True)  19.3 us
    pallas_call x4, Pallas kernels, input_grad(): pl.pallas_call(functools.partial(input_kernel, part), grid=(1,), out_shap...  15 us
    ppermute x8, starting transfers between devices, beside(): return lax.ppermute(value, axes, pairs + [(b, a) for a, b in pairs])  12.5 us
    ppermute x8, waiting for transfers between devices, beside(): return lax.ppermute(value, axes, pairs + [(b, a) for a, b in pairs])  7.4 us
  transfers between devices with their start and end apart: 18, of which 12 were waited for; matrix products, arithmetic and copies ran while one was open for 1% of the time, Pallas kernels for 9%

profile of v7, /device:TPU:1, one launch (start us, length us, event | category | flops | bytes accessed | tf_op | source)
XLA Modules:
  0.0 162.6 jit_solution(15620141672823820451)
XLA Ops:
  0.6 1.2 broadcast_select_fusion.5
  1.9 2.1 %collective-permute-start = (bf16[192,256]{1,0:T(8,128)(2,1)S(1)}, bf16[192,256]{1,0:T(8,128)(2,1)S(1)}, u32[]{:S(2)}, u32[]{:S(2)}) collective-permute-start(bf16[192,256]{1,0:T(8,128)(2,1)S(1)} %select_n.271), channel_id=1, source_target_pairs={{0,1},{2,3},{4,5},{6,7},{8,9},{10,11},{12,13},{14,15},{1,0},{3,2},... | collective-permute-start | bytes 294920 | tf_op jit(solution)/shard_map/ppermute | solution.py:413
  4.8 0.9 fusion
  6.2 6.6 %collective-permute-start.3 = (bf16[176,256]{1,0:T(8,128)(2,1)S(1)}, bf16[176,256]{1,0:T(8,128)(2,1)S(1)}, u32[]{:S(2)}, u32[]{:S(2)}) collective-permute-start(bf16[176,256]{1,0:T(8,128)(2,1)S(1)} %get-tuple-element.40), channel_id=1, source_target_pairs={{16,32},{48,64},{80,96},{112,128},{144,160},{176,192},{208,224},{3... | collective-permute-start | bytes 270344 | tf_op jit(solution)/shard_map/ppermute | solution.py:413
  13.0 2.1 %collective-permute-done.3 = bf16[176,256]{1,0:T(8,128)(2,1)S(1)} collective-permute-done((bf16[176,256]{1,0:T(8,128)(2,1)S(1)}, bf16[176,256]{1,0:T(8,128)(2,1)S(1)}, u32[]{:S(2)}, u32[]{:S(2)}) %collective-permute-start.3) | collective-permute-done | bytes 90144 | tf_op jit(solution)/shard_map/ppermute | solution.py:413
  15.1 0.7 broadcast_select_fusion.16
  15.8 45.0 %branch.1 = (bf16[64,48,256]{2,1,0:T(8,128)(2,1)}, bf16[192,256]{1,0:T(8,128)(2,1)}, bf16[192,256]{1,0:T(8,128)(2,1)}, bf16[144,256]{1,0:T(8,128)(2,1)}, bf16[14...) custom-call(s32[4,3]{1,0:T(4,128)} %tissue.1, s32[1]{0:T(128)} %bitcast.upper, ...), custom_call_target="tpu_custom_call" | custom-call | bytes 154980000 | tf_op jit(solution)/shard_map/branch/pallas_call | solution.py:283
  60.8 2.1 %collective-permute-done.8 = bf16[2176,128]{1,0:T(8,128)(2,1)S(1)} collective-permute-done((bf16[2176,128]{1,0:T(8,128)(2,1)}, bf16[2176,128]{1,0:T(8,128)(2,1)S(1)}, u32[]{:S(2)}, u32[]{:S(2)}) %collective-permute-start.8) | collective-permute-done | bytes 557088 | tf_op jit(solution)/shard_map/ppermute | solution.py:458
  62.9 1.3 convert_add_fusion
  64.3 4.1 %collective-permute-start.9 = (bf16[1088,128]{1,0:T(8,128)(2,1)S(1)}, bf16[1088,128]{1,0:T(8,128)(2,1)S(1)}, u32[]{:S(2)}, u32[]{:S(2)}) collective-permute-start(bf16[1088,128]{1,0:T(8,128)(2,1)S(1)} %select_convert_fusion), channel_id=1, source_target_pairs={{0,1},{1,0},{2,3},{3,2},{4,5},{5,4},{6,7},{7,6},{8,9},{9,8},{10,11... | collective-permute-start | bytes 835592 | tf_op jit(solution)/shard_map/ppermute | solution.py:458
  68.4 6.9 %collective-permute-done.9 = bf16[1088,128]{1,0:T(8,128)(2,1)S(1)} collective-permute-done((bf16[1088,128]{1,0:T(8,128)(2,1)S(1)}, bf16[1088,128]{1,0:T(8,128)(2,1)S(1)}, u32[]{:S(2)}, u32[]{:S(2)}) %collective-permute-start.9) | collective-permute-done | bytes 278560 | tf_op jit(solution)/shard_map/ppermute | solution.py:458
  75.4 3.4 %collective-permute-start.10 = (bf16[544,128]{1,0:T(8,128)(2,1)S(1)}, bf16[544,128]{1,0:T(8,128)(2,1)S(1)}, u32[]{:S(2)}, u32[]{:S(2)}) collective-permute-start(bf16[544,128]{1,0:T(8,128)(2,1)S(1)} %select_convert_fusion.1), channel_id=1, source_target_pairs={{0,33},{1,32},{2,35},{3,34},{4,37},{5,36},{6,39},{7,38},{8,41},{9,... | collective-permute-start | bytes 417800 | tf_op jit(solution)/shard_map/ppermute | solution.py:458
  78.8 2.8 %collective-permute-done.10 = bf16[544,128]{1,0:T(8,128)(2,1)S(1)} collective-permute-done((bf16[544,128]{1,0:T(8,128)(2,1)S(1)}, bf16[544,128]{1,0:T(8,128)(2,1)S(1)}, u32[]{:S(2)}, u32[]{:S(2)}) %collective-permute-start.10) | collective-permute-done | bytes 139296 | tf_op jit(solution)/shard_map/ppermute | solution.py:458
  81.7 2.2 %collective-permute-start.11 = (bf16[272,128]{1,0:T(8,128)(2,1)S(1)}, bf16[272,128]{1,0:T(8,128)(2,1)S(1)}, u32[]{:S(2)}, u32[]{:S(2)}) collective-permute-start(bf16[272,128]{1,0:T(8,128)(2,1)S(1)} %select_convert_fusion.2), channel_id=1, source_target_pairs={{0,64},{1,65},{2,66},{3,67},{4,68},{5,69},{6,70},{7,71},{8,72},{9,... | collective-permute-start | bytes 208904 | tf_op jit(solution)/shard_map/ppermute | solution.py:458
  83.9 1.7 %collective-permute-done.11 = bf16[272,128]{1,0:T(8,128)(2,1)S(1)} collective-permute-done((bf16[272,128]{1,0:T(8,128)(2,1)S(1)}, bf16[272,128]{1,0:T(8,128)(2,1)S(1)}, u32[]{:S(2)}, u32[]{:S(2)}) %collective-permute-start.11) | collective-permute-done | bytes 69664 | tf_op jit(solution)/shard_map/ppermute | solution.py:458
  85.7 3.0 %collective-permute-start.12 = (bf16[136,128]{1,0:T(8,128)(2,1)S(1)}, bf16[136,128]{1,0:T(8,128)(2,1)S(1)}, u32[]{:S(2)}, u32[]{:S(2)}) collective-permute-start(bf16[136,128]{1,0:T(8,128)(2,1)S(1)} %select_convert_fusion.3), channel_id=1, source_target_pairs={{0,192},{1,193},{2,194},{3,195},{4,196},{5,197},{6,198},{7,199},{8... | collective-permute-start | bytes 104456 | tf_op jit(solution)/shard_map/ppermute | solution.py:458
  88.7 1.3 collective-permute-done.12
  90.1 19.3 %all_to_all.5 = bf16[8,136,128]{2,1,0:T(8,128)(2,1)S(1)} all-to-all(bf16[8,136,128]{2,1,0:T(8,128)(2,1)S(1)} %broadcast_in_dim.2), channel_id=1, replica_groups=mesh['y'=4,'x_hi'=2,'core'=2,'z'=8,'x_lo'=2] {'z'}, dimensions={0} | all-to-all | bytes 557056 | tf_op jit(solution)/shard_map/all_to_all | solution.py:473
  109.4 2.8 %collective-permute-start.13 = (bf16[136,128]{1,0:T(8,128)(2,1)S(1)}, bf16[136,128]{1,0:T(8,128)(2,1)S(1)}, u32[]{:S(2)}, u32[]{:S(2)}) collective-permute-start(bf16[136,128]{1,0:T(8,128)(2,1)S(1)} %reduce_sum.12), channel_id=1, source_target_pairs={{0,192},{1,193},{2,194},{3,195},{4,196},{5,197},{6,198},{7,199},{8... | collective-permute-start | bytes 104456 | tf_op jit(solution)/shard_map/ppermute | solution.py:458
  112.2 1.6 collective-permute-done.13
  114.1 3.1 %collective-permute-done.14 = bf16[272,128]{1,0:T(8,128)(2,1)S(1)} collective-permute-done((bf16[272,128]{1,0:T(8,128)(2,1)S(1)}, bf16[272,128]{1,0:T(8,128)(2,1)S(1)}, u32[]{:S(2)}, u32[]{:S(2)}) %collective-permute-start.14) | collective-permute-done | bytes 69664 | tf_op jit(solution)/shard_map/ppermute | solution.py:458
  117.3 1.1 collective-permute-start.15
  119.2 3.3 %collective-permute-done.15 = bf16[544,128]{1,0:T(8,128)(2,1)S(1)} collective-permute-done((bf16[544,128]{1,0:T(8,128)(2,1)S(1)}, bf16[544,128]{1,0:T(8,128)(2,1)S(1)}, u32[]{:S(2)}, u32[]{:S(2)}) %collective-permute-start.15) | collective-permute-done | bytes 139296 | tf_op jit(solution)/shard_map/ppermute | solution.py:458
  122.8 5.3 %collective-permute-done.16 = bf16[1088,128]{1,0:T(8,128)(2,1)S(1)} collective-permute-done((bf16[1088,128]{1,0:T(8,128)(2,1)S(1)}, bf16[1088,128]{1,0:T(8,128)(2,1)S(1)}, u32[]{:S(2)}, u32[]{:S(2)}) %collective-permute-start.16) | collective-permute-done | bytes 278560 | tf_op jit(solution)/shard_map/ppermute | solution.py:458
  128.3 10.2 %collective-permute-start.17 = (bf16[2176,128]{1,0:T(8,128)(2,1)S(1)}, bf16[2176,128]{1,0:T(8,128)(2,1)S(1)}, u32[]{:S(2)}, u32[]{:S(2)}) collective-permute-start(bf16[2176,128]{1,0:T(8,128)(2,1)S(1)} %pad_maximum_fusion.mine), channel_id=1, source_target_pairs={{0,16},{1,17},{2,18},{3,19},{4,20},{5,21},{6,22},{7,23},{8,24},{9,... | collective-permute-start | bytes 1671176 | tf_op jit(solution)/shard_map/ppermute | solution.py:458
  138.6 2.2 %collective-permute-start.7 = (bf16[176,256]{1,0:T(8,128)(2,1)S(1)}, bf16[176,256]{1,0:T(8,128)(2,1)S(1)}, u32[]{:S(2)}, u32[]{:S(2)}) collective-permute-start(bf16[176,256]{1,0:T(8,128)(2,1)S(1)} %get-tuple-element.38), channel_id=1, source_target_pairs={{16,32},{48,64},{80,96},{112,128},{144,160},{176,192},{208,224},{3... | collective-permute-start | bytes 270344 | tf_op jit(solution)/shard_map/ppermute | solution.py:413
  140.9 5.1 %collective-permute-done.7 = bf16[176,256]{1,0:T(8,128)(2,1)S(1)} collective-permute-done((bf16[176,256]{1,0:T(8,128)(2,1)S(1)}, bf16[176,256]{1,0:T(8,128)(2,1)S(1)}, u32[]{:S(2)}, u32[]{:S(2)}) %collective-permute-start.7) | collective-permute-done | bytes 90144 | tf_op jit(solution)/shard_map/ppermute | solution.py:413
  146.1 3.7 %input_grad.4.rest_0_ = bf16[64,48,256]{2,1,0:T(8,128)(2,1)} custom-call(bf16[64,48,256]{2,1,0:T(8,128)(2,1)S(1)} %copy-done.1, bf16[176,256]{1,0:T(8,128)(2,1)S(1)} %get-tuple-element.43.top, bf16[176,256]{1,0:T(8,128)(2,1)S(1)} %get-tuple-element.42.bottom, bf16[192,256]{1,0:T(8,128)(2,1)S(1)} %get-tuple-element.32.left, ...), custom_call_target="tpu_custom_call" | custom-call | bytes 14760000 | tf_op jit(solution)/shard_map/input_grad/pallas_call | solution.py:341
  149.8 3.8 %input_grad.5.rest_0_ = bf16[64,48,256]{2,1,0:T(8,128)(2,1)} custom-call(bf16[64,48,256]{2,1,0:T(8,128)(2,1)S(1)} %copy-done.1, bf16[176,256]{1,0:T(8,128)(2,1)S(1)} %get-tuple-element.43.top, bf16[176,256]{1,0:T(8,128)(2,1)S(1)} %get-tuple-element.42.bottom, bf16[192,256]{1,0:T(8,128)(2,1)S(1)} %get-tuple-element.32.left, ...), custom_call_target="tpu_custom_call", output_to_operand_aliasing={{}: (7, {})} | custom-call | bytes 14760000 | tf_op jit(solution)/shard_map/input_grad/pallas_call | solution.py:341
  153.5 3.8 %input_grad.6.rest_0_ = bf16[64,48,256]{2,1,0:T(8,128)(2,1)} custom-call(bf16[64,48,256]{2,1,0:T(8,128)(2,1)S(1)} %copy-done.1, bf16[176,256]{1,0:T(8,128)(2,1)S(1)} %get-tuple-element.43.top, bf16[176,256]{1,0:T(8,128)(2,1)S(1)} %get-tuple-element.42.bottom, bf16[192,256]{1,0:T(8,128)(2,1)S(1)} %get-tuple-element.32.left, ...), custom_call_target="tpu_custom_call", output_to_operand_aliasing={{}: (7, {})} | custom-call | bytes 14760000 | tf_op jit(solution)/shard_map/input_grad/pallas_call | solution.py:341
  157.3 3.7 %input_grad.7 = bf16[64,48,256]{2,1,0:T(8,128)(2,1)} custom-call(bf16[64,48,256]{2,1,0:T(8,128)(2,1)S(1)} %copy-done.1, bf16[176,256]{1,0:T(8,128)(2,1)S(1)} %get-tuple-element.43.top, bf16[176,256]{1,0:T(8,128)(2,1)S(1)} %get-tuple-element.42.bottom, bf16[192,256]{1,0:T(8,128)(2,1)S(1)} %get-tuple-element.32.left, ...), custom_call_target="tpu_custom_call", output_to_operand_aliasing={{}: (7, {})} | custom-call | bytes 14760000 | tf_op jit(solution)/shard_map/input_grad/pallas_call | solution.py:341
  161.0 1.6 spread.1
  (64 shorter events, 3.5 us)
Async XLA Ops:
  1.9 4.1 %collective-permute-start = (bf16[192,256]{1,0:T(8,128)(2,1)S(1)}, bf16[192,256]{1,0:T(8,128)(2,1)S(1)}, u32[]{:S(2)}, u32[]{:S(2)}) collective-permute-start(bf16[192,256]{1,0:T(8,128)(2,1)S(1)} %select_n.271), channel_id=1, source_target_pairs={{0,1},{2,3},{4,5},{6,7},{8,9},{10,11},{12,13},{14,15},{1,0},{3,2},... | collective-permute-start | bytes 294920 | tf_op jit(solution)/shard_map/ppermute | solution.py:413
  4.1 1.9 %collective-permute-start.1 = (bf16[192,256]{1,0:T(8,128)(2,1)S(1)}, bf16[192,256]{1,0:T(8,128)(2,1)S(1)}, u32[]{:S(2)}, u32[]{:S(2)}) collective-permute-start(bf16[192,256]{1,0:T(8,128)(2,1)S(1)} %select_n.273), channel_id=1, source_target_pairs={{1,2},{3,4},{5,6},{7,8},{9,10},{11,12},{13,14},{2,1},{4,3},{6,5},{... | collective-permute-start | bytes 294920 | tf_op jit(solution)/shard_map/ppermute | solution.py:413
  6.1 9.7 %copy-start.3 = (bf16[192,256]{1,0:T(8,128)(2,1)}, bf16[192,256]{1,0:T(8,128)(2,1)S(1)}, u32[]{:S(2)}) copy-start(bf16[192,256]{1,0:T(8,128)(2,1)S(1)} %get-tuple-element.36.left) | copy-start | bytes 294916
  6.1 9.7 %copy-start.4 = (bf16[192,256]{1,0:T(8,128)(2,1)}, bf16[192,256]{1,0:T(8,128)(2,1)S(1)}, u32[]{:S(2)}) copy-start(bf16[192,256]{1,0:T(8,128)(2,1)S(1)} %get-tuple-element.37.right) | copy-start | bytes 294916
  6.2 8.8 %collective-permute-start.3 = (bf16[176,256]{1,0:T(8,128)(2,1)S(1)}, bf16[176,256]{1,0:T(8,128)(2,1)S(1)}, u32[]{:S(2)}, u32[]{:S(2)}) collective-permute-start(bf16[176,256]{1,0:T(8,128)(2,1)S(1)} %get-tuple-element.40), channel_id=1, source_target_pairs={{16,32},{48,64},{80,96},{112,128},{144,160},{176,192},{208,224},{3... | collective-permute-start | bytes 270344 | tf_op jit(solution)/shard_map/ppermute | solution.py:413
  12.8 2.2 %collective-permute-start.2 = (bf16[176,256]{1,0:T(8,128)(2,1)S(1)}, bf16[176,256]{1,0:T(8,128)(2,1)S(1)}, u32[]{:S(2)}, u32[]{:S(2)}) collective-permute-start(bf16[176,256]{1,0:T(8,128)(2,1)S(1)} %get-tuple-element.41), channel_id=1, source_target_pairs={{0,16},{32,48},{64,80},{96,112},{128,144},{160,176},{192,208},{224... | collective-permute-start | bytes 270344 | tf_op jit(solution)/shard_map/ppermute | solution.py:413
  60.8 2.2 %collective-permute-start.8 = (bf16[2176,128]{1,0:T(8,128)(2,1)}, bf16[2176,128]{1,0:T(8,128)(2,1)S(1)}, u32[]{:S(2)}, u32[]{:S(2)}) collective-permute-start(bf16[2176,128]{1,0:T(8,128)(2,1)} %get-tuple-element.20), channel_id=1, source_target_pairs={{0,16},{1,17},{2,18},{3,19},{4,20},{5,21},{6,22},{7,23},{8,24},{9,... | collective-permute-start | bytes 1671176 | tf_op jit(solution)/shard_map/ppermute | solution.py:458
  64.3 11.0 %collective-permute-start.9 = (bf16[1088,128]{1,0:T(8,128)(2,1)S(1)}, bf16[1088,128]{1,0:T(8,128)(2,1)S(1)}, u32[]{:S(2)}, u32[]{:S(2)}) collective-permute-start(bf16[1088,128]{1,0:T(8,128)(2,1)S(1)} %select_convert_fusion), channel_id=1, source_target_pairs={{0,1},{1,0},{2,3},{3,2},{4,5},{5,4},{6,7},{7,6},{8,9},{9,8},{10,11... | collective-permute-start | bytes 835592 | tf_op jit(solution)/shard_map/ppermute | solution.py:458
  75.4 6.3 %collective-permute-start.10 = (bf16[544,128]{1,0:T(8,128)(2,1)S(1)}, bf16[544,128]{1,0:T(8,128)(2,1)S(1)}, u32[]{:S(2)}, u32[]{:S(2)}) collective-permute-start(bf16[544,128]{1,0:T(8,128)(2,1)S(1)} %select_convert_fusion.1), channel_id=1, source_target_pairs={{0,33},{1,32},{2,35},{3,34},{4,37},{5,36},{6,39},{7,38},{8,41},{9,... | collective-permute-start | bytes 417800 | tf_op jit(solution)/shard_map/ppermute | solution.py:458
  81.7 3.9 %collective-permute-start.11 = (bf16[272,128]{1,0:T(8,128)(2,1)S(1)}, bf16[272,128]{1,0:T(8,128)(2,1)S(1)}, u32[]{:S(2)}, u32[]{:S(2)}) collective-permute-start(bf16[272,128]{1,0:T(8,128)(2,1)S(1)} %select_convert_fusion.2), channel_id=1, source_target_pairs={{0,64},{1,65},{2,66},{3,67},{4,68},{5,69},{6,70},{7,71},{8,72},{9,... | collective-permute-start | bytes 208904 | tf_op jit(solution)/shard_map/ppermute | solution.py:458
  85.7 32.7 %copy-start.5 = (bf16[192,256]{1,0:T(8,128)(2,1)S(1)}, bf16[192,256]{1,0:T(8,128)(2,1)}, u32[]{:S(2)}) copy-start(bf16[192,256]{1,0:T(8,128)(2,1)} %get-tuple-element.16) | copy-start | bytes 294916
  85.7 32.7 %copy-start.6 = (bf16[192,256]{1,0:T(8,128)(2,1)S(1)}, bf16[192,256]{1,0:T(8,128)(2,1)}, u32[]{:S(2)}) copy-start(bf16[192,256]{1,0:T(8,128)(2,1)} %get-tuple-element.17) | copy-start | bytes 294916
  85.7 4.3 %collective-permute-start.12 = (bf16[136,128]{1,0:T(8,128)(2,1)S(1)}, bf16[136,128]{1,0:T(8,128)(2,1)S(1)}, u32[]{:S(2)}, u32[]{:S(2)}) collective-permute-start(bf16[136,128]{1,0:T(8,128)(2,1)S(1)} %select_convert_fusion.3), channel_id=1, source_target_pairs={{0,192},{1,193},{2,194},{3,195},{4,196},{5,197},{6,198},{7,199},{8... | collective-permute-start | bytes 104456 | tf_op jit(solution)/shard_map/ppermute | solution.py:458
  109.4 4.4 %collective-permute-start.13 = (bf16[136,128]{1,0:T(8,128)(2,1)S(1)}, bf16[136,128]{1,0:T(8,128)(2,1)S(1)}, u32[]{:S(2)}, u32[]{:S(2)}) collective-permute-start(bf16[136,128]{1,0:T(8,128)(2,1)S(1)} %reduce_sum.12), channel_id=1, source_target_pairs={{0,192},{1,193},{2,194},{3,195},{4,196},{5,197},{6,198},{7,199},{8... | collective-permute-start | bytes 104456 | tf_op jit(solution)/shard_map/ppermute | solution.py:458
  113.8 3.4 %collective-permute-start.14 = (bf16[272,128]{1,0:T(8,128)(2,1)S(1)}, bf16[272,128]{1,0:T(8,128)(2,1)S(1)}, u32[]{:S(2)}, u32[]{:S(2)}) collective-permute-start(bf16[272,128]{1,0:T(8,128)(2,1)S(1)} %pad_maximum_fusion.3), channel_id=1, source_target_pairs={{0,64},{1,65},{2,66},{3,67},{4,68},{5,69},{6,70},{7,71},{8,72},{9,... | collective-permute-start | bytes 208904 | tf_op jit(solution)/shard_map/ppermute | solution.py:458
  117.3 5.2 %collective-permute-start.15 = (bf16[544,128]{1,0:T(8,128)(2,1)S(1)}, bf16[544,128]{1,0:T(8,128)(2,1)S(1)}, u32[]{:S(2)}, u32[]{:S(2)}) collective-permute-start(bf16[544,128]{1,0:T(8,128)(2,1)S(1)} %pad_maximum_fusion.2), channel_id=1, source_target_pairs={{0,33},{1,32},{2,35},{3,34},{4,37},{5,36},{6,39},{7,38},{8,41},{9,... | collective-permute-start | bytes 417800 | tf_op jit(solution)/shard_map/ppermute | solution.py:458
  118.4 4.3 %collective-permute-start.4 = (bf16[192,256]{1,0:T(8,128)(2,1)S(1)}, bf16[192,256]{1,0:T(8,128)(2,1)S(1)}, u32[]{:S(2)}, u32[]{:S(2)}) collective-permute-start(bf16[192,256]{1,0:T(8,128)(2,1)S(1)} %get-tuple-element.34), channel_id=1, source_target_pairs={{0,1},{2,3},{4,5},{6,7},{8,9},{10,11},{12,13},{14,15},{1,0},{3,2},... | collective-permute-start | bytes 294920 | tf_op jit(solution)/shard_map/ppermute | solution.py:413
  118.5 4.2 %collective-permute-start.5 = (bf16[192,256]{1,0:T(8,128)(2,1)S(1)}, bf16[192,256]{1,0:T(8,128)(2,1)S(1)}, u32[]{:S(2)}, u32[]{:S(2)}) collective-permute-start(bf16[192,256]{1,0:T(8,128)(2,1)S(1)} %get-tuple-element.35), channel_id=1, source_target_pairs={{1,2},{3,4},{5,6},{7,8},{9,10},{11,12},{13,14},{2,1},{4,3},{6,5},{... | collective-permute-start | bytes 294920 | tf_op jit(solution)/shard_map/ppermute | solution.py:413
  122.6 5.5 %collective-permute-start.16 = (bf16[1088,128]{1,0:T(8,128)(2,1)S(1)}, bf16[1088,128]{1,0:T(8,128)(2,1)S(1)}, u32[]{:S(2)}, u32[]{:S(2)}) collective-permute-start(bf16[1088,128]{1,0:T(8,128)(2,1)S(1)} %pad_maximum_fusion.1), channel_id=1, source_target_pairs={{0,1},{1,0},{2,3},{3,2},{4,5},{5,4},{6,7},{7,6},{8,9},{9,8},{10,11... | collective-permute-start | bytes 835592 | tf_op jit(solution)/shard_map/ppermute | solution.py:458
  122.7 23.3 %copy-start.1 = (bf16[64,48,256]{2,1,0:T(8,128)(2,1)S(1)}, bf16[64,48,256]{2,1,0:T(8,128)(2,1)}, u32[]{:S(2)}) copy-start(bf16[64,48,256]{2,1,0:T(8,128)(2,1)} %get-tuple-element.14.g_ref) | copy-start | bytes 4718596
  122.8 15.7 %copy-start.7 = (bf16[144,256]{1,0:T(8,128)(2,1)S(1)}, bf16[144,256]{1,0:T(8,128)(2,1)}, u32[]{:S(2)}) copy-start(bf16[144,256]{1,0:T(8,128)(2,1)} %get-tuple-element.15) | copy-start | bytes 221188
  122.8 15.7 %copy-start.8 = (bf16[144,256]{1,0:T(8,128)(2,1)S(1)}, bf16[144,256]{1,0:T(8,128)(2,1)}, u32[]{:S(2)}) copy-start(bf16[144,256]{1,0:T(8,128)(2,1)} %get-tuple-element.18) | copy-start | bytes 221188
  128.2 17.8 %copy-start = (bf16[64,48,256]{2,1,0:T(8,128)(2,1)S(1)}, bf16[64,48,256]{2,1,0:T(8,128)(2,1)}, u32[]{:S(2)}) copy-start(bf16[64,48,256]{2,1,0:T(8,128)(2,1)} %cot.9) | copy-start | bytes 4718596
  128.2 17.8 %copy-start.2 = (f32[49,256]{1,0:T(8,128)S(1)}, f32[49,256]{1,0:T(8,128)}, u32[]{:S(2)}) copy-start(f32[49,256]{1,0:T(8,128)} %w_ref.9) | copy-start | bytes 150532
  128.3 32.7 %collective-permute-start.17 = (bf16[2176,128]{1,0:T(8,128)(2,1)S(1)}, bf16[2176,128]{1,0:T(8,128)(2,1)S(1)}, u32[]{:S(2)}, u32[]{:S(2)}) collective-permute-start(bf16[2176,128]{1,0:T(8,128)(2,1)S(1)} %pad_maximum_fusion.mine), channel_id=1, source_target_pairs={{0,16},{1,17},{2,18},{3,19},{4,20},{5,21},{6,22},{7,23},{8,24},{9,... | collective-permute-start | bytes 1671176 | tf_op jit(solution)/shard_map/ppermute | solution.py:458
  138.6 7.4 %collective-permute-start.7 = (bf16[176,256]{1,0:T(8,128)(2,1)S(1)}, bf16[176,256]{1,0:T(8,128)(2,1)S(1)}, u32[]{:S(2)}, u32[]{:S(2)}) collective-permute-start(bf16[176,256]{1,0:T(8,128)(2,1)S(1)} %get-tuple-element.38), channel_id=1, source_target_pairs={{16,32},{48,64},{80,96},{112,128},{144,160},{176,192},{208,224},{3... | collective-permute-start | bytes 270344 | tf_op jit(solution)/shard_map/ppermute | solution.py:413
  140.8 5.2 %collective-permute-start.6 = (bf16[176,256]{1,0:T(8,128)(2,1)S(1)}, bf16[176,256]{1,0:T(8,128)(2,1)S(1)}, u32[]{:S(2)}, u32[]{:S(2)}) collective-permute-start(bf16[176,256]{1,0:T(8,128)(2,1)S(1)} %get-tuple-element.39), channel_id=1, source_target_pairs={{0,16},{32,48},{64,80},{96,112},{128,144},{160,176},{192,208},{224... | collective-permute-start | bytes 270344 | tf_op jit(solution)/shard_map/ppermute | solution.py:413
